TPU v7x, 32 devices: a whole 2x2x4 slice. The times are simulated.
32 devices in a mesh: seq: 16 (over z, y, core), head: 2 (over x).
Axes of the slice: x: 2, y: 2, z: 4, core: 2. Of those that a mesh axis runs over, the one named last changes fastest.
Arguments:
- queries: bfloat16 [2048, 3072], P('seq', 'head')
- block_keys: bfloat16 [2048, 3072], P('seq', 'head')
- block_values: bfloat16 [2048, 3072], P('seq', 'head'), may hold values from -6 to 6
- cache_keys: bfloat16 [256, 3072], P('seq', 'head'), may hold values from -6 to 6
- cache_values: bfloat16 [256, 3072], P('seq', 'head'), may hold values from -6 to 6
- cache_lengths: int32 [16], P('seq'), may hold values from 1 to 16
- out_weight: bfloat16 [3072, 5120], P('head'), may hold values from -0.15625 to 0.15625
Outputs:
- projected: bfloat16 [2048, 5120], P('seq', 'head')
All inputs are finite; a program needn't handle non-finite values.
Results may differ from a plain program's by a relative error of at most 0.014.
Values may be sent and summed in bfloat16 or wider, within the bound.
No kernel may reach another device: no remote copies, remote signals or barrier semaphores. Data moves between devices by JAX's collectives and lax.ppermute only.
A program may use at most 128 MiB of HBM per device.

v0:
```python
import math

import jax
import jax.numpy as jnp
from jax import lax
from jax.sharding import PartitionSpec as P

DH = 128


NEG_BIG = -1e30


def fold_keys(running, query_heads, key_rows, value_rows, usable):
    maxima, totals, accumulated = running
    heads_here = query_heads.shape[1]
    head_width = query_heads.shape[2]
    key_heads = key_rows.reshape(key_rows.shape[0], heads_here, head_width)
    value_heads = value_rows.reshape(value_rows.shape[0], heads_here, head_width)
    scores = jnp.einsum(
        "qhd,khd->hqk", query_heads, key_heads, preferred_element_type=jnp.float32
    ) * (1.0 / math.sqrt(head_width))
    if usable is not None:
        scores = jnp.where(usable[None, None, :], scores, NEG_BIG)
    newest = jnp.maximum(maxima, jnp.max(scores, axis=2))
    carried = jnp.exp(maxima - newest)
    weights = jnp.exp(scores - newest[:, :, None])
    totals = totals * carried + jnp.sum(weights, axis=2)
    mixed = jnp.einsum(
        "hqk,khd->hqd",
        weights.astype(jnp.bfloat16),
        value_heads,
        preferred_element_type=jnp.float32,
    )
    accumulated = accumulated * carried[:, :, None] + mixed
    return (newest, totals, accumulated)


def cache_usable(lengths_piece, slots, row_count):
    slot_index = jnp.arange(row_count, dtype=jnp.int32) % slots
    slot_limit = jnp.repeat(lengths_piece.astype(jnp.int32), slots, total_repeat_length=row_count)
    return slot_index < slot_limit


def on_device(
    queries, block_keys, block_values, cache_keys, cache_values, cache_lengths, out_weight
):
    tokens_here = queries.shape[0]
    heads_here = queries.shape[1] // DH
    query_heads = queries.reshape(tokens_here, heads_here, DH)
    slots = cache_keys.shape[0]
    start_state = (
        jnp.full((heads_here, tokens_here), NEG_BIG, jnp.float32),
        jnp.zeros((heads_here, tokens_here), jnp.float32),
        jnp.zeros((heads_here, tokens_here, DH), jnp.float32),
    )
    pieces = (
        lax.all_gather(block_keys, "seq", axis=0, tiled=True),
        lax.all_gather(block_values, "seq", axis=0, tiled=True),
    )
    running = fold_keys(start_state, query_heads, pieces[0], pieces[1], None)
    pieces = (
        lax.all_gather(cache_keys, "seq", axis=0, tiled=True),
        lax.all_gather(cache_values, "seq", axis=0, tiled=True),
        lax.all_gather(cache_lengths, "seq", axis=0, tiled=True),
    )
    usable = cache_usable(pieces[2], slots, pieces[0].shape[0])
    running = fold_keys(running, query_heads, pieces[0], pieces[1], usable)
    maxima, totals, accumulated = running
    attended = (
        (accumulated / totals[:, :, None])
        .transpose(1, 0, 2)
        .reshape(tokens_here, heads_here * DH)
        .astype(jnp.bfloat16)
    )
    partial_terms = jnp.dot(attended, out_weight, preferred_element_type=jnp.float32)
    return lax.psum_scatter(
        partial_terms.astype(jnp.bfloat16), "head", scatter_dimension=1, tiled=True
    )


def solution(mesh):
    return jax.shard_map(
        on_device,
        mesh=mesh,
        in_specs=(
            P("seq", "head"),
            P("seq", "head"),
            P("seq", "head"),
            P("seq", "head"),
            P("seq", "head"),
            P("seq"),
            P("head", None),
        ),
        out_specs=P("seq", "head"),
        check_vma=False,
    )
```

profile of v0, /device:TPU:0, one launch (start us, length us, event | category | flops | bytes accessed | tf_op | source)
XLA Modules:
  0.0 205.0 jit_solution(15468129387979567241)
XLA Ops:
  6.5 0.0 all-gather.3.cloned.1.call-start
  6.5 1.9 copy.22
  8.5 0.0 all-gather.3.cloned.1.call-update
  8.5 0.0 all-gather.5.cloned.1.call-start
  8.5 0.7 all-gather.5.cloned.1.call-update
  9.2 0.0 reduce-scatter.2.cloned.1.call-start
  9.9 1.2 dynamic-slice.6
  11.2 0.7 dynamic-update-slice.3
  11.9 15.3 %all-reduce = s32[16]{0:T(128)S(1)} all-reduce(s32[16]{0:T(128)S(1)} %dynamic-update-slice.3), channel_id=1, replica_groups=mesh['seq'=16,'head'=2] {'seq'}, use_global_device_ids=true, to_apply=%add | all-reduce | flops 16 | bytes 128
  27.2 1.2 copy.21
  28.4 21.7 %all_gather.18 = bf16[256,1536]{1,0:T(8,128)(2,1)S(1)} all-gather(bf16[16,1536]{1,0:T(8,128)(2,1)} %param.12), channel_id=1, replica_groups=mesh['seq'=16,'head'=2] {'seq'}, dimensions={0}, use_global_device_ids=true | all-gather | bytes 835584 | tf_op jit(solution)/shard_map/all_gather | solution.py:63
  50.0 0.3 copy.26
  50.3 25.3 %all_gather.19 = bf16[256,1536]{1,0:T(8,128)(2,1)S(1)} all-gather(bf16[16,1536]{1,0:T(8,128)(2,1)} %param.13), channel_id=1, replica_groups=mesh['seq'=16,'head'=2] {'seq'}, dimensions={0}, use_global_device_ids=true | all-gather | bytes 835584 | tf_op jit(solution)/shard_map/all_gather | solution.py:64
  75.6 0.3 copy.29
  75.9 0.7 fusion.30
  76.6 0.1 add_add_fusion.1
  76.7 4.3 %compare_select_fusion.1 = (s32[256,1]{0,1:T(1,128)S(1)}, s32[256,1]{0,1:T(1,128)S(1)}) fusion(s32[]{:T(128)} %bitcast.19, s32[]{:T(128)} %bitcast.20, s32[]{:T(128)} %bitcast.21, s32[]{:T(128)} %bitcast.22, s32[]{:T(128)} %bitcast.23, s32[]{:T(128)} %bitcast.25, s32[]{:T(128)} %bitcast.24, s32[256,1]{0,1:T(1,128)S(1)} %bitcast.82, s32[256,1]{0,1:T(1,128)S(1)} %bitcast.81), kind=kLoop, calls=%fused_computation.39 | loop fusion | flops 3584 | bytes 4124 | tf_op jit(solution)/shard_map/jit(_take)/gather | solution.py:41
  81.1 5.7 %fusion.26 = pred[256]{0:T(512)(128)(4,1)S(1)} fusion(pred[256]{0:T(512)(128)(4,1)S(1)} %get-tuple-element.25, pred[256]{0:T(512)(128)(4,1)S(1)} %get-tuple-element.24, pred[256]{0:T(512)(128)(4,1)S(1)} %get-tuple-element.23, pred[256]{0:T(512)(128)(4,1)S(1)} %get-tuple-element.22, pred[256]{0:T(512)(128)(4,1)S(1)} %get-tuple-element.21, ...), kind=kLoop, calls=%fused_computation.50 | loop fusion | flops 6400 | bytes 4652 | tf_op jit(solution)/shard_map/lt | solution.py:42
  86.8 0.5 fusion.31
  87.3 0.0 all-gather.3.cloned.1.call-done
  87.3 4.7 %multiply_reduce_fusion = (f32[12,128]{1,0:T(8,128)S(1)}, f32[12,128,2048]{2,1,0:T(8,128)S(1)}) fusion(bf16[128,12,128]{0,2,1:T(8,128)(2,1)S(1)} %bitcast.76, bf16[2048,12,128]{0,2,1:T(8,128)(2,1)} %bitcast.74), kind=kOutput, calls=%fused_computation.1 | convolution fusion | flops 811596288 | bytes 19273728 | tf_op jit(solution)/shard_map/qhd,khd->hqk/dot_general | solution.py:20
  92.0 0.5 fusion.6
  92.6 2.5 %fusion = f32[12,128]{1,0:T(8,128)S(1)} fusion(f32[12,128,2048]{2,1,0:T(8,128)S(1)} %get-tuple-element.54, f32[12,128]{1,0:T(8,128)S(1)} %get-tuple-element.32), kind=kLoop, calls=%fused_computation.2 | loop fusion | flops 9435648 | bytes 12595200 | tf_op jit(solution)/shard_map/reduce_sum | solution.py:28
  95.0 1.6 copy-done
  96.6 0.6 bitcast_add_fusion
  97.2 51.5 %all-gather.5.cloned.1.call-done = bf16[2048,1536]{1,0:T(8,128)(2,1)} async-done(((bf16[128,1536]{1,0:T(8,128)(2,1)}), bf16[2048,1536]{1,0:T(8,128)(2,1)}) %all-gather.5.cloned.1.call-update) | async-done | bytes 6291472 | tf_op jit(solution)/shard_map/all_gather | solution.py:59
  148.7 8.7 %copy.25 = bf16[2048,1536]{0,1:T(8,128)(2,1)} copy(bf16[2048,1536]{1,0:T(8,128)(2,1)} %all-gather.5.cloned.1.call-done) | data formatting | bytes 12582912 | tf_op jit(solution)/shard_map/all_gather | solution.py:59
  157.4 9.6 %fusion.16 = f32[128,12,128]{0,2,1:T(8,128)S(1)} fusion(bf16[2048,12,128]{0,2,1:T(8,128)(2,1)} %bitcast.73, f32[12,128,2048]{2,1,0:T(8,128)} %copy-done, f32[12,128]{1,0:T(8,128)S(1)} %get-tuple-element.32, f32[128,12]{0,1:T(8,128)S(1)} %get-tuple-element.27, f32[128,12]{0,1:T(8,128)S(1)} %get-tuple-element.30), kind=kOutput, calls=%fused_computation.17 | convolution fusion | flops 815136768 | bytes 19679232 | tf_op jit(solution)/shard_map/hqk,khd->hqd/dot_general | solution.py:29
  167.0 0.5 fusion.19
  167.5 8.8 %convolution_convert_fusion = bf16[128,5120]{1,0:T(8,128)(2,1)} fusion(bf16[128,1536]{0,1:T(8,128)(2,1)S(1)} %bitcast.79, bf16[1536,5120]{1,0:T(8,128)(2,1)} %param.15), kind=kOutput, calls=%fused_computation.7 | convolution fusion | flops 2013921280 | bytes 17432576 | tf_op jit(solution)/shard_map/dot_general | solution.py:76
  176.3 0.0 reduce-scatter.2.cloned.1.call-update
  176.3 22.1 %reduce-scatter.2.cloned.1.call-done = bf16[128,2560]{1,0:T(8,128)(2,1)} async-done(((bf16[128,5120]{1,0:T(8,128)(2,1)}), bf16[128,2560]{1,0:T(8,128)(2,1)}) %reduce-scatter.2.cloned.1.call-update) | async-done | bytes 655376 | tf_op jit(solution)/shard_map/reduce_scatter | solution.py:77
  (9 shorter events, 0.1 us)
Async XLA Ops:
  6.5 70.1 %copy-start.2 = (s32[2,128]{1,0:T(2,128)S(1)}, s32[2,128]{1,0:T(2,128)}, u32[]{:S(2)}) copy-start(s32[2,128]{1,0:T(2,128)} %constant.113.clone.1) | copy-start | bytes 3076
  6.5 80.8 %all-gather.3.cloned.1.call-start = ((), (), s32[]{:S(2)}) async-start(), calls=%async_computation.1 | async-start | bytes 6684672 | tf_op jit(solution)/shard_map/all_gather | solution.py:58
  8.5 140.2 %all-gather.5.cloned.1.call-start = ((), (), s32[]{:S(2)}) async-start(), calls=%async_computation.2 | async-start | bytes 6684672 | tf_op jit(solution)/shard_map/all_gather | solution.py:59
  9.2 189.2 %reduce-scatter.2.cloned.1.call-start = ((), (), s32[]{:S(2)}) async-start(), calls=%async_computation.3 | async-start | bytes 1966080 | tf_op jit(solution)/shard_map/reduce_scatter | solution.py:77
  92.0 4.6 %copy-start = (f32[12,128,2048]{2,1,0:T(8,128)}, f32[12,128,2048]{2,1,0:T(8,128)S(1)}, u32[]{:S(2)}) copy-start(f32[12,128,2048]{2,1,0:T(8,128)S(1)} %get-tuple-element.54) | copy-start | bytes 37748740
  157.4 9.6 %copy-start.1 = (f32[128,12]{0,1:T(8,128)S(1)}, f32[128,12]{0,1:T(8,128)}, u32[]{:S(2)}) copy-start(f32[128,12]{0,1:T(8,128)} %get-tuple-element.26) | copy-start | bytes 18436
Sparse Core Ops, SparseCore 0:
  9.5 76.2 all-gather.2
  88.1 60.5 all-gather.4
  176.5 21.9 reduce-scatter.1
where the time goes:
time: 206 us; the launch traced here: 205 us
  waiting for transfers between devices  74.4 us (36%)
  blocking collectives  62.3 us (30%)
  matrix products  24.1 us (12%)
  local copies, waits for them, and re-layouts  16.6 us (8%)
  between operations  13.8 us (7%)
  other arithmetic  13.7 us (7%)
    all_gather x1, waiting for transfers between devices, on_device(): lax.all_gather(block_values, 'seq', axis=0, tiled=True)  51.5 us
    all_gather x1, blocking collectives, on_device(): lax.all_gather(cache_values, 'seq', axis=0, tiled=True)  25.3 us
    reduce_scatter x1, waiting for transfers between devices, on_device(): lax.psum_scatter(partial_terms.astype(jnp.bfloat16), 'head', scatter_dime...  22.1 us
    all_gather x1, blocking collectives, on_device(): lax.all_gather(cache_keys, 'seq', axis=0, tiled=True)  21.7 us
    unnamed x1, blocking collectives  15.3 us
    dot_general x2, matrix products, fold_keys(): jnp.einsum('hqk,khd->hqd', weights.astype(jnp.bfloat16), value_heads, pre...  10 us
    dot_general x1, matrix products, on_device(): jnp.dot(attended, out_weight, preferred_element_type=jnp.float32)  8.81 us
    all_gather x1, local copies, waits for them, and re-layouts, on_device(): lax.all_gather(block_values, 'seq', axis=0, tiled=True)  8.7 us
  transfers between devices with their start and end apart: 3, of which 2 were waited for; matrix products, arithmetic and copies ran while one was open for 11% of the time, Pallas kernels for 0%

commit v1 on v0

--- a/solution.py
+++ b/solution.py
@@ -1,14 +1,17 @@
+import functools
 import math
 
 import jax
 import jax.numpy as jnp
 from jax import lax
+from jax.experimental import pallas as pl
+from jax.experimental.pallas import tpu as pltpu
 from jax.sharding import PartitionSpec as P
 
 DH = 128
-
-
 NEG_BIG = -1e30
+CORES = 2
+GROUPS = 4
 
 
 def fold_keys(running, query_heads, key_rows, value_rows, usable):
@@ -42,31 +45,24 @@
     return slot_index < slot_limit
 
 
-def on_device(
+def gathered_plan(
     queries, block_keys, block_values, cache_keys, cache_values, cache_lengths, out_weight
 ):
     tokens_here = queries.shape[0]
     heads_here = queries.shape[1] // DH
     query_heads = queries.reshape(tokens_here, heads_here, DH)
     slots = cache_keys.shape[0]
-    start_state = (
+    running = (
         jnp.full((heads_here, tokens_here), NEG_BIG, jnp.float32),
         jnp.zeros((heads_here, tokens_here), jnp.float32),
         jnp.zeros((heads_here, tokens_here, DH), jnp.float32),
     )
-    pieces = (
-        lax.all_gather(block_keys, "seq", axis=0, tiled=True),
-        lax.all_gather(block_values, "seq", axis=0, tiled=True),
-    )
-    running = fold_keys(start_state, query_heads, pieces[0], pieces[1], None)
-    pieces = (
-        lax.all_gather(cache_keys, "seq", axis=0, tiled=True),
-        lax.all_gather(cache_values, "seq", axis=0, tiled=True),
-        lax.all_gather(cache_lengths, "seq", axis=0, tiled=True),
-    )
-    usable = cache_usable(pieces[2], slots, pieces[0].shape[0])
-    running = fold_keys(running, query_heads, pieces[0], pieces[1], usable)
-    maxima, totals, accumulated = running
+    gather = functools.partial(lax.all_gather, axis_name="seq", axis=0, tiled=True)
+    running = fold_keys(running, query_heads, gather(block_keys), gather(block_values), None)
+    cached = gather(cache_keys)
+    usable = cache_usable(gather(cache_lengths), slots, cached.shape[0])
+    running = fold_keys(running, query_heads, cached, gather(cache_values), usable)
+    _, totals, accumulated = running
     attended = (
         (accumulated / totals[:, :, None])
         .transpose(1, 0, 2)
@@ -79,9 +75,285 @@
     )
 
 
+def inside():
+    return pl.BlockSpec(memory_space=pltpu.VMEM)
+
+
+def outside():
+    return pl.BlockSpec(memory_space=pltpu.HBM)
+
+
+def pack_kernel(seq, width, slots, len_ref, q, k, v, ck, cv, *refs):
+    outs, sems = refs[: 2 * GROUPS], refs[2 * GROUPS]
+    me = lax.div(lax.axis_index("seq"), seq // GROUPS)
+    copies = []
+    for step in (1, 2, 3, 0):
+        group = lax.bitwise_xor(me, step)
+        cols = pl.ds(pl.multiple_of(group * width, width), width)
+        kv, qo = outs[2 * step], outs[2 * step + 1]
+        row = 0
+        for src in (k, v, ck, cv):
+            rows = src.shape[0]
+            copies.append((src.at[:, cols], kv.at[pl.ds(row, rows), :]))
+            row += rows
+        copies.append((q.at[:, cols], qo))
+    started = [
+        pltpu.make_async_copy(src, dst, sems.at[i]) for i, (src, dst) in enumerate(copies)
+    ]
+    for copy in started:
+        copy.start()
+    lane = lax.broadcasted_iota(jnp.int32, (16, width), 1)
+    flags = jnp.where(lax.rem(lane, slots) < len_ref[0], 1.0, 0.0).astype(jnp.bfloat16)
+    for step in range(GROUPS):
+        kv = outs[2 * step]
+        kv[kv.shape[0] - 16 :, :] = flags
+    for copy in started:
+        copy.wait()
+
+
+def pack(seq, width, lengths, q, k, v, ck, cv):
+    tokens, slots = q.shape[0], ck.shape[0]
+    kv = jax.ShapeDtypeStruct((2 * tokens + 2 * slots + 16, width), jnp.bfloat16)
+    qs = jax.ShapeDtypeStruct((tokens, width), jnp.bfloat16)
+    return pl.pallas_call(
+        functools.partial(pack_kernel, seq, width, slots),
+        out_shape=(kv, qs) * GROUPS,
+        in_specs=[pl.BlockSpec(memory_space=pltpu.SMEM)] + [outside()] * 5,
+        out_specs=[inside()] * (2 * GROUPS),
+        scratch_shapes=[pltpu.SemaphoreType.DMA((5 * GROUPS,))],
+        compiler_params=pltpu.CompilerParams(vmem_limit_bytes=4 << 20),
+        name="pack",
+    )(lengths, q, k, v, ck, cv)
+
+
+def gather_kernel(n_kv, tokens, slots, *refs):
+    kvs, (keys, values, usable) = refs[:n_kv], refs[n_kv:]
+    block = n_kv * tokens
+    for i, kv in enumerate(kvs):
+        keys[i * tokens : (i + 1) * tokens, :] = kv[0:tokens, :]
+        values[i * tokens : (i + 1) * tokens, :] = kv[tokens : 2 * tokens, :]
+        at = slice(block + i * slots, block + (i + 1) * slots)
+        keys[at, :] = kv[2 * tokens : 2 * tokens + slots, :]
+        values[at, :] = kv[2 * tokens + slots : 2 * tokens + 2 * slots, :]
+    lane = lax.broadcasted_iota(jnp.int32, (16, 128), 1)
+    each = 128 // slots
+    for start in range(0, n_kv, each):
+        row = jnp.zeros((16, 128), jnp.float32)
+        for j in range(each):
+            kv = kvs[start + j]
+            flag = kv[kv.shape[0] - 16 :, 0:128].astype(jnp.float32)
+            row = jnp.where(lax.div(lane, slots) == j, flag, row)
+        usable[:, start * slots : start * slots + 128] = row
+
+
+def attend_rows(keys, values, usable, query, block, cols):
+    scale = math.log2(math.e) / math.sqrt(DH)
+    contract = (((1,), (1,)), ((), ()))
+    main = lax.dot_general(
+        query, keys[0:block, cols], contract, preferred_element_type=jnp.float32
+    )
+    tail = lax.dot_general(
+        query, keys[block:, cols], contract, preferred_element_type=jnp.float32
+    )
+    tail = jnp.where(usable, tail, -3e38)
+    top = jnp.maximum(jnp.max(main, axis=1, keepdims=True), jnp.max(tail, axis=1, keepdims=True))
+    main = jnp.exp2((main - top) * scale)
+    tail = jnp.exp2((tail - top) * scale)
+    total = jnp.sum(main, axis=1, keepdims=True) + jnp.sum(tail, axis=1, keepdims=True)
+    mixed = jnp.dot(
+        main.astype(jnp.bfloat16), values[0:block, cols], preferred_element_type=jnp.float32
+    ) + jnp.dot(tail.astype(jnp.bfloat16), values[block:, cols], preferred_element_type=jnp.float32)
+    return (mixed / total).astype(jnp.bfloat16)
+
+
+def attend_kernel(block, n_q, *refs):
+    keys, values, usable = refs[:3]
+    qs, outs = refs[3 : 3 + n_q], refs[3 + n_q : 3 + 2 * n_q]
+    query = refs[3 + 2 * n_q]
+    tokens = qs[0].shape[0]
+    flags = usable[0:1, :] > 0.5
+    for j in range(n_q):
+        query[j * tokens : (j + 1) * tokens, :] = qs[j][...]
+    for h in range(keys.shape[1] // DH):
+        cols = slice(h * DH, (h + 1) * DH)
+        out = attend_rows(keys, values, flags, query[:, cols], block, cols)
+        for j in range(n_q):
+            outs[j][:, cols] = out[j * tokens : (j + 1) * tokens]
+
+
+def gather_and_attend_kernel(n_kv, n_q, tokens, slots, *refs):
+    kvs, qs = refs[:n_kv], refs[n_kv : n_kv + n_q]
+    outs = refs[n_kv + n_q : n_kv + 2 * n_q]
+    whole, query = refs[n_kv + 2 * n_q : -1], refs[-1]
+    gather_kernel(n_kv, tokens, slots, *kvs, *whole)
+    attend_kernel(n_kv * tokens, n_q, *whole, *qs, *outs, query)
+
+
+def gather_and_attend(kvs, qs, slots):
+    tokens, width = qs[0].shape
+    rows = len(kvs) * (tokens + slots)
+    out = jax.ShapeDtypeStruct((tokens, width), jnp.bfloat16)
+    rows_kept = jax.ShapeDtypeStruct((rows, width), jnp.bfloat16)
+    flags = jax.ShapeDtypeStruct((16, len(kvs) * slots), jnp.float32)
+    made = pl.pallas_call(
+        functools.partial(gather_and_attend_kernel, len(kvs), len(qs), tokens, slots),
+        out_shape=[out] * len(qs) + [rows_kept, rows_kept, flags],
+        in_specs=[inside()] * (len(kvs) + len(qs)),
+        out_specs=[inside()] * (len(qs) + 3),
+        scratch_shapes=[pltpu.VMEM((len(qs) * tokens, width), jnp.bfloat16)],
+        compiler_params=pltpu.CompilerParams(vmem_limit_bytes=24 << 20),
+        name="gather_and_attend",
+    )(*kvs, *qs)
+    return made[: len(qs)], made[len(qs) :]
+
+
+def attend(kept, qs, block):
+    tokens, width = qs[0].shape
+    return pl.pallas_call(
+        functools.partial(attend_kernel, block, len(qs)),
+        out_shape=[jax.ShapeDtypeStruct((tokens, width), jnp.bfloat16)] * len(qs),
+        in_specs=[inside()] * (3 + len(qs)),
+        out_specs=[inside()] * len(qs),
+        scratch_shapes=[pltpu.VMEM((len(qs) * tokens, width), jnp.bfloat16)],
+        compiler_params=pltpu.CompilerParams(vmem_limit_bytes=16 << 20),
+        name="attend",
+    )(*kept, *qs)
+
+
+def stage_kernel(seq, other, w, after, out, sems):
+    del after
+    me = lax.div(lax.axis_index("seq"), seq // GROUPS)
+    x = lax.axis_index("head")
+    half = lax.bitwise_xor(x, 1) if other else x
+    width, n = out.shape[0] // GROUPS, out.shape[1]
+    cols = pl.ds(pl.multiple_of(half * n, n), n)
+    copies = []
+    for j in range(GROUPS):
+        rows = pl.ds(pl.multiple_of(lax.bitwise_xor(me, j) * width, width), width)
+        copies.append(
+            pltpu.make_async_copy(w.at[rows, cols], out.at[pl.ds(j * width, width), :], sems.at[j])
+        )
+    for copy in copies:
+        copy.start()
+    for copy in copies:
+        copy.wait()
+
+
+def stage(seq, other, w, after):
+    return pl.pallas_call(
+        functools.partial(stage_kernel, seq, other),
+        out_shape=jax.ShapeDtypeStruct((w.shape[0], w.shape[1] // 2), w.dtype),
+        in_specs=[outside(), outside()],
+        out_specs=inside(),
+        scratch_shapes=[pltpu.SemaphoreType.DMA((GROUPS,))],
+        compiler_params=pltpu.CompilerParams(vmem_limit_bytes=45 << 20),
+        name="stage_other" if other else "stage_own",
+    )(w, after)
+
+
+def project_kernel(start, n_parts, *refs):
+    parts, w, out = refs[:n_parts], refs[n_parts], refs[n_parts + 1]
+    n = out.shape[1]
+    attended = jnp.concatenate([p[...] for p in parts], axis=1)
+    out[...] = jnp.dot(
+        attended, w[:, start : start + n], preferred_element_type=jnp.float32
+    ).astype(out.dtype)
+
+
+def project(parts, w, start, n, dtype):
+    return pl.pallas_call(
+        functools.partial(project_kernel, start, len(parts)),
+        out_shape=jax.ShapeDtypeStruct((parts[0].shape[0], n), dtype),
+        in_specs=[inside()] * (len(parts) + 1),
+        out_specs=inside(),
+        compiler_params=pltpu.CompilerParams(vmem_limit_bytes=8 << 20),
+        name="project",
+    )(*parts, w)
+
+
+def add_kernel(own, *refs):
+    out, start = refs[-1], 0
+    for piece in refs[:-1]:
+        n = piece.shape[1]
+        at = slice(start, start + n)
+        out[:, at] = (own[:, at] + piece[...].astype(jnp.float32)).astype(out.dtype)
+        start += n
+
+
+def add(own, pieces):
+    return pl.pallas_call(
+        add_kernel,
+        out_shape=jax.ShapeDtypeStruct(own.shape, jnp.bfloat16),
+        in_specs=[inside()] * (1 + len(pieces)),
+        out_specs=inside(),
+        compiler_params=pltpu.CompilerParams(vmem_limit_bytes=4 << 20),
+        name="add",
+    )(own, *pieces)
+
+
+def dealt_plan(
+    seq, queries, block_keys, block_values, cache_keys, cache_values, cache_lengths, out_weight
+):
+    tokens, slots = queries.shape[0], cache_keys.shape[0]
+    width = queries.shape[1] // GROUPS
+    stride = seq // GROUPS
+    rows_y = stride // CORES
+
+    def over(x, flip):
+        return lax.ppermute(x, "seq", [(s, s ^ flip) for s in range(seq)])
+
+    def over_z(x, step):
+        return over(x, step * stride)
+
+    def over_y(x, step):
+        return over(x, step * CORES)
+
+    packed = pack(
+        seq, width, cache_lengths, queries, block_keys, block_values, cache_keys, cache_values
+    )
+    kvs = [packed[0]] + [over_z(packed[2 * j], j) for j in range(1, GROUPS)]
+    qs = [packed[1]] + [over_z(packed[2 * j + 1], j) for j in range(1, GROUPS)]
+    gathered = []
+    for kv in kvs:
+        near = [kv] + [over_y(kv, j) for j in range(1, rows_y)]
+        for piece in near:
+            gathered += [piece, over(piece, 1)]
+    late, kept = gather_and_attend(gathered, qs[2:], slots)
+    early = attend(kept, qs[:2], len(gathered) * tokens)
+    parts = [early[0], over_z(early[1], 1), over_z(late[0], 2), over_z(late[1], 3)]
+    w_other = stage(seq, True, out_weight, packed[1])
+    w_own = stage(seq, False, out_weight, packed[1])
+    half = w_own.shape[1]
+    cuts = [0, half // 4, half]
+    arrived = []
+    for i in range(len(cuts) - 1):
+        theirs = project(parts, w_other, cuts[i], cuts[i + 1] - cuts[i], jnp.bfloat16)
+        arrived.append(lax.ppermute(theirs, "head", [(0, 1), (1, 0)]))
+    own = project(parts, w_own, 0, half, jnp.float32)
+    return add(own, arrived)
+
+
+def on_device(seq, head, *args):
+    queries, cache_keys = args[0], args[3]
+    heads_here = queries.shape[1] // DH
+    slots = cache_keys.shape[0]
+    rows_y = seq // (GROUPS * CORES)
+    fits = (
+        head == 2
+        and seq % (GROUPS * CORES) == 0
+        and rows_y & (rows_y - 1) == 0
+        and heads_here % GROUPS == 0
+        and slots == 16
+        and (seq * slots) % 128 == 0
+        and queries.shape[0] % 16 == 0
+        and args[6].shape[1] % 1024 == 0
+    )
+    return dealt_plan(seq, *args) if fits else gathered_plan(*args)
+
+
 def solution(mesh):
     return jax.shard_map(
-        on_device,
+        functools.partial(on_device, mesh.shape["seq"], mesh.shape["head"]),
         mesh=mesh,
         in_specs=(
             P("seq", "head"),

time: 206 us -> 89 us (0.43)
  blocking collectives: 62.3 us -> 0 us
  waiting for transfers between devices: 74.4 us -> 37.3 us
  starting transfers between devices: 0.08 us -> 28.1 us
  matrix products: 24.1 us -> 0 us
  Pallas kernels: 0 us -> 16.8 us
  other arithmetic: 13.7 us -> 0 us
  between operations: 13.8 us -> 0.76 us
  local copies, waits for them, and re-layouts: 16.6 us -> 4.58 us
    all_gather x2 -> x0, waiting for transfers between devices: 51.5 us -> none  [the longest x1 51.5 us: on_device(): lax.all_gather(block_values, 'seq', axis=0, tiled=True)]
    all_gather x2 -> x0, blocking collectives: 47 us -> none  [the longest x1 25.3 us: on_device(): lax.all_gather(cache_values, 'seq', axis=0, tiled=True)]
    ppermute x0 -> x23, waiting for transfers between devices: none -> 37.3 us  [the longest x21 29.9 us: over(): return lax.ppermute(x, 'seq', [(s, s ^ flip) for s in range(seq)])]
    ppermute x0 -> x23, starting transfers between devices: none -> 28.1 us  [the longest x21 26 us: over(): return lax.ppermute(x, 'seq', [(s, s ^ flip) for s in range(seq)])]
    dot_general x5 -> x0, matrix products: 24.1 us -> none  [the longest x2 10 us: fold_keys(): jnp.einsum('hqk,khd->hqd', weights.astype(jnp.bfloat16), value_heads, pre...]
    reduce_scatter x1 -> x0, waiting for transfers between devices: 22.1 us -> none  [on_device(): lax.psum_scatter(partial_terms.astype(jnp.bfloat16), 'head', scatter_dime...]
    pallas_call x0 -> x9, Pallas kernels: none -> 16.8 us  [the longest x2 6.69 us: stage(): pl.pallas_call(functools.partial(stage_kernel, seq, other), out_shape=jax...]
    unnamed x1 -> x0, blocking collectives: 15.3 us -> none
  transfers between devices with their start and end apart: 3 -> 23, of which waited for: 2 -> 8; matrix products, arithmetic and copies ran while one was open for 11% -> 0% of each run, Pallas kernels for 0% -> 13%
where the time goes in v1:
time: 89 us; the launch traced here: 87.6 us
  waiting for transfers between devices  37.3 us (42%)
  starting transfers between devices  28.1 us (32%)
  Pallas kernels  16.8 us (19%)
  local copies, waits for them, and re-layouts  4.58 us (5%)
    ppermute x21, waiting for transfers between devices, over(): return lax.ppermute(x, 'seq', [(s, s ^ flip) for s in range(seq)])  29.9 us
    ppermute x21, starting transfers between devices, over(): return lax.ppermute(x, 'seq', [(s, s ^ flip) for s in range(seq)])  26 us
    ppermute x2, waiting for transfers between devices, dealt_plan(): arrived.append(lax.ppermute(theirs, 'head', [(0, 1), (1, 0)]))  7.45 us
    pallas_call x2, Pallas kernels, stage(): pl.pallas_call(functools.partial(stage_kernel, seq, other), out_shape=jax...  6.69 us
    unnamed x10, local copies, waits for them, and re-layouts  4.58 us
    pallas_call x1, Pallas kernels, gather_and_attend(): pl.pallas_call(functools.partial(gather_and_attend_kernel, len(kvs), len(...  3.18 us
    pallas_call x1, Pallas kernels, attend(): pl.pallas_call(functools.partial(attend_kernel, block, len(qs)), out_shap...  2.91 us
    pallas_call x3, Pallas kernels, project(): pl.pallas_call(functools.partial(project_kernel, start, len(parts)), out_...  2.65 us
  transfers between devices with their start and end apart: 23, of which 8 were waited for; matrix products, arithmetic and copies ran while one was open for 0% of the time, Pallas kernels for 13%

profile of v1, /device:TPU:0, one launch (start us, length us, event | category | flops | bytes accessed | tf_op | source)
XLA Modules:
  0.0 87.6 jit_solution(10518309867306403466)
XLA Ops:
  0.7 1.0 %copy-done = bf16[128,1536]{1,0:T(8,128)(2,1)S(1)} copy-done((bf16[128,1536]{1,0:T(8,128)(2,1)S(1)}, bf16[128,1536]{1,0:T(8,128)(2,1)}, u32[]{:S(2)}) %copy-start) | copy-done | bytes 393240
  1.7 1.0 %copy-done.1 = bf16[128,1536]{1,0:T(8,128)(2,1)S(1)} copy-done((bf16[128,1536]{1,0:T(8,128)(2,1)S(1)}, bf16[128,1536]{1,0:T(8,128)(2,1)}, u32[]{:S(2)}) %copy-start.1) | copy-done | bytes 393240
  2.6 1.0 %copy-done.2 = bf16[128,1536]{1,0:T(8,128)(2,1)S(1)} copy-done((bf16[128,1536]{1,0:T(8,128)(2,1)S(1)}, bf16[128,1536]{1,0:T(8,128)(2,1)}, u32[]{:S(2)}) %copy-start.2) | copy-done | bytes 393240
  3.6 0.8 copy-done.3
  4.4 0.8 copy-done.4
  5.7 4.1 %collective-permute-start.15 = (bf16[128,384]{1,0:T(8,128)(2,1)S(1)}, bf16[128,384]{1,0:T(8,128)(2,1)S(1)}, u32[]{:S(2)}, u32[]{:S(2)}) collective-permute-start(bf16[128,384]{1,0:T(8,128)(2,1)S(1)} %get-tuple-element.24), channel_id=1, source_target_pairs={{0,16},{2,18},{4,20},{6,22},{8,24},{10,26},{12,28},{14,30},{16,0},... | collective-permute-start | bytes 294920 | tf_op jit(solution)/shard_map/ppermute | solution.py:303
  9.8 1.3 %collective-permute-start.16 = (bf16[128,384]{1,0:T(8,128)(2,1)S(1)}, bf16[128,384]{1,0:T(8,128)(2,1)S(1)}, u32[]{:S(2)}, u32[]{:S(2)}) collective-permute-start(bf16[128,384]{1,0:T(8,128)(2,1)S(1)} %get-tuple-element.25), channel_id=1, source_target_pairs={{0,24},{2,26},{4,28},{6,30},{8,16},{10,18},{12,20},{14,22},{16,8},... | collective-permute-start | bytes 294920 | tf_op jit(solution)/shard_map/ppermute | solution.py:303
  11.4 2.8 %collective-permute-start.7 = (bf16[304,384]{1,0:T(8,128)(2,1)S(1)}, bf16[304,384]{1,0:T(8,128)(2,1)S(1)}, u32[]{:S(2)}, u32[]{:S(2)}) collective-permute-start(bf16[304,384]{1,0:T(8,128)(2,1)S(1)} %get-tuple-element.22), channel_id=1, source_target_pairs={{0,16},{2,18},{4,20},{6,22},{8,24},{10,26},{12,28},{14,30},{16,0},... | collective-permute-start | bytes 700424 | tf_op jit(solution)/shard_map/ppermute | solution.py:303
  14.2 1.3 %collective-permute-start.11 = (bf16[304,384]{1,0:T(8,128)(2,1)S(1)}, bf16[304,384]{1,0:T(8,128)(2,1)S(1)}, u32[]{:S(2)}, u32[]{:S(2)}) collective-permute-start(bf16[304,384]{1,0:T(8,128)(2,1)S(1)} %get-tuple-element.23), channel_id=1, source_target_pairs={{0,24},{2,26},{4,28},{6,30},{8,16},{10,18},{12,20},{14,22},{16,8},... | collective-permute-start | bytes 700424 | tf_op jit(solution)/shard_map/ppermute | solution.py:303
  15.5 2.2 %collective-permute-done.15.refs_16_ = bf16[128,384]{1,0:T(8,128)(2,1)S(1)} collective-permute-done((bf16[128,384]{1,0:T(8,128)(2,1)S(1)}, bf16[128,384]{1,0:T(8,128)(2,1)S(1)}, u32[]{:S(2)}, u32[]{:S(2)}) %collective-permute-start.15) | collective-permute-done | bytes 98336 | tf_op jit(solution)/shard_map/ppermute | solution.py:303
  17.7 1.7 %collective-permute-start.1 = (bf16[304,384]{1,0:T(8,128)(2,1)S(1)}, bf16[304,384]{1,0:T(8,128)(2,1)S(1)}, u32[]{:S(2)}, u32[]{:S(2)}) collective-permute-start(bf16[304,384]{1,0:T(8,128)(2,1)S(1)} %get-tuple-element.20.refs_0_), channel_id=1, source_target_pairs={{0,4},{2,6},{4,0},{6,2},{8,12},{10,14},{12,8},{14,10},{16,20},{18,... | collective-permute-start | bytes 700424 | tf_op jit(solution)/shard_map/ppermute | solution.py:303
  19.4 3.7 %collective-permute-done.3.refs_4_ = bf16[304,384]{1,0:T(8,128)(2,1)S(1)} collective-permute-done((bf16[304,384]{1,0:T(8,128)(2,1)S(1)}, bf16[304,384]{1,0:T(8,128)(2,1)S(1)}, u32[]{:S(2)}, u32[]{:S(2)}) %collective-permute-start.3) | collective-permute-done | bytes 233504 | tf_op jit(solution)/shard_map/ppermute | solution.py:303
  23.1 1.5 %collective-permute-start.5 = (bf16[304,384]{1,0:T(8,128)(2,1)S(1)}, bf16[304,384]{1,0:T(8,128)(2,1)S(1)}, u32[]{:S(2)}, u32[]{:S(2)}) collective-permute-start(bf16[304,384]{1,0:T(8,128)(2,1)S(1)} %collective-permute-done.3.refs_4_), channel_id=1, source_target_pairs={{0,4},{2,6},{4,0},{6,2},{8,12},{10,14},{12,8},{14,10},{16,20},{18,... | collective-permute-start | bytes 700424 | tf_op jit(solution)/shard_map/ppermute | solution.py:303
  24.6 10.2 %collective-permute-done.7.refs_8_ = bf16[304,384]{1,0:T(8,128)(2,1)S(1)} collective-permute-done((bf16[304,384]{1,0:T(8,128)(2,1)S(1)}, bf16[304,384]{1,0:T(8,128)(2,1)S(1)}, u32[]{:S(2)}, u32[]{:S(2)}) %collective-permute-start.7) | collective-permute-done | bytes 233504 | tf_op jit(solution)/shard_map/ppermute | solution.py:303
  34.8 1.7 %collective-permute-start.9 = (bf16[304,384]{1,0:T(8,128)(2,1)S(1)}, bf16[304,384]{1,0:T(8,128)(2,1)S(1)}, u32[]{:S(2)}, u32[]{:S(2)}) collective-permute-start(bf16[304,384]{1,0:T(8,128)(2,1)S(1)} %collective-permute-done.7.refs_8_), channel_id=1, source_target_pairs={{0,4},{2,6},{4,0},{6,2},{8,12},{10,14},{12,8},{14,10},{16,20},{18,... | collective-permute-start | bytes 700424 | tf_op jit(solution)/shard_map/ppermute | solution.py:303
  37.6 5.8 %collective-permute-done.9.refs_10_ = bf16[304,384]{1,0:T(8,128)(2,1)S(1)} collective-permute-done((bf16[304,384]{1,0:T(8,128)(2,1)S(1)}, bf16[304,384]{1,0:T(8,128)(2,1)S(1)}, u32[]{:S(2)}, u32[]{:S(2)}) %collective-permute-start.9) | collective-permute-done | bytes 233504 | tf_op jit(solution)/shard_map/ppermute | solution.py:303
  43.9 4.0 %collective-permute-done.13.refs_14_ = bf16[304,384]{1,0:T(8,128)(2,1)S(1)} collective-permute-done((bf16[304,384]{1,0:T(8,128)(2,1)S(1)}, bf16[304,384]{1,0:T(8,128)(2,1)S(1)}, u32[]{:S(2)}, u32[]{:S(2)}) %collective-permute-start.13) | collective-permute-done | bytes 233504 | tf_op jit(solution)/shard_map/ppermute | solution.py:303
  47.9 4.4 %collective-permute-start.17 = (bf16[128,384]{1,0:T(8,128)(2,1)S(1)}, bf16[128,384]{1,0:T(8,128)(2,1)S(1)}, u32[]{:S(2)}, u32[]{:S(2)}) collective-permute-start(bf16[128,384]{1,0:T(8,128)(2,1)S(1)} %get-tuple-element.30), channel_id=1, source_target_pairs={{0,8},{2,10},{4,12},{6,14},{8,0},{10,2},{12,4},{14,6},{16,24},{18,... | collective-permute-start | bytes 294920 | tf_op jit(solution)/shard_map/ppermute | solution.py:303
  52.3 3.2 %gather_and_attend.1 = (bf16[128,384]{1,0:T(8,128)(2,1)S(1)}, bf16[128,384]{1,0:T(8,128)(2,1)S(1)}, bf16[2304,384]{1,0:T(8,128)(2,1)S(1)}, bf16[2304,384]{1,0:T(8,128)(2,1)S(1)}, f32[16,256]{1,0:T(8,128)S(1)}) custom-call(bf16[304,384]{1,0:T(8,128)(2,1)S(1)} %get-tuple-element.20.refs_0_, bf16[304,384]{1,0:T(8,128)(2,1)S(1)} %collective-permute-done.refs_1_, ...), custom_call_target="tpu_custom_call" | custom-call | tf_op jit(solution)/shard_map/gather_and_attend/pallas_call | solution.py:198
  55.8 2.9 %attend.1 = (bf16[128,384]{1,0:T(8,128)(2,1)S(1)}, bf16[128,384]{1,0:T(8,128)(2,1)S(1)}) custom-call(bf16[2304,384]{1,0:T(8,128)(2,1)S(1)} %get-tuple-element.26.refs_0_, bf16[2304,384]{1,0:T(8,128)(2,1)S(1)} %get-tuple-element.27.refs_1_, f32[16,256]{1,0:T(8,128)S(1)} %get-tuple-element.28.refs_2_, bf16[128,384]{1,0:T(8,128)(2,1)S(1)} %get-tuple-element.29.refs_3_.after, ...), custom_call_target="tpu_custom_call" | custom-call | tf_op jit(solution)/shard_map/attend/pallas_call | solution.py:212
  58.7 1.8 %collective-permute-start.18 = (bf16[128,384]{1,0:T(8,128)(2,1)S(1)}, bf16[128,384]{1,0:T(8,128)(2,1)S(1)}, u32[]{:S(2)}, u32[]{:S(2)}) collective-permute-start(bf16[128,384]{1,0:T(8,128)(2,1)S(1)} %get-tuple-element.32), channel_id=1, source_target_pairs={{0,8},{2,10},{4,12},{6,14},{8,0},{10,2},{12,4},{14,6},{16,24},{18,... | collective-permute-start | bytes 294920 | tf_op jit(solution)/shard_map/ppermute | solution.py:303
  60.5 2.2 %collective-permute-start.19 = (bf16[128,384]{1,0:T(8,128)(2,1)S(1)}, bf16[128,384]{1,0:T(8,128)(2,1)S(1)}, u32[]{:S(2)}, u32[]{:S(2)}) collective-permute-start(bf16[128,384]{1,0:T(8,128)(2,1)S(1)} %get-tuple-element.33), channel_id=1, source_target_pairs={{0,16},{2,18},{4,20},{6,22},{8,24},{10,26},{12,28},{14,30},{16,0},... | collective-permute-start | bytes 294920 | tf_op jit(solution)/shard_map/ppermute | solution.py:303
  62.7 1.2 %collective-permute-start.20 = (bf16[128,384]{1,0:T(8,128)(2,1)S(1)}, bf16[128,384]{1,0:T(8,128)(2,1)S(1)}, u32[]{:S(2)}, u32[]{:S(2)}) collective-permute-start(bf16[128,384]{1,0:T(8,128)(2,1)S(1)} %get-tuple-element.34), channel_id=1, source_target_pairs={{0,24},{2,26},{4,28},{6,30},{8,16},{10,18},{12,20},{14,22},{16,8},... | collective-permute-start | bytes 294920 | tf_op jit(solution)/shard_map/ppermute | solution.py:303
  63.9 3.3 %stage_other.1.refs_4_ = bf16[1536,2560]{1,0:T(8,128)(2,1)S(1)} custom-call(bf16[1536,5120]{1,0:T(8,128)(2,1)} %w.3, bf16[128,384]{1,0:T(8,128)(2,1)S(1)} %get-tuple-element.29.refs_3_.after), custom_call_target="tpu_custom_call" | custom-call | tf_op jit(solution)/shard_map/stage_other/pallas_call | solution.py:243
  67.2 3.8 %collective-permute-done.19.refs_2_ = bf16[128,384]{1,0:T(8,128)(2,1)S(1)} collective-permute-done((bf16[128,384]{1,0:T(8,128)(2,1)S(1)}, bf16[128,384]{1,0:T(8,128)(2,1)S(1)}, u32[]{:S(2)}, u32[]{:S(2)}) %collective-permute-start.19) | collective-permute-done | bytes 98336 | tf_op jit(solution)/shard_map/ppermute | solution.py:303
  71.0 1.0 %project.5 = bf16[128,1920]{1,0:T(8,128)(2,1)S(1)} custom-call(bf16[128,384]{1,0:T(8,128)(2,1)S(1)} %get-tuple-element.31.refs_0_, bf16[128,384]{1,0:T(8,128)(2,1)S(1)} %collective-permute-done.18.refs_1_, bf16[128,384]{1,0:T(8,128)(2,1)S(1)} %collective-permute-done.19.refs_2_, bf16[128,384]{1,0:T(8,128)(2,1)S(1)} %collective-permute-done.20.refs_3_, ...), custom_call_target="tpu_custom_call" | custom-call | tf_op jit(solution)/shard_map/project/pallas_call | solution.py:264
  72.0 1.6 %collective-permute-start.22 = (bf16[128,1920]{1,0:T(8,128)(2,1)S(1)}, bf16[128,1920]{1,0:T(8,128)(2,1)S(1)}, u32[]{:S(2)}, u32[]{:S(2)}) collective-permute-start(bf16[128,1920]{1,0:T(8,128)(2,1)S(1)} %project.5), channel_id=1, source_target_pairs={{0,1},{1,0},{2,3},{3,2},{4,5},{5,4},{6,7},{7,6},{8,9},{9,8},{10,11... | collective-permute-start | bytes 1474568 | tf_op jit(solution)/shard_map/ppermute | solution.py:331
  74.0 0.6 collective-permute-start.21
  74.6 3.3 %stage_own.1.refs_4_ = bf16[1536,2560]{1,0:T(8,128)(2,1)S(1)} custom-call(bf16[1536,5120]{1,0:T(8,128)(2,1)} %w.3, bf16[128,384]{1,0:T(8,128)(2,1)S(1)} %get-tuple-element.29.refs_3_.after), custom_call_target="tpu_custom_call" | custom-call | tf_op jit(solution)/shard_map/stage_own/pallas_call | solution.py:243
  78.0 1.2 %project.3.own = f32[128,2560]{1,0:T(8,128)S(1)} custom-call(bf16[128,384]{1,0:T(8,128)(2,1)S(1)} %get-tuple-element.31.refs_0_, bf16[128,384]{1,0:T(8,128)(2,1)S(1)} %collective-permute-done.18.refs_1_, bf16[128,384]{1,0:T(8,128)(2,1)S(1)} %collective-permute-done.19.refs_2_, bf16[128,384]{1,0:T(8,128)(2,1)S(1)} %collective-permute-done.20.refs_3_, ...), custom_call_target="tpu_custom_call" | custom-call | tf_op jit(solution)/shard_map/project/pallas_call | solution.py:264
  79.2 7.4 %collective-permute-done.21.refs_0_ = bf16[128,640]{1,0:T(8,128)(2,1)S(1)} collective-permute-done((bf16[128,640]{1,0:T(8,128)(2,1)S(1)}, bf16[128,640]{1,0:T(8,128)(2,1)S(1)}, u32[]{:S(2)}, u32[]{:S(2)}) %collective-permute-start.21) | collective-permute-done | bytes 163872 | tf_op jit(solution)/shard_map/ppermute | solution.py:331
  86.6 0.9 %add.1 = bf16[128,2560]{1,0:T(8,128)(2,1)} custom-call(f32[128,2560]{1,0:T(8,128)S(1)} %project.3.own, bf16[128,640]{1,0:T(8,128)(2,1)S(1)} %collective-permute-done.21.refs_0_, bf16[128,1920]{1,0:T(8,128)(2,1)S(1)} %collective-permute-done.22.refs_1_), custom_call_target="tpu_custom_call" | custom-call | tf_op jit(solution)/shard_map/add/pallas_call | solution.py:284
  (33 shorter events, 3.0 us)
Async XLA Ops:
  0.7 1.0 %copy-start = (bf16[128,1536]{1,0:T(8,128)(2,1)S(1)}, bf16[128,1536]{1,0:T(8,128)(2,1)}, u32[]{:S(2)}) copy-start(bf16[128,1536]{1,0:T(8,128)(2,1)} %q.1) | copy-start | bytes 1179652
  1.6 1.0 %copy-start.1 = (bf16[128,1536]{1,0:T(8,128)(2,1)S(1)}, bf16[128,1536]{1,0:T(8,128)(2,1)}, u32[]{:S(2)}) copy-start(bf16[128,1536]{1,0:T(8,128)(2,1)} %k.1) | copy-start | bytes 1179652
  2.6 1.0 %copy-start.2 = (bf16[128,1536]{1,0:T(8,128)(2,1)S(1)}, bf16[128,1536]{1,0:T(8,128)(2,1)}, u32[]{:S(2)}) copy-start(bf16[128,1536]{1,0:T(8,128)(2,1)} %v.1) | copy-start | bytes 1179652
  3.6 0.8 copy-start.3
  4.4 0.8 copy-start.4
  5.7 12.0 %collective-permute-start.15 = (bf16[128,384]{1,0:T(8,128)(2,1)S(1)}, bf16[128,384]{1,0:T(8,128)(2,1)S(1)}, u32[]{:S(2)}, u32[]{:S(2)}) collective-permute-start(bf16[128,384]{1,0:T(8,128)(2,1)S(1)} %get-tuple-element.24), channel_id=1, source_target_pairs={{0,16},{2,18},{4,20},{6,22},{8,24},{10,26},{12,28},{14,30},{16,0},... | collective-permute-start | bytes 294920 | tf_op jit(solution)/shard_map/ppermute | solution.py:303
  9.8 9.6 %collective-permute-start.16 = (bf16[128,384]{1,0:T(8,128)(2,1)S(1)}, bf16[128,384]{1,0:T(8,128)(2,1)S(1)}, u32[]{:S(2)}, u32[]{:S(2)}) collective-permute-start(bf16[128,384]{1,0:T(8,128)(2,1)S(1)} %get-tuple-element.25), channel_id=1, source_target_pairs={{0,24},{2,26},{4,28},{6,30},{8,16},{10,18},{12,20},{14,22},{16,8},... | collective-permute-start | bytes 294920 | tf_op jit(solution)/shard_map/ppermute | solution.py:303
  11.1 11.9 %collective-permute-start.3 = (bf16[304,384]{1,0:T(8,128)(2,1)S(1)}, bf16[304,384]{1,0:T(8,128)(2,1)S(1)}, u32[]{:S(2)}, u32[]{:S(2)}) collective-permute-start(bf16[304,384]{1,0:T(8,128)(2,1)S(1)} %get-tuple-element.21), channel_id=1, source_target_pairs={{0,8},{2,10},{4,12},{6,14},{8,0},{10,2},{12,4},{14,6},{16,24},{18,... | collective-permute-start | bytes 700424 | tf_op jit(solution)/shard_map/ppermute | solution.py:303
  11.4 23.4 %collective-permute-start.7 = (bf16[304,384]{1,0:T(8,128)(2,1)S(1)}, bf16[304,384]{1,0:T(8,128)(2,1)S(1)}, u32[]{:S(2)}, u32[]{:S(2)}) collective-permute-start(bf16[304,384]{1,0:T(8,128)(2,1)S(1)} %get-tuple-element.22), channel_id=1, source_target_pairs={{0,16},{2,18},{4,20},{6,22},{8,24},{10,26},{12,28},{14,30},{16,0},... | collective-permute-start | bytes 700424 | tf_op jit(solution)/shard_map/ppermute | solution.py:303
  14.2 20.6 %collective-permute-start.11 = (bf16[304,384]{1,0:T(8,128)(2,1)S(1)}, bf16[304,384]{1,0:T(8,128)(2,1)S(1)}, u32[]{:S(2)}, u32[]{:S(2)}) collective-permute-start(bf16[304,384]{1,0:T(8,128)(2,1)S(1)} %get-tuple-element.23), channel_id=1, source_target_pairs={{0,24},{2,26},{4,28},{6,30},{8,16},{10,18},{12,20},{14,22},{16,8},... | collective-permute-start | bytes 700424 | tf_op jit(solution)/shard_map/ppermute | solution.py:303
  17.7 18.8 %collective-permute-start.1 = (bf16[304,384]{1,0:T(8,128)(2,1)S(1)}, bf16[304,384]{1,0:T(8,128)(2,1)S(1)}, u32[]{:S(2)}, u32[]{:S(2)}) collective-permute-start(bf16[304,384]{1,0:T(8,128)(2,1)S(1)} %get-tuple-element.20.refs_0_), channel_id=1, source_target_pairs={{0,4},{2,6},{4,0},{6,2},{8,12},{10,14},{12,8},{14,10},{16,20},{18,... | collective-permute-start | bytes 700424 | tf_op jit(solution)/shard_map/ppermute | solution.py:303
  19.4 17.4 %collective-permute-start = (bf16[304,384]{1,0:T(8,128)(2,1)S(1)}, bf16[304,384]{1,0:T(8,128)(2,1)S(1)}, u32[]{:S(2)}, u32[]{:S(2)}) collective-permute-start(bf16[304,384]{1,0:T(8,128)(2,1)S(1)} %get-tuple-element.20.refs_0_), channel_id=1, source_target_pairs={{0,2},{2,0},{4,6},{6,4},{8,10},{10,8},{12,14},{14,12},{16,18},{18,... | collective-permute-start | bytes 700424 | tf_op jit(solution)/shard_map/ppermute | solution.py:303
  23.1 14.0 %collective-permute-start.5 = (bf16[304,384]{1,0:T(8,128)(2,1)S(1)}, bf16[304,384]{1,0:T(8,128)(2,1)S(1)}, u32[]{:S(2)}, u32[]{:S(2)}) collective-permute-start(bf16[304,384]{1,0:T(8,128)(2,1)S(1)} %collective-permute-done.3.refs_4_), channel_id=1, source_target_pairs={{0,4},{2,6},{4,0},{6,2},{8,12},{10,14},{12,8},{14,10},{16,20},{18,... | collective-permute-start | bytes 700424 | tf_op jit(solution)/shard_map/ppermute | solution.py:303
  34.8 2.3 %collective-permute-start.4 = (bf16[304,384]{1,0:T(8,128)(2,1)S(1)}, bf16[304,384]{1,0:T(8,128)(2,1)S(1)}, u32[]{:S(2)}, u32[]{:S(2)}) collective-permute-start(bf16[304,384]{1,0:T(8,128)(2,1)S(1)} %collective-permute-done.3.refs_4_), channel_id=1, source_target_pairs={{0,2},{2,0},{4,6},{6,4},{8,10},{10,8},{12,14},{14,12},{16,18},{18,... | collective-permute-start | bytes 700424 | tf_op jit(solution)/shard_map/ppermute | solution.py:303
  34.8 8.6 %collective-permute-start.9 = (bf16[304,384]{1,0:T(8,128)(2,1)S(1)}, bf16[304,384]{1,0:T(8,128)(2,1)S(1)}, u32[]{:S(2)}, u32[]{:S(2)}) collective-permute-start(bf16[304,384]{1,0:T(8,128)(2,1)S(1)} %collective-permute-done.7.refs_8_), channel_id=1, source_target_pairs={{0,4},{2,6},{4,0},{6,2},{8,12},{10,14},{12,8},{14,10},{16,20},{18,... | collective-permute-start | bytes 700424 | tf_op jit(solution)/shard_map/ppermute | solution.py:303
  36.5 6.9 %collective-permute-start.8 = (bf16[304,384]{1,0:T(8,128)(2,1)S(1)}, bf16[304,384]{1,0:T(8,128)(2,1)S(1)}, u32[]{:S(2)}, u32[]{:S(2)}) collective-permute-start(bf16[304,384]{1,0:T(8,128)(2,1)S(1)} %collective-permute-done.7.refs_8_), channel_id=1, source_target_pairs={{0,2},{2,0},{4,6},{6,4},{8,10},{10,8},{12,14},{14,12},{16,18},{18,... | collective-permute-start | bytes 700424 | tf_op jit(solution)/shard_map/ppermute | solution.py:303
  36.8 11.2 %collective-permute-start.13 = (bf16[304,384]{1,0:T(8,128)(2,1)S(1)}, bf16[304,384]{1,0:T(8,128)(2,1)S(1)}, u32[]{:S(2)}, u32[]{:S(2)}) collective-permute-start(bf16[304,384]{1,0:T(8,128)(2,1)S(1)} %collective-permute-done.11.refs_12_), channel_id=1, source_target_pairs={{0,4},{2,6},{4,0},{6,2},{8,12},{10,14},{12,8},{14,10},{16,20},{18,... | collective-permute-start | bytes 700424 | tf_op jit(solution)/shard_map/ppermute | solution.py:303
  37.1 10.8 %collective-permute-start.12 = (bf16[304,384]{1,0:T(8,128)(2,1)S(1)}, bf16[304,384]{1,0:T(8,128)(2,1)S(1)}, u32[]{:S(2)}, u32[]{:S(2)}) collective-permute-start(bf16[304,384]{1,0:T(8,128)(2,1)S(1)} %collective-permute-done.11.refs_12_), channel_id=1, source_target_pairs={{0,2},{2,0},{4,6},{6,4},{8,10},{10,8},{12,14},{14,12},{16,18},{18,... | collective-permute-start | bytes 700424 | tf_op jit(solution)/shard_map/ppermute | solution.py:303
  37.1 15.2 %collective-permute-start.2 = (bf16[304,384]{1,0:T(8,128)(2,1)S(1)}, bf16[304,384]{1,0:T(8,128)(2,1)S(1)}, u32[]{:S(2)}, u32[]{:S(2)}) collective-permute-start(bf16[304,384]{1,0:T(8,128)(2,1)S(1)} %collective-permute-done.1.refs_2_), channel_id=1, source_target_pairs={{0,2},{2,0},{4,6},{6,4},{8,10},{10,8},{12,14},{14,12},{16,18},{18,... | collective-permute-start | bytes 700424 | tf_op jit(solution)/shard_map/ppermute | solution.py:303
  43.4 8.9 %collective-permute-start.6 = (bf16[304,384]{1,0:T(8,128)(2,1)S(1)}, bf16[304,384]{1,0:T(8,128)(2,1)S(1)}, u32[]{:S(2)}, u32[]{:S(2)}) collective-permute-start(bf16[304,384]{1,0:T(8,128)(2,1)S(1)} %collective-permute-done.5.refs_6_), channel_id=1, source_target_pairs={{0,2},{2,0},{4,6},{6,4},{8,10},{10,8},{12,14},{14,12},{16,18},{18,... | collective-permute-start | bytes 700424 | tf_op jit(solution)/shard_map/ppermute | solution.py:303
  43.4 8.9 %collective-permute-start.10 = (bf16[304,384]{1,0:T(8,128)(2,1)S(1)}, bf16[304,384]{1,0:T(8,128)(2,1)S(1)}, u32[]{:S(2)}, u32[]{:S(2)}) collective-permute-start(bf16[304,384]{1,0:T(8,128)(2,1)S(1)} %collective-permute-done.9.refs_10_), channel_id=1, source_target_pairs={{0,2},{2,0},{4,6},{6,4},{8,10},{10,8},{12,14},{14,12},{16,18},{18,... | collective-permute-start | bytes 700424 | tf_op jit(solution)/shard_map/ppermute | solution.py:303
  47.9 4.4 %collective-permute-start.14 = (bf16[304,384]{1,0:T(8,128)(2,1)S(1)}, bf16[304,384]{1,0:T(8,128)(2,1)S(1)}, u32[]{:S(2)}, u32[]{:S(2)}) collective-permute-start(bf16[304,384]{1,0:T(8,128)(2,1)S(1)} %collective-permute-done.13.refs_14_), channel_id=1, source_target_pairs={{0,2},{2,0},{4,6},{6,4},{8,10},{10,8},{12,14},{14,12},{16,18},{18,... | collective-permute-start | bytes 700424 | tf_op jit(solution)/shard_map/ppermute | solution.py:303
  47.9 7.8 %collective-permute-start.17 = (bf16[128,384]{1,0:T(8,128)(2,1)S(1)}, bf16[128,384]{1,0:T(8,128)(2,1)S(1)}, u32[]{:S(2)}, u32[]{:S(2)}) collective-permute-start(bf16[128,384]{1,0:T(8,128)(2,1)S(1)} %get-tuple-element.30), channel_id=1, source_target_pairs={{0,8},{2,10},{4,12},{6,14},{8,0},{10,2},{12,4},{14,6},{16,24},{18,... | collective-permute-start | bytes 294920 | tf_op jit(solution)/shard_map/ppermute | solution.py:303
  58.7 8.5 %collective-permute-start.18 = (bf16[128,384]{1,0:T(8,128)(2,1)S(1)}, bf16[128,384]{1,0:T(8,128)(2,1)S(1)}, u32[]{:S(2)}, u32[]{:S(2)}) collective-permute-start(bf16[128,384]{1,0:T(8,128)(2,1)S(1)} %get-tuple-element.32), channel_id=1, source_target_pairs={{0,8},{2,10},{4,12},{6,14},{8,0},{10,2},{12,4},{14,6},{16,24},{18,... | collective-permute-start | bytes 294920 | tf_op jit(solution)/shard_map/ppermute | solution.py:303
  60.5 10.5 %collective-permute-start.19 = (bf16[128,384]{1,0:T(8,128)(2,1)S(1)}, bf16[128,384]{1,0:T(8,128)(2,1)S(1)}, u32[]{:S(2)}, u32[]{:S(2)}) collective-permute-start(bf16[128,384]{1,0:T(8,128)(2,1)S(1)} %get-tuple-element.33), channel_id=1, source_target_pairs={{0,16},{2,18},{4,20},{6,22},{8,24},{10,26},{12,28},{14,30},{16,0},... | collective-permute-start | bytes 294920 | tf_op jit(solution)/shard_map/ppermute | solution.py:303
  62.7 8.3 %collective-permute-start.20 = (bf16[128,384]{1,0:T(8,128)(2,1)S(1)}, bf16[128,384]{1,0:T(8,128)(2,1)S(1)}, u32[]{:S(2)}, u32[]{:S(2)}) collective-permute-start(bf16[128,384]{1,0:T(8,128)(2,1)S(1)} %get-tuple-element.34), channel_id=1, source_target_pairs={{0,24},{2,26},{4,28},{6,30},{8,16},{10,18},{12,20},{14,22},{16,8},... | collective-permute-start | bytes 294920 | tf_op jit(solution)/shard_map/ppermute | solution.py:303
  72.0 14.6 %collective-permute-start.22 = (bf16[128,1920]{1,0:T(8,128)(2,1)S(1)}, bf16[128,1920]{1,0:T(8,128)(2,1)S(1)}, u32[]{:S(2)}, u32[]{:S(2)}) collective-permute-start(bf16[128,1920]{1,0:T(8,128)(2,1)S(1)} %project.5), channel_id=1, source_target_pairs={{0,1},{1,0},{2,3},{3,2},{4,5},{5,4},{6,7},{7,6},{8,9},{9,8},{10,11... | collective-permute-start | bytes 1474568 | tf_op jit(solution)/shard_map/ppermute | solution.py:331
  74.0 12.6 %collective-permute-start.21 = (bf16[128,640]{1,0:T(8,128)(2,1)S(1)}, bf16[128,640]{1,0:T(8,128)(2,1)S(1)}, u32[]{:S(2)}, u32[]{:S(2)}) collective-permute-start(bf16[128,640]{1,0:T(8,128)(2,1)S(1)} %project.4), channel_id=1, source_target_pairs={{0,1},{1,0},{2,3},{3,2},{4,5},{5,4},{6,7},{7,6},{8,9},{9,8},{10,11... | collective-permute-start | bytes 491528 | tf_op jit(solution)/shard_map/ppermute | solution.py:331

commit v2 on v1

--- a/solution.py
+++ b/solution.py
@@ -121,9 +121,25 @@
         in_specs=[pl.BlockSpec(memory_space=pltpu.SMEM)] + [outside()] * 5,
         out_specs=[inside()] * (2 * GROUPS),
         scratch_shapes=[pltpu.SemaphoreType.DMA((5 * GROUPS,))],
-        compiler_params=pltpu.CompilerParams(vmem_limit_bytes=4 << 20),
+        compiler_params=pltpu.CompilerParams(vmem_limit_bytes=61 << 20),
         name="pack",
     )(lengths, q, k, v, ck, cv)
+
+
+def hold_kernel(*refs):
+    for src, dst in zip(refs[: len(refs) // 2], refs[len(refs) // 2 :]):
+        dst[...] = src[...]
+
+
+def hold(*arrays):
+    return pl.pallas_call(
+        hold_kernel,
+        out_shape=[jax.ShapeDtypeStruct(a.shape, a.dtype) for a in arrays],
+        in_specs=[inside()] * len(arrays),
+        out_specs=[inside()] * len(arrays),
+        compiler_params=pltpu.CompilerParams(vmem_limit_bytes=4 << 20),
+        name="hold",
+    )(*arrays)
 
 
 def gather_kernel(n_kv, tokens, slots, *refs):
@@ -220,8 +236,7 @@
     )(*kept, *qs)
 
 
-def stage_kernel(seq, other, w, after, out, sems):
-    del after
+def stage_kernel(seq, other, w, out, sems):
     me = lax.div(lax.axis_index("seq"), seq // GROUPS)
     x = lax.axis_index("head")
     half = lax.bitwise_xor(x, 1) if other else x
@@ -239,16 +254,16 @@
         copy.wait()
 
 
-def stage(seq, other, w, after):
+def stage(seq, other, w):
     return pl.pallas_call(
         functools.partial(stage_kernel, seq, other),
         out_shape=jax.ShapeDtypeStruct((w.shape[0], w.shape[1] // 2), w.dtype),
-        in_specs=[outside(), outside()],
+        in_specs=[outside()],
         out_specs=inside(),
         scratch_shapes=[pltpu.SemaphoreType.DMA((GROUPS,))],
         compiler_params=pltpu.CompilerParams(vmem_limit_bytes=45 << 20),
         name="stage_other" if other else "stage_own",
-    )(w, after)
+    )(w)
 
 
 def project_kernel(start, n_parts, *refs):
@@ -313,16 +328,18 @@
     )
     kvs = [packed[0]] + [over_z(packed[2 * j], j) for j in range(1, GROUPS)]
     qs = [packed[1]] + [over_z(packed[2 * j + 1], j) for j in range(1, GROUPS)]
+    kept_kv, qs[0] = hold(kvs[0], qs[0])
     gathered = []
-    for kv in kvs:
+    for i, kv in enumerate(kvs):
         near = [kv] + [over_y(kv, j) for j in range(1, rows_y)]
-        for piece in near:
-            gathered += [piece, over(piece, 1)]
+        for j, piece in enumerate(near):
+            kept = kept_kv if i == j == 0 else piece
+            gathered += [kept, over(piece, 1)]
     late, kept = gather_and_attend(gathered, qs[2:], slots)
     early = attend(kept, qs[:2], len(gathered) * tokens)
     parts = [early[0], over_z(early[1], 1), over_z(late[0], 2), over_z(late[1], 3)]
-    w_other = stage(seq, True, out_weight, packed[1])
-    w_own = stage(seq, False, out_weight, packed[1])
+    w_other = stage(seq, True, out_weight)
+    w_own = stage(seq, False, out_weight)
     half = w_own.shape[1]
     cuts = [0, half // 4, half]
     arrived = []

time: 89 us -> 87.4 us (0.982); the launches traced: 87.6 us -> 87.1 us
  local copies, waits for them, and re-layouts: 4.58 us -> 1.83 us
  Pallas kernels: 16.8 us -> 19 us
    unnamed x10 -> x4, local copies, waits for them, and re-layouts: 4.58 us -> 1.83 us
    pallas_call x1, Pallas kernels: 0.41 us -> 2.63 us  [pack(): pl.pallas_call(functools.partial(pack_kernel, seq, width, slots), out_sha...]
  transfers between devices with their start and end apart: 23 -> 23, of which waited for: 8 -> 7; matrix products, arithmetic and copies ran while one was open for 0% -> 0% of each run, Pallas kernels for 13% -> 13%
where the time goes in v2:
time: 87.4 us; the launch traced here: 87.1 us
  waiting for transfers between devices  38 us (43%)
  starting transfers between devices  27.5 us (31%)
  Pallas kernels  19 us (22%)
  local copies, waits for them, and re-layouts  1.83 us (2%)
    ppermute x21, waiting for transfers between devices, over(): return lax.ppermute(x, 'seq', [(s, s ^ flip) for s in range(seq)])  30.1 us
    ppermute x21, starting transfers between devices, over(): return lax.ppermute(x, 'seq', [(s, s ^ flip) for s in range(seq)])  25.4 us
    ppermute x2, waiting for transfers between devices, dealt_plan(): arrived.append(lax.ppermute(theirs, 'head', [(0, 1), (1, 0)]))  7.94 us
    pallas_call x2, Pallas kernels, stage(): pl.pallas_call(functools.partial(stage_kernel, seq, other), out_shape=jax...  6.69 us
    pallas_call x1, Pallas kernels, gather_and_attend(): pl.pallas_call(functools.partial(gather_and_attend_kernel, len(kvs), len(...  3.18 us
    pallas_call x1, Pallas kernels, attend(): pl.pallas_call(functools.partial(attend_kernel, block, len(qs)), out_shap...  2.92 us
    pallas_call x3, Pallas kernels, project(): pl.pallas_call(functools.partial(project_kernel, start, len(parts)), out_...  2.65 us
    pallas_call x1, Pallas kernels, pack(): pl.pallas_call(functools.partial(pack_kernel, seq, width, slots), out_sha...  2.63 us
  transfers between devices with their start and end apart: 23, of which 7 were waited for; matrix products, arithmetic and copies ran while one was open for 0% of the time, Pallas kernels for 13%

profile of v2, /device:TPU:0, one launch (start us, length us, event | category | flops | bytes accessed | tf_op | source)
XLA Modules:
  0.0 87.1 jit_solution(9022224898626024446)
XLA Ops:
  0.7 2.6 %pack.1 = (bf16[304,384]{1,0:T(8,128)(2,1)}, bf16[128,384]{1,0:T(8,128)(2,1)}, bf16[304,384]{1,0:T(8,128)(2,1)}, bf16[128,384]{1,0:T(8,128)(2,1)}, bf16[304,384]...) custom-call(s32[1]{0:T(128)S(6)} %copy.8.len_ref, ...), custom_call_target="tpu_custom_call" | custom-call | tf_op jit(solution)/shard_map/pack/pallas_call | solution.py:118
  3.3 4.1 %collective-permute-start.15 = (bf16[128,384]{1,0:T(8,128)(2,1)}, bf16[128,384]{1,0:T(8,128)(2,1)S(1)}, u32[]{:S(2)}, u32[]{:S(2)}) collective-permute-start(bf16[128,384]{1,0:T(8,128)(2,1)} %get-tuple-element.28), channel_id=1, source_target_pairs={{0,16},{2,18},{4,20},{6,22},{8,24},{10,26},{12,28},{14,30},{16,0},... | collective-permute-start | bytes 294920 | tf_op jit(solution)/shard_map/ppermute | solution.py:318
  7.4 1.3 %collective-permute-start.16 = (bf16[128,384]{1,0:T(8,128)(2,1)}, bf16[128,384]{1,0:T(8,128)(2,1)S(1)}, u32[]{:S(2)}, u32[]{:S(2)}) collective-permute-start(bf16[128,384]{1,0:T(8,128)(2,1)} %get-tuple-element.29), channel_id=1, source_target_pairs={{0,24},{2,26},{4,28},{6,30},{8,16},{10,18},{12,20},{14,22},{16,8},... | collective-permute-start | bytes 294920 | tf_op jit(solution)/shard_map/ppermute | solution.py:318
  9.0 2.8 %collective-permute-start.7 = (bf16[304,384]{1,0:T(8,128)(2,1)}, bf16[304,384]{1,0:T(8,128)(2,1)S(1)}, u32[]{:S(2)}, u32[]{:S(2)}) collective-permute-start(bf16[304,384]{1,0:T(8,128)(2,1)} %get-tuple-element.26), channel_id=1, source_target_pairs={{0,16},{2,18},{4,20},{6,22},{8,24},{10,26},{12,28},{14,30},{16,0},... | collective-permute-start | bytes 700424 | tf_op jit(solution)/shard_map/ppermute | solution.py:318
  11.8 1.3 %collective-permute-start.11 = (bf16[304,384]{1,0:T(8,128)(2,1)}, bf16[304,384]{1,0:T(8,128)(2,1)S(1)}, u32[]{:S(2)}, u32[]{:S(2)}) collective-permute-start(bf16[304,384]{1,0:T(8,128)(2,1)} %get-tuple-element.27), channel_id=1, source_target_pairs={{0,24},{2,26},{4,28},{6,30},{8,16},{10,18},{12,20},{14,22},{16,8},... | collective-permute-start | bytes 700424 | tf_op jit(solution)/shard_map/ppermute | solution.py:318
  13.2 2.4 %collective-permute-done.15.refs_16_ = bf16[128,384]{1,0:T(8,128)(2,1)S(1)} collective-permute-done((bf16[128,384]{1,0:T(8,128)(2,1)}, bf16[128,384]{1,0:T(8,128)(2,1)S(1)}, u32[]{:S(2)}, u32[]{:S(2)}) %collective-permute-start.15) | collective-permute-done | bytes 98336 | tf_op jit(solution)/shard_map/ppermute | solution.py:318
  15.5 1.7 %collective-permute-start.1 = (bf16[304,384]{1,0:T(8,128)(2,1)}, bf16[304,384]{1,0:T(8,128)(2,1)S(1)}, u32[]{:S(2)}, u32[]{:S(2)}) collective-permute-start(bf16[304,384]{1,0:T(8,128)(2,1)} %get-tuple-element.22.refs_0_), channel_id=1, source_target_pairs={{0,4},{2,6},{4,0},{6,2},{8,12},{10,14},{12,8},{14,10},{16,20},{18,... | collective-permute-start | bytes 700424 | tf_op jit(solution)/shard_map/ppermute | solution.py:318
  17.2 3.7 %collective-permute-done.3.refs_4_ = bf16[304,384]{1,0:T(8,128)(2,1)S(1)} collective-permute-done((bf16[304,384]{1,0:T(8,128)(2,1)}, bf16[304,384]{1,0:T(8,128)(2,1)S(1)}, u32[]{:S(2)}, u32[]{:S(2)}) %collective-permute-start.3) | collective-permute-done | bytes 233504 | tf_op jit(solution)/shard_map/ppermute | solution.py:318
  20.9 1.5 %collective-permute-start.5 = (bf16[304,384]{1,0:T(8,128)(2,1)S(1)}, bf16[304,384]{1,0:T(8,128)(2,1)S(1)}, u32[]{:S(2)}, u32[]{:S(2)}) collective-permute-start(bf16[304,384]{1,0:T(8,128)(2,1)S(1)} %collective-permute-done.3.refs_4_), channel_id=1, source_target_pairs={{0,4},{2,6},{4,0},{6,2},{8,12},{10,14},{12,8},{14,10},{16,20},{18,... | collective-permute-start | bytes 700424 | tf_op jit(solution)/shard_map/ppermute | solution.py:318
  22.4 10.2 %collective-permute-done.7.refs_8_ = bf16[304,384]{1,0:T(8,128)(2,1)S(1)} collective-permute-done((bf16[304,384]{1,0:T(8,128)(2,1)}, bf16[304,384]{1,0:T(8,128)(2,1)S(1)}, u32[]{:S(2)}, u32[]{:S(2)}) %collective-permute-start.7) | collective-permute-done | bytes 233504 | tf_op jit(solution)/shard_map/ppermute | solution.py:318
  32.7 1.7 %collective-permute-start.9 = (bf16[304,384]{1,0:T(8,128)(2,1)S(1)}, bf16[304,384]{1,0:T(8,128)(2,1)S(1)}, u32[]{:S(2)}, u32[]{:S(2)}) collective-permute-start(bf16[304,384]{1,0:T(8,128)(2,1)S(1)} %collective-permute-done.7.refs_8_), channel_id=1, source_target_pairs={{0,4},{2,6},{4,0},{6,2},{8,12},{10,14},{12,8},{14,10},{16,20},{18,... | collective-permute-start | bytes 700424 | tf_op jit(solution)/shard_map/ppermute | solution.py:318
  35.0 0.5 collective-permute-start.2
  35.5 5.7 %collective-permute-done.9.refs_10_ = bf16[304,384]{1,0:T(8,128)(2,1)S(1)} collective-permute-done((bf16[304,384]{1,0:T(8,128)(2,1)S(1)}, bf16[304,384]{1,0:T(8,128)(2,1)S(1)}, u32[]{:S(2)}, u32[]{:S(2)}) %collective-permute-start.9) | collective-permute-done | bytes 233504 | tf_op jit(solution)/shard_map/ppermute | solution.py:318
  41.2 0.5 collective-permute-start.10
  41.7 4.0 %collective-permute-done.13.refs_14_ = bf16[304,384]{1,0:T(8,128)(2,1)S(1)} collective-permute-done((bf16[304,384]{1,0:T(8,128)(2,1)S(1)}, bf16[304,384]{1,0:T(8,128)(2,1)S(1)}, u32[]{:S(2)}, u32[]{:S(2)}) %collective-permute-start.13) | collective-permute-done | bytes 233504 | tf_op jit(solution)/shard_map/ppermute | solution.py:318
  45.8 4.5 %collective-permute-start.17 = (bf16[128,384]{1,0:T(8,128)(2,1)}, bf16[128,384]{1,0:T(8,128)(2,1)S(1)}, u32[]{:S(2)}, u32[]{:S(2)}) collective-permute-start(bf16[128,384]{1,0:T(8,128)(2,1)} %get-tuple-element.34), channel_id=1, source_target_pairs={{0,8},{2,10},{4,12},{6,14},{8,0},{10,2},{12,4},{14,6},{16,24},{18,... | collective-permute-start | bytes 294920 | tf_op jit(solution)/shard_map/ppermute | solution.py:318
  50.3 0.9 %copy-done = bf16[304,384]{1,0:T(8,128)(2,1)S(1)} copy-done((bf16[304,384]{1,0:T(8,128)(2,1)S(1)}, bf16[304,384]{1,0:T(8,128)(2,1)}, u32[]{:S(2)}) %copy-start) | copy-done | bytes 233496
  51.2 0.9 %copy-done.1 = bf16[128,384]{1,0:T(8,128)(2,1)S(1)} copy-done((bf16[128,384]{1,0:T(8,128)(2,1)S(1)}, bf16[128,384]{1,0:T(8,128)(2,1)}, u32[]{:S(2)}) %copy-start.1) | copy-done | bytes 98328
  52.2 3.2 %gather_and_attend.1 = (bf16[128,384]{1,0:T(8,128)(2,1)S(1)}, bf16[128,384]{1,0:T(8,128)(2,1)S(1)}, bf16[2304,384]{1,0:T(8,128)(2,1)S(1)}, bf16[2304,384]{1,0:T(8,128)(2,1)S(1)}, f32[16,256]{1,0:T(8,128)S(1)}) custom-call(bf16[304,384]{1,0:T(8,128)(2,1)S(1)} %get-tuple-element.24.refs_0_, bf16[304,384]{1,0:T(8,128)(2,1)S(1)} %collective-permute-done.refs_1_, ...), custom_call_target="tpu_custom_call" | custom-call | tf_op jit(solution)/shard_map/gather_and_attend/pallas_call | solution.py:214
  55.4 2.9 %attend.1 = (bf16[128,384]{1,0:T(8,128)(2,1)S(1)}, bf16[128,384]{1,0:T(8,128)(2,1)S(1)}) custom-call(bf16[2304,384]{1,0:T(8,128)(2,1)S(1)} %get-tuple-element.30.refs_0_, bf16[2304,384]{1,0:T(8,128)(2,1)S(1)} %get-tuple-element.31.refs_1_, f32[16,256]{1,0:T(8,128)S(1)} %get-tuple-element.32.refs_2_, bf16[128,384]{1,0:T(8,128)(2,1)S(1)} %get-tuple-element.33.refs_3_, ...), custom_call_target="tpu_custom_call" | custom-call | tf_op jit(solution)/shard_map/attend/pallas_call | solution.py:228
  58.7 3.5 %collective-permute-start.19 = (bf16[128,384]{1,0:T(8,128)(2,1)S(1)}, bf16[128,384]{1,0:T(8,128)(2,1)S(1)}, u32[]{:S(2)}, u32[]{:S(2)}) collective-permute-start(bf16[128,384]{1,0:T(8,128)(2,1)S(1)} %get-tuple-element.37), channel_id=1, source_target_pairs={{0,16},{2,18},{4,20},{6,22},{8,24},{10,26},{12,28},{14,30},{16,0},... | collective-permute-start | bytes 294920 | tf_op jit(solution)/shard_map/ppermute | solution.py:318
  62.2 0.5 collective-permute-start.20
  62.7 3.3 %stage_other.1.refs_4_ = bf16[1536,2560]{1,0:T(8,128)(2,1)S(1)} custom-call(bf16[1536,5120]{1,0:T(8,128)(2,1)} %w.3), custom_call_target="tpu_custom_call" | custom-call | tf_op jit(solution)/shard_map/stage_other/pallas_call | solution.py:258
  66.1 4.0 %collective-permute-done.19.refs_2_ = bf16[128,384]{1,0:T(8,128)(2,1)S(1)} collective-permute-done((bf16[128,384]{1,0:T(8,128)(2,1)S(1)}, bf16[128,384]{1,0:T(8,128)(2,1)S(1)}, u32[]{:S(2)}, u32[]{:S(2)}) %collective-permute-start.19) | collective-permute-done | bytes 98336 | tf_op jit(solution)/shard_map/ppermute | solution.py:318
  70.1 1.0 %project.5 = bf16[128,1920]{1,0:T(8,128)(2,1)S(1)} custom-call(bf16[128,384]{1,0:T(8,128)(2,1)S(1)} %get-tuple-element.35.refs_0_, bf16[128,384]{1,0:T(8,128)(2,1)S(1)} %collective-permute-done.18.refs_1_, bf16[128,384]{1,0:T(8,128)(2,1)S(1)} %collective-permute-done.19.refs_2_, bf16[128,384]{1,0:T(8,128)(2,1)S(1)} %collective-permute-done.20.refs_3_, ...), custom_call_target="tpu_custom_call" | custom-call | tf_op jit(solution)/shard_map/project/pallas_call | solution.py:279
  71.1 1.6 %collective-permute-start.22 = (bf16[128,1920]{1,0:T(8,128)(2,1)S(1)}, bf16[128,1920]{1,0:T(8,128)(2,1)S(1)}, u32[]{:S(2)}, u32[]{:S(2)}) collective-permute-start(bf16[128,1920]{1,0:T(8,128)(2,1)S(1)} %project.5), channel_id=1, source_target_pairs={{0,1},{1,0},{2,3},{3,2},{4,5},{5,4},{6,7},{7,6},{8,9},{9,8},{10,11... | collective-permute-start | bytes 1474568 | tf_op jit(solution)/shard_map/ppermute | solution.py:348
  72.6 0.5 project.4
  73.1 0.6 collective-permute-start.21
  73.7 3.3 %stage_own.1.refs_4_ = bf16[1536,2560]{1,0:T(8,128)(2,1)S(1)} custom-call(bf16[1536,5120]{1,0:T(8,128)(2,1)} %w.3), custom_call_target="tpu_custom_call" | custom-call | tf_op jit(solution)/shard_map/stage_own/pallas_call | solution.py:258
  77.1 1.2 %project.3.own = f32[128,2560]{1,0:T(8,128)S(1)} custom-call(bf16[128,384]{1,0:T(8,128)(2,1)S(1)} %get-tuple-element.35.refs_0_, bf16[128,384]{1,0:T(8,128)(2,1)S(1)} %collective-permute-done.18.refs_1_, bf16[128,384]{1,0:T(8,128)(2,1)S(1)} %collective-permute-done.19.refs_2_, bf16[128,384]{1,0:T(8,128)(2,1)S(1)} %collective-permute-done.20.refs_3_, ...), custom_call_target="tpu_custom_call" | custom-call | tf_op jit(solution)/shard_map/project/pallas_call | solution.py:279
  78.3 7.9 %collective-permute-done.21.refs_0_ = bf16[128,640]{1,0:T(8,128)(2,1)S(1)} collective-permute-done((bf16[128,640]{1,0:T(8,128)(2,1)S(1)}, bf16[128,640]{1,0:T(8,128)(2,1)S(1)}, u32[]{:S(2)}, u32[]{:S(2)}) %collective-permute-start.21) | collective-permute-done | bytes 163872 | tf_op jit(solution)/shard_map/ppermute | solution.py:348
  86.2 0.9 %add.1 = bf16[128,2560]{1,0:T(8,128)(2,1)} custom-call(f32[128,2560]{1,0:T(8,128)S(1)} %project.3.own, bf16[128,640]{1,0:T(8,128)(2,1)S(1)} %collective-permute-done.21.refs_0_, bf16[128,1920]{1,0:T(8,128)(2,1)S(1)} %collective-permute-done.22.refs_1_), custom_call_target="tpu_custom_call" | custom-call | tf_op jit(solution)/shard_map/add/pallas_call | solution.py:299
  (28 shorter events, 1.3 us)
Async XLA Ops:
  3.3 12.2 %collective-permute-start.15 = (bf16[128,384]{1,0:T(8,128)(2,1)}, bf16[128,384]{1,0:T(8,128)(2,1)S(1)}, u32[]{:S(2)}, u32[]{:S(2)}) collective-permute-start(bf16[128,384]{1,0:T(8,128)(2,1)} %get-tuple-element.28), channel_id=1, source_target_pairs={{0,16},{2,18},{4,20},{6,22},{8,24},{10,26},{12,28},{14,30},{16,0},... | collective-permute-start | bytes 294920 | tf_op jit(solution)/shard_map/ppermute | solution.py:318
  7.4 9.8 %collective-permute-start.16 = (bf16[128,384]{1,0:T(8,128)(2,1)}, bf16[128,384]{1,0:T(8,128)(2,1)S(1)}, u32[]{:S(2)}, u32[]{:S(2)}) collective-permute-start(bf16[128,384]{1,0:T(8,128)(2,1)} %get-tuple-element.29), channel_id=1, source_target_pairs={{0,24},{2,26},{4,28},{6,30},{8,16},{10,18},{12,20},{14,22},{16,8},... | collective-permute-start | bytes 294920 | tf_op jit(solution)/shard_map/ppermute | solution.py:318
  8.8 12.2 %collective-permute-start.3 = (bf16[304,384]{1,0:T(8,128)(2,1)}, bf16[304,384]{1,0:T(8,128)(2,1)S(1)}, u32[]{:S(2)}, u32[]{:S(2)}) collective-permute-start(bf16[304,384]{1,0:T(8,128)(2,1)} %get-tuple-element.25), channel_id=1, source_target_pairs={{0,8},{2,10},{4,12},{6,14},{8,0},{10,2},{12,4},{14,6},{16,24},{18,... | collective-permute-start | bytes 700424 | tf_op jit(solution)/shard_map/ppermute | solution.py:318
  9.0 23.6 %collective-permute-start.7 = (bf16[304,384]{1,0:T(8,128)(2,1)}, bf16[304,384]{1,0:T(8,128)(2,1)S(1)}, u32[]{:S(2)}, u32[]{:S(2)}) collective-permute-start(bf16[304,384]{1,0:T(8,128)(2,1)} %get-tuple-element.26), channel_id=1, source_target_pairs={{0,16},{2,18},{4,20},{6,22},{8,24},{10,26},{12,28},{14,30},{16,0},... | collective-permute-start | bytes 700424 | tf_op jit(solution)/shard_map/ppermute | solution.py:318
  11.8 20.8 %collective-permute-start.11 = (bf16[304,384]{1,0:T(8,128)(2,1)}, bf16[304,384]{1,0:T(8,128)(2,1)S(1)}, u32[]{:S(2)}, u32[]{:S(2)}) collective-permute-start(bf16[304,384]{1,0:T(8,128)(2,1)} %get-tuple-element.27), channel_id=1, source_target_pairs={{0,24},{2,26},{4,28},{6,30},{8,16},{10,18},{12,20},{14,22},{16,8},... | collective-permute-start | bytes 700424 | tf_op jit(solution)/shard_map/ppermute | solution.py:318
  15.5 18.8 %collective-permute-start.1 = (bf16[304,384]{1,0:T(8,128)(2,1)}, bf16[304,384]{1,0:T(8,128)(2,1)S(1)}, u32[]{:S(2)}, u32[]{:S(2)}) collective-permute-start(bf16[304,384]{1,0:T(8,128)(2,1)} %get-tuple-element.22.refs_0_), channel_id=1, source_target_pairs={{0,4},{2,6},{4,0},{6,2},{8,12},{10,14},{12,8},{14,10},{16,20},{18,... | collective-permute-start | bytes 700424 | tf_op jit(solution)/shard_map/ppermute | solution.py:318
  17.2 17.4 %collective-permute-start = (bf16[304,384]{1,0:T(8,128)(2,1)}, bf16[304,384]{1,0:T(8,128)(2,1)S(1)}, u32[]{:S(2)}, u32[]{:S(2)}) collective-permute-start(bf16[304,384]{1,0:T(8,128)(2,1)} %get-tuple-element.22.refs_0_), channel_id=1, source_target_pairs={{0,2},{2,0},{4,6},{6,4},{8,10},{10,8},{12,14},{14,12},{16,18},{18,... | collective-permute-start | bytes 700424 | tf_op jit(solution)/shard_map/ppermute | solution.py:318
  20.9 14.0 %collective-permute-start.5 = (bf16[304,384]{1,0:T(8,128)(2,1)S(1)}, bf16[304,384]{1,0:T(8,128)(2,1)S(1)}, u32[]{:S(2)}, u32[]{:S(2)}) collective-permute-start(bf16[304,384]{1,0:T(8,128)(2,1)S(1)} %collective-permute-done.3.refs_4_), channel_id=1, source_target_pairs={{0,4},{2,6},{4,0},{6,2},{8,12},{10,14},{12,8},{14,10},{16,20},{18,... | collective-permute-start | bytes 700424 | tf_op jit(solution)/shard_map/ppermute | solution.py:318
  32.6 2.3 %collective-permute-start.4 = (bf16[304,384]{1,0:T(8,128)(2,1)S(1)}, bf16[304,384]{1,0:T(8,128)(2,1)S(1)}, u32[]{:S(2)}, u32[]{:S(2)}) collective-permute-start(bf16[304,384]{1,0:T(8,128)(2,1)S(1)} %collective-permute-done.3.refs_4_), channel_id=1, source_target_pairs={{0,2},{2,0},{4,6},{6,4},{8,10},{10,8},{12,14},{14,12},{16,18},{18,... | collective-permute-start | bytes 700424 | tf_op jit(solution)/shard_map/ppermute | solution.py:318
  32.7 8.6 %collective-permute-start.9 = (bf16[304,384]{1,0:T(8,128)(2,1)S(1)}, bf16[304,384]{1,0:T(8,128)(2,1)S(1)}, u32[]{:S(2)}, u32[]{:S(2)}) collective-permute-start(bf16[304,384]{1,0:T(8,128)(2,1)S(1)} %collective-permute-done.7.refs_8_), channel_id=1, source_target_pairs={{0,4},{2,6},{4,0},{6,2},{8,12},{10,14},{12,8},{14,10},{16,20},{18,... | collective-permute-start | bytes 700424 | tf_op jit(solution)/shard_map/ppermute | solution.py:318
  34.4 6.9 %collective-permute-start.8 = (bf16[304,384]{1,0:T(8,128)(2,1)S(1)}, bf16[304,384]{1,0:T(8,128)(2,1)S(1)}, u32[]{:S(2)}, u32[]{:S(2)}) collective-permute-start(bf16[304,384]{1,0:T(8,128)(2,1)S(1)} %collective-permute-done.7.refs_8_), channel_id=1, source_target_pairs={{0,2},{2,0},{4,6},{6,4},{8,10},{10,8},{12,14},{14,12},{16,18},{18,... | collective-permute-start | bytes 700424 | tf_op jit(solution)/shard_map/ppermute | solution.py:318
  34.6 11.2 %collective-permute-start.13 = (bf16[304,384]{1,0:T(8,128)(2,1)S(1)}, bf16[304,384]{1,0:T(8,128)(2,1)S(1)}, u32[]{:S(2)}, u32[]{:S(2)}) collective-permute-start(bf16[304,384]{1,0:T(8,128)(2,1)S(1)} %collective-permute-done.11.refs_12_), channel_id=1, source_target_pairs={{0,4},{2,6},{4,0},{6,2},{8,12},{10,14},{12,8},{14,10},{16,20},{18,... | collective-permute-start | bytes 700424 | tf_op jit(solution)/shard_map/ppermute | solution.py:318
  35.0 10.8 %collective-permute-start.12 = (bf16[304,384]{1,0:T(8,128)(2,1)S(1)}, bf16[304,384]{1,0:T(8,128)(2,1)S(1)}, u32[]{:S(2)}, u32[]{:S(2)}) collective-permute-start(bf16[304,384]{1,0:T(8,128)(2,1)S(1)} %collective-permute-done.11.refs_12_), channel_id=1, source_target_pairs={{0,2},{2,0},{4,6},{6,4},{8,10},{10,8},{12,14},{14,12},{16,18},{18,... | collective-permute-start | bytes 700424 | tf_op jit(solution)/shard_map/ppermute | solution.py:318
  35.0 17.2 %collective-permute-start.2 = (bf16[304,384]{1,0:T(8,128)(2,1)S(1)}, bf16[304,384]{1,0:T(8,128)(2,1)S(1)}, u32[]{:S(2)}, u32[]{:S(2)}) collective-permute-start(bf16[304,384]{1,0:T(8,128)(2,1)S(1)} %collective-permute-done.1.refs_2_), channel_id=1, source_target_pairs={{0,2},{2,0},{4,6},{6,4},{8,10},{10,8},{12,14},{14,12},{16,18},{18,... | collective-permute-start | bytes 700424 | tf_op jit(solution)/shard_map/ppermute | solution.py:318
  41.2 10.9 %collective-permute-start.6 = (bf16[304,384]{1,0:T(8,128)(2,1)S(1)}, bf16[304,384]{1,0:T(8,128)(2,1)S(1)}, u32[]{:S(2)}, u32[]{:S(2)}) collective-permute-start(bf16[304,384]{1,0:T(8,128)(2,1)S(1)} %collective-permute-done.5.refs_6_), channel_id=1, source_target_pairs={{0,2},{2,0},{4,6},{6,4},{8,10},{10,8},{12,14},{14,12},{16,18},{18,... | collective-permute-start | bytes 700424 | tf_op jit(solution)/shard_map/ppermute | solution.py:318
  41.2 10.9 %collective-permute-start.10 = (bf16[304,384]{1,0:T(8,128)(2,1)S(1)}, bf16[304,384]{1,0:T(8,128)(2,1)S(1)}, u32[]{:S(2)}, u32[]{:S(2)}) collective-permute-start(bf16[304,384]{1,0:T(8,128)(2,1)S(1)} %collective-permute-done.9.refs_10_), channel_id=1, source_target_pairs={{0,2},{2,0},{4,6},{6,4},{8,10},{10,8},{12,14},{14,12},{16,18},{18,... | collective-permute-start | bytes 700424 | tf_op jit(solution)/shard_map/ppermute | solution.py:318
  45.8 6.4 %collective-permute-start.14 = (bf16[304,384]{1,0:T(8,128)(2,1)S(1)}, bf16[304,384]{1,0:T(8,128)(2,1)S(1)}, u32[]{:S(2)}, u32[]{:S(2)}) collective-permute-start(bf16[304,384]{1,0:T(8,128)(2,1)S(1)} %collective-permute-done.13.refs_14_), channel_id=1, source_target_pairs={{0,2},{2,0},{4,6},{6,4},{8,10},{10,8},{12,14},{14,12},{16,18},{18,... | collective-permute-start | bytes 700424 | tf_op jit(solution)/shard_map/ppermute | solution.py:318
  45.8 9.6 %collective-permute-start.17 = (bf16[128,384]{1,0:T(8,128)(2,1)}, bf16[128,384]{1,0:T(8,128)(2,1)S(1)}, u32[]{:S(2)}, u32[]{:S(2)}) collective-permute-start(bf16[128,384]{1,0:T(8,128)(2,1)} %get-tuple-element.34), channel_id=1, source_target_pairs={{0,8},{2,10},{4,12},{6,14},{8,0},{10,2},{12,4},{14,6},{16,24},{18,... | collective-permute-start | bytes 294920 | tf_op jit(solution)/shard_map/ppermute | solution.py:318
  50.3 0.9 %copy-start = (bf16[304,384]{1,0:T(8,128)(2,1)S(1)}, bf16[304,384]{1,0:T(8,128)(2,1)}, u32[]{:S(2)}) copy-start(bf16[304,384]{1,0:T(8,128)(2,1)} %get-tuple-element.22.refs_0_) | copy-start | bytes 700420
  51.2 0.9 %copy-start.1 = (bf16[128,384]{1,0:T(8,128)(2,1)S(1)}, bf16[128,384]{1,0:T(8,128)(2,1)}, u32[]{:S(2)}) copy-start(bf16[128,384]{1,0:T(8,128)(2,1)} %get-tuple-element.23.refs_1_) | copy-start | bytes 294916
  58.3 7.8 %collective-permute-start.18 = (bf16[128,384]{1,0:T(8,128)(2,1)S(1)}, bf16[128,384]{1,0:T(8,128)(2,1)S(1)}, u32[]{:S(2)}, u32[]{:S(2)}) collective-permute-start(bf16[128,384]{1,0:T(8,128)(2,1)S(1)} %get-tuple-element.36), channel_id=1, source_target_pairs={{0,8},{2,10},{4,12},{6,14},{8,0},{10,2},{12,4},{14,6},{16,24},{18,... | collective-permute-start | bytes 294920 | tf_op jit(solution)/shard_map/ppermute | solution.py:318
  58.7 11.4 %collective-permute-start.19 = (bf16[128,384]{1,0:T(8,128)(2,1)S(1)}, bf16[128,384]{1,0:T(8,128)(2,1)S(1)}, u32[]{:S(2)}, u32[]{:S(2)}) collective-permute-start(bf16[128,384]{1,0:T(8,128)(2,1)S(1)} %get-tuple-element.37), channel_id=1, source_target_pairs={{0,16},{2,18},{4,20},{6,22},{8,24},{10,26},{12,28},{14,30},{16,0},... | collective-permute-start | bytes 294920 | tf_op jit(solution)/shard_map/ppermute | solution.py:318
  62.2 7.9 %collective-permute-start.20 = (bf16[128,384]{1,0:T(8,128)(2,1)S(1)}, bf16[128,384]{1,0:T(8,128)(2,1)S(1)}, u32[]{:S(2)}, u32[]{:S(2)}) collective-permute-start(bf16[128,384]{1,0:T(8,128)(2,1)S(1)} %get-tuple-element.38), channel_id=1, source_target_pairs={{0,24},{2,26},{4,28},{6,30},{8,16},{10,18},{12,20},{14,22},{16,8},... | collective-permute-start | bytes 294920 | tf_op jit(solution)/shard_map/ppermute | solution.py:318
  71.1 15.1 %collective-permute-start.22 = (bf16[128,1920]{1,0:T(8,128)(2,1)S(1)}, bf16[128,1920]{1,0:T(8,128)(2,1)S(1)}, u32[]{:S(2)}, u32[]{:S(2)}) collective-permute-start(bf16[128,1920]{1,0:T(8,128)(2,1)S(1)} %project.5), channel_id=1, source_target_pairs={{0,1},{1,0},{2,3},{3,2},{4,5},{5,4},{6,7},{7,6},{8,9},{9,8},{10,11... | collective-permute-start | bytes 1474568 | tf_op jit(solution)/shard_map/ppermute | solution.py:348
  73.1 13.1 %collective-permute-start.21 = (bf16[128,640]{1,0:T(8,128)(2,1)S(1)}, bf16[128,640]{1,0:T(8,128)(2,1)S(1)}, u32[]{:S(2)}, u32[]{:S(2)}) collective-permute-start(bf16[128,640]{1,0:T(8,128)(2,1)S(1)} %project.4), channel_id=1, source_target_pairs={{0,1},{1,0},{2,3},{3,2},{4,5},{5,4},{6,7},{7,6},{8,9},{9,8},{10,11... | collective-permute-start | bytes 491528 | tf_op jit(solution)/shard_map/ppermute | solution.py:348

commit v3 on v2

v3 whole, which is shorter than its diff:
```python
import functools
import math

import jax
import jax.numpy as jnp
from jax import lax
from jax.experimental import pallas as pl
from jax.experimental.pallas import tpu as pltpu
from jax.sharding import PartitionSpec as P

DH = 128
NEG_BIG = -1e30
CORES = 2
GROUPS = 4


def fold_keys(running, query_heads, key_rows, value_rows, usable):
    maxima, totals, accumulated = running
    heads_here = query_heads.shape[1]
    head_width = query_heads.shape[2]
    key_heads = key_rows.reshape(key_rows.shape[0], heads_here, head_width)
    value_heads = value_rows.reshape(value_rows.shape[0], heads_here, head_width)
    scores = jnp.einsum(
        "qhd,khd->hqk", query_heads, key_heads, preferred_element_type=jnp.float32
    ) * (1.0 / math.sqrt(head_width))
    if usable is not None:
        scores = jnp.where(usable[None, None, :], scores, NEG_BIG)
    newest = jnp.maximum(maxima, jnp.max(scores, axis=2))
    carried = jnp.exp(maxima - newest)
    weights = jnp.exp(scores - newest[:, :, None])
    totals = totals * carried + jnp.sum(weights, axis=2)
    mixed = jnp.einsum(
        "hqk,khd->hqd",
        weights.astype(jnp.bfloat16),
        value_heads,
        preferred_element_type=jnp.float32,
    )
    accumulated = accumulated * carried[:, :, None] + mixed
    return (newest, totals, accumulated)


def cache_usable(lengths_piece, slots, row_count):
    slot_index = jnp.arange(row_count, dtype=jnp.int32) % slots
    slot_limit = jnp.repeat(lengths_piece.astype(jnp.int32), slots, total_repeat_length=row_count)
    return slot_index < slot_limit


def gathered_plan(
    queries, block_keys, block_values, cache_keys, cache_values, cache_lengths, out_weight
):
    tokens_here = queries.shape[0]
    heads_here = queries.shape[1] // DH
    query_heads = queries.reshape(tokens_here, heads_here, DH)
    slots = cache_keys.shape[0]
    running = (
        jnp.full((heads_here, tokens_here), NEG_BIG, jnp.float32),
        jnp.zeros((heads_here, tokens_here), jnp.float32),
        jnp.zeros((heads_here, tokens_here, DH), jnp.float32),
    )
    gather = functools.partial(lax.all_gather, axis_name="seq", axis=0, tiled=True)
    running = fold_keys(running, query_heads, gather(block_keys), gather(block_values), None)
    cached = gather(cache_keys)
    usable = cache_usable(gather(cache_lengths), slots, cached.shape[0])
    running = fold_keys(running, query_heads, cached, gather(cache_values), usable)
    _, totals, accumulated = running
    attended = (
        (accumulated / totals[:, :, None])
        .transpose(1, 0, 2)
        .reshape(tokens_here, heads_here * DH)
        .astype(jnp.bfloat16)
    )
    partial_terms = jnp.dot(attended, out_weight, preferred_element_type=jnp.float32)
    return lax.psum_scatter(
        partial_terms.astype(jnp.bfloat16), "head", scatter_dimension=1, tiled=True
    )


def inside():
    return pl.BlockSpec(memory_space=pltpu.VMEM)


def outside():
    return pl.BlockSpec(memory_space=pltpu.HBM)


def pack_kernel(seq, width, late, slots, len_ref, q, k, v, ck, cv, *refs):
    outs, sems = refs[:-1], refs[-1]
    own_kv, own_q = outs[:2]
    first, last = outs[2 : 2 * GROUPS], outs[2 * GROUPS :]
    me = lax.div(lax.axis_index("seq"), seq // GROUPS)
    copies = []

    def cut(kv, group, start, n):
        cols = pl.ds(pl.multiple_of(group * width + start, 128), n)
        row = 0
        for src in (k, v, ck, cv):
            rows = src.shape[0]
            copies.append((src.at[:, cols], kv.at[pl.ds(row, rows), :]))
            row += rows
        return cols

    for step in range(1, GROUPS):
        kv, qo = first[2 * step - 2], first[2 * step - 1]
        cols = cut(kv, lax.bitwise_xor(me, step), 0, width - late)
        copies.append((q.at[:, cols], qo))
    copies.append((q.at[:, cut(own_kv, me, 0, width)], own_q))
    for step in range(1, GROUPS):
        kv = last[step - 1]
        cols = cut(kv, lax.bitwise_xor(me, step), width - late, late)
        tokens = q.shape[0]
        copies.append((q.at[:, cols], kv.at[pl.ds(kv.shape[0] - tokens, tokens), :]))
    started = [
        pltpu.make_async_copy(src, dst, sems.at[i]) for i, (src, dst) in enumerate(copies)
    ]
    for copy in started:
        copy.start()
    row = 2 * k.shape[0] + 2 * slots
    for kv in (own_kv, *first[::2], *last):
        lane = lax.broadcasted_iota(jnp.int32, (16, kv.shape[1]), 1)
        kv[row : row + 16, :] = jnp.where(lax.rem(lane, slots) < len_ref[0], 1.0, 0.0).astype(
            jnp.bfloat16
        )
    for copy in started:
        copy.wait()


def pack(seq, width, late, lengths, q, k, v, ck, cv):
    tokens, slots = q.shape[0], ck.shape[0]
    rows = 2 * tokens + 2 * slots + 16

    def array(n, columns):
        return jax.ShapeDtypeStruct((n, columns), jnp.bfloat16)

    shapes = [array(rows, width), array(tokens, width)]
    shapes += [array(rows, width - late), array(tokens, width - late)] * (GROUPS - 1)
    shapes += [array(rows + tokens, late)] * (GROUPS - 1)
    made = pl.pallas_call(
        functools.partial(pack_kernel, seq, width, late, slots),
        out_shape=shapes,
        in_specs=[pl.BlockSpec(memory_space=pltpu.SMEM)] + [outside()] * 5,
        out_specs=[inside()] * len(shapes),
        scratch_shapes=[pltpu.SemaphoreType.DMA((5 * (2 * GROUPS - 1),))],
        compiler_params=pltpu.CompilerParams(vmem_limit_bytes=61 << 20),
        name="pack",
    )(lengths, q, k, v, ck, cv)
    return made[:2], made[2 : 2 * GROUPS], made[2 * GROUPS :]


def hold_kernel(*refs):
    for src, dst in zip(refs[: len(refs) // 2], refs[len(refs) // 2 :]):
        dst[...] = src[...]


def hold(*arrays):
    return pl.pallas_call(
        hold_kernel,
        out_shape=[jax.ShapeDtypeStruct(a.shape, a.dtype) for a in arrays],
        in_specs=[inside()] * len(arrays),
        out_specs=[inside()] * len(arrays),
        compiler_params=pltpu.CompilerParams(vmem_limit_bytes=4 << 20),
        name="hold",
    )(*arrays)


def join_kernel(axis, *refs):
    out, start = refs[-1], 0
    for piece in refs[:-1]:
        if axis == 0:
            n = out.shape[0] // (len(refs) - 1)
            out[start : start + n, :] = piece[0:n, :]
        else:
            n = piece.shape[1]
            out[:, start : start + n] = piece[...]
        start += n


def join(axis, pieces, n):
    shape = list(pieces[0].shape)
    shape[axis] = n * len(pieces)
    return pl.pallas_call(
        functools.partial(join_kernel, axis),
        out_shape=jax.ShapeDtypeStruct(tuple(shape), jnp.bfloat16),
        in_specs=[inside()] * len(pieces),
        out_specs=inside(),
        compiler_params=pltpu.CompilerParams(vmem_limit_bytes=4 << 20),
    )(*pieces)


def gather_kernel(places, tokens, slots, refs, keys, values, usable):
    block = len(places) * tokens
    n = keys.shape[1]
    for i, (which, row, col) in enumerate(places):
        kv, cols = refs[which], slice(col, col + n)
        at = slice(i * tokens, (i + 1) * tokens)
        keys[at, :] = kv[row : row + tokens, cols]
        values[at, :] = kv[row + tokens : row + 2 * tokens, cols]
        at = slice(block + i * slots, block + (i + 1) * slots)
        row += 2 * tokens
        keys[at, :] = kv[row : row + slots, cols]
        values[at, :] = kv[row + slots : row + 2 * slots, cols]
    lane = lax.broadcasted_iota(jnp.int32, (16, 128), 1)
    each = 128 // slots
    for start in range(0, len(places), each):
        flags = jnp.zeros((16, 128), jnp.float32)
        for j in range(each):
            which, row, _ = places[start + j]
            row += 2 * tokens + 2 * slots
            flag = refs[which][row : row + 16, 0:128].astype(jnp.float32)
            flags = jnp.where(lax.div(lane, slots) == j, flag, flags)
        usable[:, start * slots : start * slots + 128] = flags


def attend_rows(keys, values, usable, query, block, cols):
    scale = math.log2(math.e) / math.sqrt(DH)
    contract = (((1,), (1,)), ((), ()))
    main = lax.dot_general(
        query, keys[0:block, cols], contract, preferred_element_type=jnp.float32
    )
    tail = lax.dot_general(
        query, keys[block:, cols], contract, preferred_element_type=jnp.float32
    )
    tail = jnp.where(usable, tail, -3e38)
    top = jnp.maximum(jnp.max(main, axis=1, keepdims=True), jnp.max(tail, axis=1, keepdims=True))
    main = jnp.exp2((main - top) * scale)
    tail = jnp.exp2((tail - top) * scale)
    total = jnp.sum(main, axis=1, keepdims=True) + jnp.sum(tail, axis=1, keepdims=True)
    mixed = jnp.dot(
        main.astype(jnp.bfloat16), values[0:block, cols], preferred_element_type=jnp.float32
    ) + jnp.dot(tail.astype(jnp.bfloat16), values[block:, cols], preferred_element_type=jnp.float32)
    return (mixed / total).astype(jnp.bfloat16)


def attend_kernel(block, tokens, places, refs, keys, values, usable, outs, query):
    flags = usable[0:1, :] > 0.5
    n = keys.shape[1]
    for j, (which, row, col) in enumerate(places):
        query[j * tokens : (j + 1) * tokens, :] = refs[which][row : row + tokens, col : col + n]
    for h in range(n // DH):
        cols = slice(h * DH, (h + 1) * DH)
        step = min(2, len(places)) * tokens
        for start in range(0, len(places) * tokens, step):
            out = attend_rows(keys, values, flags, query[start : start + step, cols], block, cols)
            for row in range(0, step, tokens):
                outs[(start + row) // tokens][:, cols] = out[row : row + tokens]


def gather_and_attend_kernel(n_in, kv_places, q_places, tokens, slots, *refs):
    ins, outs = refs[:n_in], refs[n_in : n_in + len(q_places)]
    whole, query = refs[n_in + len(q_places) : -1], refs[-1]
    gather_kernel(kv_places, tokens, slots, ins, *whole)
    attend_kernel(len(kv_places) * tokens, tokens, q_places, ins, *whole, outs, query)


def gather_and_attend(arrays, kv_places, q_places, width, tokens, slots):
    rows = len(kv_places) * (tokens + slots)
    out = jax.ShapeDtypeStruct((tokens, width), jnp.bfloat16)
    rows_kept = jax.ShapeDtypeStruct((rows, width), jnp.bfloat16)
    flags = jax.ShapeDtypeStruct((16, len(kv_places) * slots), jnp.float32)
    made = pl.pallas_call(
        functools.partial(
            gather_and_attend_kernel, len(arrays), tuple(kv_places), tuple(q_places), tokens, slots
        ),
        out_shape=[out] * len(q_places) + [rows_kept, rows_kept, flags],
        in_specs=[inside()] * len(arrays),
        out_specs=[inside()] * (len(q_places) + 3),
        scratch_shapes=[pltpu.VMEM((len(q_places) * tokens, width), jnp.bfloat16)],
        compiler_params=pltpu.CompilerParams(vmem_limit_bytes=20 << 20),
        name="gather_and_attend",
    )(*arrays)
    return made[: len(q_places)], made[len(q_places) :]


def kept_attend_kernel(block, tokens, places, *refs):
    n = len(places)
    attend_kernel(block, tokens, places, refs[3:-1 - n], *refs[:3], refs[-1 - n : -1], refs[-1])


def attend(kept, qs, places, tokens):
    width, rows = kept[0].shape[1], kept[0].shape[0]
    block = rows - kept[2].shape[1]
    return pl.pallas_call(
        functools.partial(kept_attend_kernel, block, tokens, tuple(places)),
        out_shape=[jax.ShapeDtypeStruct((tokens, width), jnp.bfloat16)] * len(places),
        in_specs=[inside()] * (3 + len(qs)),
        out_specs=[inside()] * len(places),
        scratch_shapes=[pltpu.VMEM((len(places) * tokens, width), jnp.bfloat16)],
        compiler_params=pltpu.CompilerParams(vmem_limit_bytes=16 << 20),
        name="attend",
    )(*kept, *qs)


def stage_kernel(seq, width, start, each, count, by_core, other, w, out, sems):
    me = lax.div(lax.axis_index("seq"), seq // GROUPS)
    x = lax.axis_index("head")
    half = lax.bitwise_xor(x, 1) if other else x
    n = out.shape[1]
    cols = pl.ds(pl.multiple_of(half * n, n), n)
    base = count * lax.rem(lax.axis_index("seq"), CORES) if by_core else 0
    copies = []
    for j in range(count):
        group = lax.bitwise_xor(me, base + j)
        rows = pl.ds(pl.multiple_of(group * width + start, 128), each)
        copies.append(
            pltpu.make_async_copy(w.at[rows, cols], out.at[pl.ds(j * each, each), :], sems.at[j])
        )
    for copy in copies:
        copy.start()
    for copy in copies:
        copy.wait()


def stage(seq, width, start, each, count, by_core, other, w):
    return pl.pallas_call(
        functools.partial(stage_kernel, seq, width, start, each, count, by_core, other),
        out_shape=jax.ShapeDtypeStruct((count * each, w.shape[1] // 2), w.dtype),
        in_specs=[outside()],
        out_specs=inside(),
        scratch_shapes=[pltpu.SemaphoreType.DMA((count,))],
        compiler_params=pltpu.CompilerParams(vmem_limit_bytes=45 << 20),
    )(w)


def project_kernel(start, n_parts, *refs):
    parts, w, out = refs[:n_parts], refs[n_parts], refs[n_parts + 1]
    n = out.shape[1]
    attended = jnp.concatenate([p[...] for p in parts], axis=1)
    out[...] = jnp.dot(
        attended, w[:, start : start + n], preferred_element_type=jnp.float32
    ).astype(out.dtype)


def project(parts, w, start, n, dtype):
    return pl.pallas_call(
        functools.partial(project_kernel, start, len(parts)),
        out_shape=jax.ShapeDtypeStruct((parts[0].shape[0], n), dtype),
        in_specs=[inside()] * (len(parts) + 1),
        out_specs=inside(),
        compiler_params=pltpu.CompilerParams(vmem_limit_bytes=8 << 20),
        name="project",
    )(*parts, w)


def finish_kernel(own, attended, w_mine, w_near, *refs):
    out, start = refs[-1], 0
    n = w_mine.shape[0]
    core = lax.rem(lax.axis_index("seq"), CORES)
    mine = attended[:, pl.ds(pl.multiple_of(core * n, n), n)]
    near = attended[:, pl.ds(pl.multiple_of((1 - core) * n, n), n)]
    for piece in refs[:-1]:
        at = slice(start, start + piece.shape[1])
        total = own[:, at] + piece[...].astype(jnp.float32)
        total += jnp.dot(mine, w_mine[:, at], preferred_element_type=jnp.float32)
        total += jnp.dot(near, w_near[:, at], preferred_element_type=jnp.float32)
        out[:, at] = total.astype(out.dtype)
        start += piece.shape[1]


def finish(own, attended, w_mine, w_near, pieces):
    return pl.pallas_call(
        finish_kernel,
        out_shape=jax.ShapeDtypeStruct(own.shape, jnp.bfloat16),
        in_specs=[inside()] * (4 + len(pieces)),
        out_specs=inside(),
        compiler_params=pltpu.CompilerParams(vmem_limit_bytes=8 << 20),
        name="finish",
    )(own, attended, w_mine, w_near, *pieces)


def dealt_plan(
    seq, queries, block_keys, block_values, cache_keys, cache_values, cache_lengths, out_weight
):
    tokens, slots = queries.shape[0], cache_keys.shape[0]
    width = queries.shape[1] // GROUPS
    late = DH
    early = width - late
    stride = seq // GROUPS

    def over(x, flip):
        return lax.ppermute(x, "seq", [(s, s ^ flip) for s in range(seq)])

    def over_z(x, step):
        return over(x, step * stride)

    def over_x(x):
        return lax.ppermute(x, "head", [(0, 1), (1, 0)])

    (own_kv, own_q), first, last = pack(
        seq, width, late, cache_lengths, queries, block_keys, block_values, cache_keys, cache_values
    )
    steps = range(1, GROUPS)
    kvs = [over_z(first[2 * j - 2], j) for j in steps]
    qs = [over_z(first[2 * j - 1], j) for j in steps]
    ends = [over_z(last[j - 1], j) for j in steps]
    shipped = stage(seq, width, early, late, GROUPS // CORES, True, True, out_weight)
    w_mine = over_x(shipped)
    w_near = over(w_mine, 1)
    held_kv, held_q = hold(own_kv, own_q)
    gathered = []
    for i, kv in enumerate([own_kv] + kvs):
        far = over(kv, CORES)
        near, across = over(kv, 1), over(far, 1)
        gathered += [held_kv if i == 0 else kv, near, far, across]
    owns = gathered[:4]
    n = len(gathered)
    far_parts, kept = gather_and_attend(
        gathered + qs[1:],
        [(i, 0, 0) for i in range(n)],
        [(n, 0, 0), (n + 1, 0, 0)],
        early,
        tokens,
        slots,
    )
    near_parts = attend(kept, [held_q, qs[0]], [(0, 0, 0), (1, 0, 0)], tokens)
    parts = [near_parts[0], over_z(near_parts[1], 1)]
    parts += [over_z(far_parts[j], j + 2) for j in range(2)]
    rows = 2 * tokens + 2 * slots + 16
    joined = join(0, ends, rows)
    far = over(joined, CORES)
    near, across = over(joined, 1), over(far, 1)
    places = [(i, 0, early) for i in range(4)]
    places += [(4 + i, j * rows, 0) for i in range(4) for j in range(GROUPS - 1)]
    end_parts, _ = gather_and_attend(
        owns + [joined, near, far, across, held_q] + ends,
        places,
        [(8, 0, early)] + [(9 + j, rows, 0) for j in range(GROUPS - 1)],
        late,
        tokens,
        slots,
    )
    end_parts = [end_parts[0]] + [over_z(end_parts[j], j) for j in steps]
    half = out_weight.shape[1] // 2
    w_other = stage(seq, width, 0, early, GROUPS, False, True, out_weight)
    cuts = [0, half // 4, half]
    arrived = []
    for i in range(len(cuts) - 1):
        theirs = project(parts, w_other, cuts[i], cuts[i + 1] - cuts[i], jnp.bfloat16)
        arrived.append(over_x(theirs))
    ending = join(1, end_parts, late)
    attended = over_x(ending)
    w_own = stage(seq, width, 0, width, GROUPS, False, False, out_weight)
    both = [p for pair in zip(parts, end_parts) for p in pair]
    own = project(both, w_own, 0, half, jnp.float32)
    return finish(own, attended, w_mine, w_near, arrived)


def on_device(seq, head, *args):
    queries, cache_keys = args[0], args[3]
    heads_here = queries.shape[1] // DH
    slots = cache_keys.shape[0]
    rows_y = seq // (GROUPS * CORES)
    fits = (
        head == 2
        and seq % (GROUPS * CORES) == 0
        and rows_y == 2
        and heads_here % GROUPS == 0
        and heads_here > GROUPS
        and slots == 16
        and (seq * slots) % 128 == 0
        and queries.shape[0] % 16 == 0
        and args[6].shape[1] % 1024 == 0
    )
    return dealt_plan(seq, *args) if fits else gathered_plan(*args)


def solution(mesh):
    return jax.shard_map(
        functools.partial(on_device, mesh.shape["seq"], mesh.shape["head"]),
        mesh=mesh,
        in_specs=(
            P("seq", "head"),
            P("seq", "head"),
            P("seq", "head"),
            P("seq", "head"),
            P("seq", "head"),
            P("seq"),
            P("head", None),
        ),
        out_specs=P("seq", "head"),
        check_vma=False,
    )
```

time: 87.4 us -> 109 us (1.25)
  starting transfers between devices: 27.5 us -> 41.8 us
  waiting for transfers between devices: 38 us -> 43.5 us
  Pallas kernels: 19 us -> 20.9 us
    ppermute x21 -> x31, starting transfers between devices: 25.4 us -> 36.1 us  [over(): return lax.ppermute(x, 'seq', [(s, s ^ flip) for s in range(seq)])]
    ppermute x2 -> x4, waiting for transfers between devices: 7.94 us -> 16.7 us  [over_x(): return lax.ppermute(x, 'head', [(0, 1), (1, 0)])]
    ppermute x2 -> x4, starting transfers between devices: 2.15 us -> 5.7 us  [over_x(): return lax.ppermute(x, 'head', [(0, 1), (1, 0)])]
    ppermute x21 -> x31, waiting for transfers between devices: 30.1 us -> 26.8 us  [over(): return lax.ppermute(x, 'seq', [(s, s ^ flip) for s in range(seq)])]
    pallas_call x6 -> x10, Pallas kernels: 16.4 us -> 18.6 us  [the longest x3 7.18 us: stage(): pl.pallas_call(functools.partial(stage_kernel, seq, width, start, each, c...]
  transfers between devices with their start and end apart: 23 -> 35, of which waited for: 7 -> 13; matrix products, arithmetic and copies ran while one was open for 0% -> 0% of each run, Pallas kernels for 13% -> 17%
where the time goes in v3:
time: 109 us
  waiting for transfers between devices  43.5 us (40%)
  starting transfers between devices  41.8 us (38%)
  Pallas kernels  20.9 us (19%)
  local copies, waits for them, and re-layouts  1.83 us (2%)
    ppermute x31, starting transfers between devices, over(): return lax.ppermute(x, 'seq', [(s, s ^ flip) for s in range(seq)])  36.1 us
    ppermute x31, waiting for transfers between devices, over(): return lax.ppermute(x, 'seq', [(s, s ^ flip) for s in range(seq)])  26.8 us
    ppermute x4, waiting for transfers between devices, over_x(): return lax.ppermute(x, 'head', [(0, 1), (1, 0)])  16.7 us
    pallas_call x3, Pallas kernels, stage(): pl.pallas_call(functools.partial(stage_kernel, seq, width, start, each, c...  7.18 us
    ppermute x4, starting transfers between devices, over_x(): return lax.ppermute(x, 'head', [(0, 1), (1, 0)])  5.7 us
    pallas_call x2, Pallas kernels, gather_and_attend(): pl.pallas_call(functools.partial(gather_and_attend_kernel, len(arrays), t...  5.22 us
    pallas_call x1, Pallas kernels, pack(): pl.pallas_call(functools.partial(pack_kernel, seq, width, late, slots), o...  2.73 us
    pallas_call x3, Pallas kernels, project(): pl.pallas_call(functools.partial(project_kernel, start, len(parts)), out_...  2.27 us
  transfers between devices with their start and end apart: 35, of which 13 were waited for; matrix products, arithmetic and copies ran while one was open for 0% of the time, Pallas kernels for 17%

profile of v3, /device:TPU:0, one launch (start us, length us, event | category | flops | bytes accessed | tf_op | source)
XLA Modules:
  0.0 108.9 jit_solution(12287076257443817984)
XLA Ops:
  0.0 1.3 %shard_map.76 = bf16[256,2560]{1,0:T(8,128)(2,1)S(1)} custom-call(bf16[1536,5120]{1,0:T(8,128)(2,1)} %w.5), custom_call_target="tpu_custom_call" | custom-call | tf_op jit(solution)/shard_map/pallas_call | solution.py:313
  1.3 3.0 %collective-permute-start.31 = (bf16[256,2560]{1,0:T(8,128)(2,1)S(1)}, bf16[256,2560]{1,0:T(8,128)(2,1)S(1)}, u32[]{:S(2)}, u32[]{:S(2)}) collective-permute-start(bf16[256,2560]{1,0:T(8,128)(2,1)S(1)} %shard_map.76), channel_id=1, source_target_pairs={{0,1},{1,0},{2,3},{3,2},{4,5},{5,4},{6,7},{7,6},{8,9},{9,8},{10,11... | collective-permute-start | bytes 3932168 | tf_op jit(solution)/shard_map/ppermute | solution.py:385
  5.0 2.7 %pack.1 = (bf16[304,384]{1,0:T(8,128)(2,1)}, bf16[128,384]{1,0:T(8,128)(2,1)}, bf16[304,256]{1,0:T(8,128)(2,1)}, bf16[128,256]{1,0:T(8,128)(2,1)}, bf16[304,256]...) custom-call(s32[1]{0:T(128)S(6)} %copy.8.len_ref, ...), custom_call_target="tpu_custom_call" | custom-call | tf_op jit(solution)/shard_map/pack/pallas_call | solution.py:137
  7.7 2.7 %collective-permute-start.15 = (bf16[128,256]{1,0:T(8,128)(2,1)}, bf16[128,256]{1,0:T(8,128)(2,1)S(1)}, u32[]{:S(2)}, u32[]{:S(2)}) collective-permute-start(bf16[128,256]{1,0:T(8,128)(2,1)} %get-tuple-element.35), channel_id=1, source_target_pairs={{0,16},{2,18},{4,20},{6,22},{8,24},{10,26},{12,28},{14,30},{16,0},... | collective-permute-start | bytes 196616 | tf_op jit(solution)/shard_map/ppermute | solution.py:379
  10.4 1.6 %collective-permute-start.18 = (bf16[432,128]{1,0:T(8,128)(2,1)}, bf16[432,128]{1,0:T(8,128)(2,1)S(1)}, u32[]{:S(2)}, u32[]{:S(2)}) collective-permute-start(bf16[432,128]{1,0:T(8,128)(2,1)} %get-tuple-element.43), channel_id=1, source_target_pairs={{0,8},{2,10},{4,12},{6,14},{8,0},{10,2},{12,4},{14,6},{16,24},{18,... | collective-permute-start | bytes 331784 | tf_op jit(solution)/shard_map/ppermute | solution.py:379
  13.6 2.9 %collective-permute-start.19 = (bf16[432,128]{1,0:T(8,128)(2,1)}, bf16[432,128]{1,0:T(8,128)(2,1)S(1)}, u32[]{:S(2)}, u32[]{:S(2)}) collective-permute-start(bf16[432,128]{1,0:T(8,128)(2,1)} %get-tuple-element.44), channel_id=1, source_target_pairs={{0,16},{2,18},{4,20},{6,22},{8,24},{10,26},{12,28},{14,30},{16,0},... | collective-permute-start | bytes 331784 | tf_op jit(solution)/shard_map/ppermute | solution.py:379
  16.5 16.7 %collective-permute-done.31.w_mine = bf16[256,2560]{1,0:T(8,128)(2,1)S(1)} collective-permute-done((bf16[256,2560]{1,0:T(8,128)(2,1)S(1)}, bf16[256,2560]{1,0:T(8,128)(2,1)S(1)}, u32[]{:S(2)}, u32[]{:S(2)}) %collective-permute-start.31) | collective-permute-done | bytes 1310752 | tf_op jit(solution)/shard_map/ppermute | solution.py:385
  33.1 3.9 %collective-permute-start.20 = (bf16[432,128]{1,0:T(8,128)(2,1)}, bf16[432,128]{1,0:T(8,128)(2,1)S(1)}, u32[]{:S(2)}, u32[]{:S(2)}) collective-permute-start(bf16[432,128]{1,0:T(8,128)(2,1)} %get-tuple-element.45), channel_id=1, source_target_pairs={{0,24},{2,26},{4,28},{6,30},{8,16},{10,18},{12,20},{14,22},{16,8},... | collective-permute-start | bytes 331784 | tf_op jit(solution)/shard_map/ppermute | solution.py:379
  37.2 4.0 %collective-permute-done.20.refs_2_.refs_11_ = bf16[432,128]{1,0:T(8,128)(2,1)S(1)} collective-permute-done((bf16[432,128]{1,0:T(8,128)(2,1)}, bf16[432,128]{1,0:T(8,128)(2,1)S(1)}, u32[]{:S(2)}, u32[]{:S(2)}) %collective-permute-start.20) | collective-permute-done | bytes 110624 | tf_op jit(solution)/shard_map/ppermute | solution.py:379
  41.2 3.8 %collective-permute-start.11 = (bf16[304,256]{1,0:T(8,128)(2,1)}, bf16[304,256]{1,0:T(8,128)(2,1)S(1)}, u32[]{:S(2)}, u32[]{:S(2)}) collective-permute-start(bf16[304,256]{1,0:T(8,128)(2,1)} %get-tuple-element.34), channel_id=1, source_target_pairs={{0,24},{2,26},{4,28},{6,30},{8,16},{10,18},{12,20},{14,22},{16,8},... | collective-permute-start | bytes 466952 | tf_op jit(solution)/shard_map/ppermute | solution.py:379
  45.0 1.5 %collective-permute-start.1 = (bf16[304,384]{1,0:T(8,128)(2,1)}, bf16[304,384]{1,0:T(8,128)(2,1)S(1)}, u32[]{:S(2)}, u32[]{:S(2)}) collective-permute-start(bf16[304,384]{1,0:T(8,128)(2,1)} %get-tuple-element.29.refs_0_), channel_id=1, source_target_pairs={{0,4},{2,6},{4,0},{6,2},{8,12},{10,14},{12,8},{14,10},{16,20},{18,... | collective-permute-start | bytes 700424 | tf_op jit(solution)/shard_map/ppermute | solution.py:379
  46.5 6.4 %collective-permute-done.7.refs_8_ = bf16[304,256]{1,0:T(8,128)(2,1)S(1)} collective-permute-done((bf16[304,256]{1,0:T(8,128)(2,1)}, bf16[304,256]{1,0:T(8,128)(2,1)S(1)}, u32[]{:S(2)}, u32[]{:S(2)}) %collective-permute-start.7) | collective-permute-done | bytes 155680 | tf_op jit(solution)/shard_map/ppermute | solution.py:379
  52.9 1.5 %collective-permute-start.5 = (bf16[304,256]{1,0:T(8,128)(2,1)S(1)}, bf16[304,256]{1,0:T(8,128)(2,1)S(1)}, u32[]{:S(2)}, u32[]{:S(2)}) collective-permute-start(bf16[304,256]{1,0:T(8,128)(2,1)S(1)} %collective-permute-done.3.refs_4_), channel_id=1, source_target_pairs={{0,4},{2,6},{4,0},{6,2},{8,12},{10,14},{12,8},{14,10},{16,20},{18,... | collective-permute-start | bytes 466952 | tf_op jit(solution)/shard_map/ppermute | solution.py:379
  55.2 4.6 %collective-permute-done.5.refs_6_ = bf16[304,256]{1,0:T(8,128)(2,1)S(1)} collective-permute-done((bf16[304,256]{1,0:T(8,128)(2,1)S(1)}, bf16[304,256]{1,0:T(8,128)(2,1)S(1)}, u32[]{:S(2)}, u32[]{:S(2)}) %collective-permute-start.5) | collective-permute-done | bytes 155680 | tf_op jit(solution)/shard_map/ppermute | solution.py:379
  59.8 1.5 %collective-permute-start.13 = (bf16[304,256]{1,0:T(8,128)(2,1)S(1)}, bf16[304,256]{1,0:T(8,128)(2,1)S(1)}, u32[]{:S(2)}, u32[]{:S(2)}) collective-permute-start(bf16[304,256]{1,0:T(8,128)(2,1)S(1)} %collective-permute-done.11.refs_12_), channel_id=1, source_target_pairs={{0,4},{2,6},{4,0},{6,2},{8,12},{10,14},{12,8},{14,10},{16,20},{18,... | collective-permute-start | bytes 466952 | tf_op jit(solution)/shard_map/ppermute | solution.py:379
  61.3 1.3 %collective-permute-done.9.refs_10_ = bf16[304,256]{1,0:T(8,128)(2,1)S(1)} collective-permute-done((bf16[304,256]{1,0:T(8,128)(2,1)S(1)}, bf16[304,256]{1,0:T(8,128)(2,1)S(1)}, u32[]{:S(2)}, u32[]{:S(2)}) %collective-permute-start.9) | collective-permute-done | bytes 155680 | tf_op jit(solution)/shard_map/ppermute | solution.py:379
  63.2 3.1 %collective-permute-done.13.refs_14_ = bf16[304,256]{1,0:T(8,128)(2,1)S(1)} collective-permute-done((bf16[304,256]{1,0:T(8,128)(2,1)S(1)}, bf16[304,256]{1,0:T(8,128)(2,1)S(1)}, u32[]{:S(2)}, u32[]{:S(2)}) %collective-permute-start.13) | collective-permute-done | bytes 155680 | tf_op jit(solution)/shard_map/ppermute | solution.py:379
  66.3 1.6 %collective-permute-start.22 = (bf16[912,128]{1,0:T(8,128)(2,1)S(1)}, bf16[912,128]{1,0:T(8,128)(2,1)S(1)}, u32[]{:S(2)}, u32[]{:S(2)}) collective-permute-start(bf16[912,128]{1,0:T(8,128)(2,1)S(1)} %shard_map.73.refs_4_), channel_id=1, source_target_pairs={{0,4},{2,6},{4,0},{6,2},{8,12},{10,14},{12,8},{14,10},{16,20},{18,... | collective-permute-start | bytes 700424 | tf_op jit(solution)/shard_map/ppermute | solution.py:379
  67.9 3.4 %collective-permute-start.17 = (bf16[128,256]{1,0:T(8,128)(2,1)}, bf16[128,256]{1,0:T(8,128)(2,1)S(1)}, u32[]{:S(2)}, u32[]{:S(2)}) collective-permute-start(bf16[128,256]{1,0:T(8,128)(2,1)} %get-tuple-element.41), channel_id=1, source_target_pairs={{0,8},{2,10},{4,12},{6,14},{8,0},{10,2},{12,4},{14,6},{16,24},{18,... | collective-permute-start | bytes 196616 | tf_op jit(solution)/shard_map/ppermute | solution.py:379
  73.1 2.2 %gather_and_attend.2 = (bf16[128,256]{1,0:T(8,128)(2,1)S(1)}, bf16[128,256]{1,0:T(8,128)(2,1)S(1)}, bf16[2304,256]{1,0:T(8,128)(2,1)S(1)}, bf16[2304,256]{1,0:T(8,128)(2,1)S(1)}, f32[16,256]{1,0:T(8,128)S(1)}) custom-call(bf16[304,384]{1,0:T(8,128)(2,1)S(1)} %get-tuple-element.31.refs_0_, bf16[304,384]{1,0:T(8,128)(2,1)S(1)} %collective-permute-done.refs_1_, ...), custom_call_target="tpu_custom_call" | custom-call | tf_op jit(solution)/shard_map/gather_and_attend/pallas_call | solution.py:259
  75.3 2.1 %attend.1 = (bf16[128,256]{1,0:T(8,128)(2,1)S(1)}, bf16[128,256]{1,0:T(8,128)(2,1)S(1)}) custom-call(bf16[2304,256]{1,0:T(8,128)(2,1)S(1)} %get-tuple-element.37.refs_0_, bf16[2304,256]{1,0:T(8,128)(2,1)S(1)} %get-tuple-element.38.refs_1_, f32[16,256]{1,0:T(8,128)S(1)} %get-tuple-element.39.refs_2_, bf16[128,384]{1,0:T(8,128)(2,1)S(1)} %get-tuple-element.40.refs_3_.refs_8_, ...), custom_call_target="tpu_custom_call" | custom-call | tf_op jit(solution)/shard_map/attend/pallas_call | solution.py:281
  77.9 2.7 %collective-permute-start.26 = (bf16[128,256]{1,0:T(8,128)(2,1)S(1)}, bf16[128,256]{1,0:T(8,128)(2,1)S(1)}, u32[]{:S(2)}, u32[]{:S(2)}) collective-permute-start(bf16[128,256]{1,0:T(8,128)(2,1)S(1)} %get-tuple-element.49), channel_id=1, source_target_pairs={{0,16},{2,18},{4,20},{6,22},{8,24},{10,26},{12,28},{14,30},{16,0},... | collective-permute-start | bytes 196616 | tf_op jit(solution)/shard_map/ppermute | solution.py:379
  80.5 1.3 %collective-permute-start.28 = (bf16[128,256]{1,0:T(8,128)(2,1)S(1)}, bf16[128,256]{1,0:T(8,128)(2,1)S(1)}, u32[]{:S(2)}, u32[]{:S(2)}) collective-permute-start(bf16[128,256]{1,0:T(8,128)(2,1)S(1)} %get-tuple-element.51), channel_id=1, source_target_pairs={{0,24},{2,26},{4,28},{6,30},{8,16},{10,18},{12,20},{14,22},{16,8},... | collective-permute-start | bytes 196616 | tf_op jit(solution)/shard_map/ppermute | solution.py:379
  81.8 2.5 %shard_map.77.refs_4_ = bf16[1024,2560]{1,0:T(8,128)(2,1)S(1)} custom-call(bf16[1536,5120]{1,0:T(8,128)(2,1)} %w.5), custom_call_target="tpu_custom_call" | custom-call | tf_op jit(solution)/shard_map/pallas_call | solution.py:313
  84.4 1.3 %collective-permute-done.26.refs_4_.refs_2_ = bf16[128,256]{1,0:T(8,128)(2,1)S(1)} collective-permute-done((bf16[128,256]{1,0:T(8,128)(2,1)S(1)}, bf16[128,256]{1,0:T(8,128)(2,1)S(1)}, u32[]{:S(2)}, u32[]{:S(2)}) %collective-permute-start.26) | collective-permute-done | bytes 65568 | tf_op jit(solution)/shard_map/ppermute | solution.py:379
  87.4 1.6 %collective-permute-start.34 = (bf16[128,1920]{1,0:T(8,128)(2,1)S(1)}, bf16[128,1920]{1,0:T(8,128)(2,1)S(1)}, u32[]{:S(2)}, u32[]{:S(2)}) collective-permute-start(bf16[128,1920]{1,0:T(8,128)(2,1)S(1)} %project.5), channel_id=1, source_target_pairs={{0,1},{1,0},{2,3},{3,2},{4,5},{5,4},{6,7},{7,6},{8,9},{9,8},{10,11... | collective-permute-start | bytes 1474568 | tf_op jit(solution)/shard_map/ppermute | solution.py:385
  90.8 3.1 %gather_and_attend.3 = (bf16[128,128]{1,0:T(8,128)(2,1)S(1)}, bf16[128,128]{1,0:T(8,128)(2,1)S(1)}, bf16[128,128]{1,0:T(8,128)(2,1)S(1)}, bf16[128,128]{1,0:T(8,...) custom-call(bf16[304,384]{1,0:T(8,128)(2,1)S(1)} %get-tuple-element.31.refs_0_, ...), custom_call_target="tpu_custom_call" | custom-call | tf_op jit(solution)/shard_map/gather_and_attend/pallas_call | solution.py:259
  95.2 1.4 %collective-permute-start.27 = (bf16[128,128]{1,0:T(8,128)(2,1)S(1)}, bf16[128,128]{1,0:T(8,128)(2,1)S(1)}, u32[]{:S(2)}, u32[]{:S(2)}) collective-permute-start(bf16[128,128]{1,0:T(8,128)(2,1)S(1)} %get-tuple-element.50), channel_id=1, source_target_pairs={{0,16},{2,18},{4,20},{6,22},{8,24},{10,26},{12,28},{14,30},{16,0},... | collective-permute-start | bytes 98312 | tf_op jit(solution)/shard_map/ppermute | solution.py:379
  96.6 2.1 %collective-permute-start.29 = (bf16[128,128]{1,0:T(8,128)(2,1)S(1)}, bf16[128,128]{1,0:T(8,128)(2,1)S(1)}, u32[]{:S(2)}, u32[]{:S(2)}) collective-permute-start(bf16[128,128]{1,0:T(8,128)(2,1)S(1)} %get-tuple-element.52), channel_id=1, source_target_pairs={{0,24},{2,26},{4,28},{6,30},{8,16},{10,18},{12,20},{14,22},{16,8},... | collective-permute-start | bytes 98312 | tf_op jit(solution)/shard_map/ppermute | solution.py:379
  100.2 2.1 %collective-permute-done.29.refs_7_.refs_3_ = bf16[128,128]{1,0:T(8,128)(2,1)S(1)} collective-permute-done((bf16[128,128]{1,0:T(8,128)(2,1)S(1)}, bf16[128,128]{1,0:T(8,128)(2,1)S(1)}, u32[]{:S(2)}, u32[]{:S(2)}) %collective-permute-start.29) | collective-permute-done | bytes 32800 | tf_op jit(solution)/shard_map/ppermute | solution.py:379
  102.9 3.3 %shard_map.74.refs_8_ = bf16[1536,2560]{1,0:T(8,128)(2,1)S(1)} custom-call(bf16[1536,5120]{1,0:T(8,128)(2,1)} %w.5), custom_call_target="tpu_custom_call" | custom-call | tf_op jit(solution)/shard_map/pallas_call | solution.py:313
  107.5 1.4 %finish.1 = bf16[128,2560]{1,0:T(8,128)(2,1)} custom-call(f32[128,2560]{1,0:T(8,128)S(1)} %project.3.own, bf16[128,512]{1,0:T(8,128)(2,1)S(1)} %collective-permute-done.30.attended, bf16[256,2560]{1,0:T(8,128)(2,1)S(1)} %collective-permute-done.31.w_mine, bf16[256,2560]{1,0:T(8,128)(2,1)S(1)} %collective-permute-done.32.w_near, ...), custom_call_target="tpu_custom_call" | custom-call | tf_op jit(solution)/shard_map/finish/pallas_call | solution.py:359
  (56 shorter events, 13.7 us)
Async XLA Ops:
  1.3 31.8 %collective-permute-start.31 = (bf16[256,2560]{1,0:T(8,128)(2,1)S(1)}, bf16[256,2560]{1,0:T(8,128)(2,1)S(1)}, u32[]{:S(2)}, u32[]{:S(2)}) collective-permute-start(bf16[256,2560]{1,0:T(8,128)(2,1)S(1)} %shard_map.76), channel_id=1, source_target_pairs={{0,1},{1,0},{2,3},{3,2},{4,5},{5,4},{6,7},{7,6},{8,9},{9,8},{10,11... | collective-permute-start | bytes 3932168 | tf_op jit(solution)/shard_map/ppermute | solution.py:385
  7.7 5.8 %collective-permute-start.15 = (bf16[128,256]{1,0:T(8,128)(2,1)}, bf16[128,256]{1,0:T(8,128)(2,1)S(1)}, u32[]{:S(2)}, u32[]{:S(2)}) collective-permute-start(bf16[128,256]{1,0:T(8,128)(2,1)} %get-tuple-element.35), channel_id=1, source_target_pairs={{0,16},{2,18},{4,20},{6,22},{8,24},{10,26},{12,28},{14,30},{16,0},... | collective-permute-start | bytes 196616 | tf_op jit(solution)/shard_map/ppermute | solution.py:379
  10.4 26.6 %collective-permute-start.18 = (bf16[432,128]{1,0:T(8,128)(2,1)}, bf16[432,128]{1,0:T(8,128)(2,1)S(1)}, u32[]{:S(2)}, u32[]{:S(2)}) collective-permute-start(bf16[432,128]{1,0:T(8,128)(2,1)} %get-tuple-element.43), channel_id=1, source_target_pairs={{0,8},{2,10},{4,12},{6,14},{8,0},{10,2},{12,4},{14,6},{16,24},{18,... | collective-permute-start | bytes 331784 | tf_op jit(solution)/shard_map/ppermute | solution.py:379
  12.0 21.2 %collective-permute-start.16 = (bf16[128,256]{1,0:T(8,128)(2,1)}, bf16[128,256]{1,0:T(8,128)(2,1)S(1)}, u32[]{:S(2)}, u32[]{:S(2)}) collective-permute-start(bf16[128,256]{1,0:T(8,128)(2,1)} %get-tuple-element.36), channel_id=1, source_target_pairs={{0,24},{2,26},{4,28},{6,30},{8,16},{10,18},{12,20},{14,22},{16,8},... | collective-permute-start | bytes 196616 | tf_op jit(solution)/shard_map/ppermute | solution.py:379
  12.2 32.8 %collective-permute-start.3 = (bf16[304,256]{1,0:T(8,128)(2,1)}, bf16[304,256]{1,0:T(8,128)(2,1)S(1)}, u32[]{:S(2)}, u32[]{:S(2)}) collective-permute-start(bf16[304,256]{1,0:T(8,128)(2,1)} %get-tuple-element.32), channel_id=1, source_target_pairs={{0,8},{2,10},{4,12},{6,14},{8,0},{10,2},{12,4},{14,6},{16,24},{18,... | collective-permute-start | bytes 466952 | tf_op jit(solution)/shard_map/ppermute | solution.py:379
  13.6 23.6 %collective-permute-start.19 = (bf16[432,128]{1,0:T(8,128)(2,1)}, bf16[432,128]{1,0:T(8,128)(2,1)S(1)}, u32[]{:S(2)}, u32[]{:S(2)}) collective-permute-start(bf16[432,128]{1,0:T(8,128)(2,1)} %get-tuple-element.44), channel_id=1, source_target_pairs={{0,16},{2,18},{4,20},{6,22},{8,24},{10,26},{12,28},{14,30},{16,0},... | collective-permute-start | bytes 331784 | tf_op jit(solution)/shard_map/ppermute | solution.py:379
  33.1 74.4 %collective-permute-start.32 = (bf16[256,2560]{1,0:T(8,128)(2,1)S(1)}, bf16[256,2560]{1,0:T(8,128)(2,1)S(1)}, u32[]{:S(2)}, u32[]{:S(2)}) collective-permute-start(bf16[256,2560]{1,0:T(8,128)(2,1)S(1)} %collective-permute-done.31.w_mine), channel_id=1, source_target_pairs={{0,2},{2,0},{4,6},{6,4},{8,10},{10,8},{12,14},{14,12},{16,18},{18,... | collective-permute-start | bytes 3932168 | tf_op jit(solution)/shard_map/ppermute | solution.py:379
  33.1 8.1 %collective-permute-start.20 = (bf16[432,128]{1,0:T(8,128)(2,1)}, bf16[432,128]{1,0:T(8,128)(2,1)S(1)}, u32[]{:S(2)}, u32[]{:S(2)}) collective-permute-start(bf16[432,128]{1,0:T(8,128)(2,1)} %get-tuple-element.45), channel_id=1, source_target_pairs={{0,24},{2,26},{4,28},{6,30},{8,16},{10,18},{12,20},{14,22},{16,8},... | collective-permute-start | bytes 331784 | tf_op jit(solution)/shard_map/ppermute | solution.py:379
  37.0 17.5 %collective-permute-start = (bf16[304,384]{1,0:T(8,128)(2,1)}, bf16[304,384]{1,0:T(8,128)(2,1)S(1)}, u32[]{:S(2)}, u32[]{:S(2)}) collective-permute-start(bf16[304,384]{1,0:T(8,128)(2,1)} %get-tuple-element.29.refs_0_), channel_id=1, source_target_pairs={{0,2},{2,0},{4,6},{6,4},{8,10},{10,8},{12,14},{14,12},{16,18},{18,... | collective-permute-start | bytes 700424 | tf_op jit(solution)/shard_map/ppermute | solution.py:379
  37.2 15.7 %collective-permute-start.7 = (bf16[304,256]{1,0:T(8,128)(2,1)}, bf16[304,256]{1,0:T(8,128)(2,1)S(1)}, u32[]{:S(2)}, u32[]{:S(2)}) collective-permute-start(bf16[304,256]{1,0:T(8,128)(2,1)} %get-tuple-element.33), channel_id=1, source_target_pairs={{0,16},{2,18},{4,20},{6,22},{8,24},{10,26},{12,28},{14,30},{16,0},... | collective-permute-start | bytes 466952 | tf_op jit(solution)/shard_map/ppermute | solution.py:379
  41.2 11.7 %collective-permute-start.11 = (bf16[304,256]{1,0:T(8,128)(2,1)}, bf16[304,256]{1,0:T(8,128)(2,1)S(1)}, u32[]{:S(2)}, u32[]{:S(2)}) collective-permute-start(bf16[304,256]{1,0:T(8,128)(2,1)} %get-tuple-element.34), channel_id=1, source_target_pairs={{0,24},{2,26},{4,28},{6,30},{8,16},{10,18},{12,20},{14,22},{16,8},... | collective-permute-start | bytes 466952 | tf_op jit(solution)/shard_map/ppermute | solution.py:379
  45.0 9.6 %collective-permute-start.1 = (bf16[304,384]{1,0:T(8,128)(2,1)}, bf16[304,384]{1,0:T(8,128)(2,1)S(1)}, u32[]{:S(2)}, u32[]{:S(2)}) collective-permute-start(bf16[304,384]{1,0:T(8,128)(2,1)} %get-tuple-element.29.refs_0_), channel_id=1, source_target_pairs={{0,4},{2,6},{4,0},{6,2},{8,12},{10,14},{12,8},{14,10},{16,20},{18,... | collective-permute-start | bytes 700424 | tf_op jit(solution)/shard_map/ppermute | solution.py:379
  52.9 6.9 %collective-permute-start.5 = (bf16[304,256]{1,0:T(8,128)(2,1)S(1)}, bf16[304,256]{1,0:T(8,128)(2,1)S(1)}, u32[]{:S(2)}, u32[]{:S(2)}) collective-permute-start(bf16[304,256]{1,0:T(8,128)(2,1)S(1)} %collective-permute-done.3.refs_4_), channel_id=1, source_target_pairs={{0,4},{2,6},{4,0},{6,2},{8,12},{10,14},{12,8},{14,10},{16,20},{18,... | collective-permute-start | bytes 466952 | tf_op jit(solution)/shard_map/ppermute | solution.py:379
  54.4 5.4 %collective-permute-start.8 = (bf16[304,256]{1,0:T(8,128)(2,1)S(1)}, bf16[304,256]{1,0:T(8,128)(2,1)S(1)}, u32[]{:S(2)}, u32[]{:S(2)}) collective-permute-start(bf16[304,256]{1,0:T(8,128)(2,1)S(1)} %collective-permute-done.7.refs_8_), channel_id=1, source_target_pairs={{0,2},{2,0},{4,6},{6,4},{8,10},{10,8},{12,14},{14,12},{16,18},{18,... | collective-permute-start | bytes 466952 | tf_op jit(solution)/shard_map/ppermute | solution.py:379
  54.7 8.0 %collective-permute-start.9 = (bf16[304,256]{1,0:T(8,128)(2,1)S(1)}, bf16[304,256]{1,0:T(8,128)(2,1)S(1)}, u32[]{:S(2)}, u32[]{:S(2)}) collective-permute-start(bf16[304,256]{1,0:T(8,128)(2,1)S(1)} %collective-permute-done.7.refs_8_), channel_id=1, source_target_pairs={{0,4},{2,6},{4,0},{6,2},{8,12},{10,14},{12,8},{14,10},{16,20},{18,... | collective-permute-start | bytes 466952 | tf_op jit(solution)/shard_map/ppermute | solution.py:379
  55.2 11.1 %collective-permute-start.2 = (bf16[304,384]{1,0:T(8,128)(2,1)S(1)}, bf16[304,384]{1,0:T(8,128)(2,1)S(1)}, u32[]{:S(2)}, u32[]{:S(2)}) collective-permute-start(bf16[304,384]{1,0:T(8,128)(2,1)S(1)} %collective-permute-done.1.refs_2_), channel_id=1, source_target_pairs={{0,2},{2,0},{4,6},{6,4},{8,10},{10,8},{12,14},{14,12},{16,18},{18,... | collective-permute-start | bytes 700424 | tf_op jit(solution)/shard_map/ppermute | solution.py:379
  59.8 2.9 %collective-permute-start.12 = (bf16[304,256]{1,0:T(8,128)(2,1)S(1)}, bf16[304,256]{1,0:T(8,128)(2,1)S(1)}, u32[]{:S(2)}, u32[]{:S(2)}) collective-permute-start(bf16[304,256]{1,0:T(8,128)(2,1)S(1)} %collective-permute-done.11.refs_12_), channel_id=1, source_target_pairs={{0,2},{2,0},{4,6},{6,4},{8,10},{10,8},{12,14},{14,12},{16,18},{18,... | collective-permute-start | bytes 466952 | tf_op jit(solution)/shard_map/ppermute | solution.py:379
  59.8 6.4 %collective-permute-start.13 = (bf16[304,256]{1,0:T(8,128)(2,1)S(1)}, bf16[304,256]{1,0:T(8,128)(2,1)S(1)}, u32[]{:S(2)}, u32[]{:S(2)}) collective-permute-start(bf16[304,256]{1,0:T(8,128)(2,1)S(1)} %collective-permute-done.11.refs_12_), channel_id=1, source_target_pairs={{0,4},{2,6},{4,0},{6,2},{8,12},{10,14},{12,8},{14,10},{16,20},{18,... | collective-permute-start | bytes 466952 | tf_op jit(solution)/shard_map/ppermute | solution.py:379
  62.7 5.2 %collective-permute-start.6 = (bf16[304,256]{1,0:T(8,128)(2,1)S(1)}, bf16[304,256]{1,0:T(8,128)(2,1)S(1)}, u32[]{:S(2)}, u32[]{:S(2)}) collective-permute-start(bf16[304,256]{1,0:T(8,128)(2,1)S(1)} %collective-permute-done.5.refs_6_), channel_id=1, source_target_pairs={{0,2},{2,0},{4,6},{6,4},{8,10},{10,8},{12,14},{14,12},{16,18},{18,... | collective-permute-start | bytes 466952 | tf_op jit(solution)/shard_map/ppermute | solution.py:379
  62.7 10.4 %collective-permute-start.10 = (bf16[304,256]{1,0:T(8,128)(2,1)S(1)}, bf16[304,256]{1,0:T(8,128)(2,1)S(1)}, u32[]{:S(2)}, u32[]{:S(2)}) collective-permute-start(bf16[304,256]{1,0:T(8,128)(2,1)S(1)} %collective-permute-done.9.refs_10_), channel_id=1, source_target_pairs={{0,2},{2,0},{4,6},{6,4},{8,10},{10,8},{12,14},{14,12},{16,18},{18,... | collective-permute-start | bytes 466952 | tf_op jit(solution)/shard_map/ppermute | solution.py:379
  66.3 6.9 %collective-permute-start.14 = (bf16[304,256]{1,0:T(8,128)(2,1)S(1)}, bf16[304,256]{1,0:T(8,128)(2,1)S(1)}, u32[]{:S(2)}, u32[]{:S(2)}) collective-permute-start(bf16[304,256]{1,0:T(8,128)(2,1)S(1)} %collective-permute-done.13.refs_14_), channel_id=1, source_target_pairs={{0,2},{2,0},{4,6},{6,4},{8,10},{10,8},{12,14},{14,12},{16,18},{18,... | collective-permute-start | bytes 466952 | tf_op jit(solution)/shard_map/ppermute | solution.py:379
  66.3 22.7 %collective-permute-start.22 = (bf16[912,128]{1,0:T(8,128)(2,1)S(1)}, bf16[912,128]{1,0:T(8,128)(2,1)S(1)}, u32[]{:S(2)}, u32[]{:S(2)}) collective-permute-start(bf16[912,128]{1,0:T(8,128)(2,1)S(1)} %shard_map.73.refs_4_), channel_id=1, source_target_pairs={{0,4},{2,6},{4,0},{6,2},{8,12},{10,14},{12,8},{14,10},{16,20},{18,... | collective-permute-start | bytes 700424 | tf_op jit(solution)/shard_map/ppermute | solution.py:379
  67.9 7.4 %collective-permute-start.17 = (bf16[128,256]{1,0:T(8,128)(2,1)}, bf16[128,256]{1,0:T(8,128)(2,1)S(1)}, u32[]{:S(2)}, u32[]{:S(2)}) collective-permute-start(bf16[128,256]{1,0:T(8,128)(2,1)} %get-tuple-element.41), channel_id=1, source_target_pairs={{0,8},{2,10},{4,12},{6,14},{8,0},{10,2},{12,4},{14,6},{16,24},{18,... | collective-permute-start | bytes 196616 | tf_op jit(solution)/shard_map/ppermute | solution.py:379
  77.4 7.0 %collective-permute-start.24 = (bf16[128,256]{1,0:T(8,128)(2,1)S(1)}, bf16[128,256]{1,0:T(8,128)(2,1)S(1)}, u32[]{:S(2)}, u32[]{:S(2)}) collective-permute-start(bf16[128,256]{1,0:T(8,128)(2,1)S(1)} %get-tuple-element.47), channel_id=1, source_target_pairs={{0,8},{2,10},{4,12},{6,14},{8,0},{10,2},{12,4},{14,6},{16,24},{18,... | collective-permute-start | bytes 196616 | tf_op jit(solution)/shard_map/ppermute | solution.py:379
  77.9 7.8 %collective-permute-start.26 = (bf16[128,256]{1,0:T(8,128)(2,1)S(1)}, bf16[128,256]{1,0:T(8,128)(2,1)S(1)}, u32[]{:S(2)}, u32[]{:S(2)}) collective-permute-start(bf16[128,256]{1,0:T(8,128)(2,1)S(1)} %get-tuple-element.49), channel_id=1, source_target_pairs={{0,16},{2,18},{4,20},{6,22},{8,24},{10,26},{12,28},{14,30},{16,0},... | collective-permute-start | bytes 196616 | tf_op jit(solution)/shard_map/ppermute | solution.py:379
  80.5 6.2 %collective-permute-start.28 = (bf16[128,256]{1,0:T(8,128)(2,1)S(1)}, bf16[128,256]{1,0:T(8,128)(2,1)S(1)}, u32[]{:S(2)}, u32[]{:S(2)}) collective-permute-start(bf16[128,256]{1,0:T(8,128)(2,1)S(1)} %get-tuple-element.51), channel_id=1, source_target_pairs={{0,24},{2,26},{4,28},{6,30},{8,16},{10,18},{12,20},{14,22},{16,8},... | collective-permute-start | bytes 196616 | tf_op jit(solution)/shard_map/ppermute | solution.py:379
  87.4 20.1 %collective-permute-start.34 = (bf16[128,1920]{1,0:T(8,128)(2,1)S(1)}, bf16[128,1920]{1,0:T(8,128)(2,1)S(1)}, u32[]{:S(2)}, u32[]{:S(2)}) collective-permute-start(bf16[128,1920]{1,0:T(8,128)(2,1)S(1)} %project.5), channel_id=1, source_target_pairs={{0,1},{1,0},{2,3},{3,2},{4,5},{5,4},{6,7},{7,6},{8,9},{9,8},{10,11... | collective-permute-start | bytes 1474568 | tf_op jit(solution)/shard_map/ppermute | solution.py:385
  93.9 4.8 %collective-permute-start.25 = (bf16[128,128]{1,0:T(8,128)(2,1)S(1)}, bf16[128,128]{1,0:T(8,128)(2,1)S(1)}, u32[]{:S(2)}, u32[]{:S(2)}) collective-permute-start(bf16[128,128]{1,0:T(8,128)(2,1)S(1)} %get-tuple-element.48), channel_id=1, source_target_pairs={{0,8},{2,10},{4,12},{6,14},{8,0},{10,2},{12,4},{14,6},{16,24},{18,... | collective-permute-start | bytes 98312 | tf_op jit(solution)/shard_map/ppermute | solution.py:379
  95.2 5.0 %collective-permute-start.27 = (bf16[128,128]{1,0:T(8,128)(2,1)S(1)}, bf16[128,128]{1,0:T(8,128)(2,1)S(1)}, u32[]{:S(2)}, u32[]{:S(2)}) collective-permute-start(bf16[128,128]{1,0:T(8,128)(2,1)S(1)} %get-tuple-element.50), channel_id=1, source_target_pairs={{0,16},{2,18},{4,20},{6,22},{8,24},{10,26},{12,28},{14,30},{16,0},... | collective-permute-start | bytes 98312 | tf_op jit(solution)/shard_map/ppermute | solution.py:379
  96.6 5.7 %collective-permute-start.29 = (bf16[128,128]{1,0:T(8,128)(2,1)S(1)}, bf16[128,128]{1,0:T(8,128)(2,1)S(1)}, u32[]{:S(2)}, u32[]{:S(2)}) collective-permute-start(bf16[128,128]{1,0:T(8,128)(2,1)S(1)} %get-tuple-element.52), channel_id=1, source_target_pairs={{0,24},{2,26},{4,28},{6,30},{8,16},{10,18},{12,20},{14,22},{16,8},... | collective-permute-start | bytes 98312 | tf_op jit(solution)/shard_map/ppermute | solution.py:379
  98.7 8.8 %collective-permute-start.33 = (bf16[128,640]{1,0:T(8,128)(2,1)S(1)}, bf16[128,640]{1,0:T(8,128)(2,1)S(1)}, u32[]{:S(2)}, u32[]{:S(2)}) collective-permute-start(bf16[128,640]{1,0:T(8,128)(2,1)S(1)} %project.4), channel_id=1, source_target_pairs={{0,1},{1,0},{2,3},{3,2},{4,5},{5,4},{6,7},{7,6},{8,9},{9,8},{10,11... | collective-permute-start | bytes 491528 | tf_op jit(solution)/shard_map/ppermute | solution.py:385
  102.4 5.1 %collective-permute-start.30 = (bf16[128,512]{1,0:T(8,128)(2,1)S(1)}, bf16[128,512]{1,0:T(8,128)(2,1)S(1)}, u32[]{:S(2)}, u32[]{:S(2)}) collective-permute-start(bf16[128,512]{1,0:T(8,128)(2,1)S(1)} %shard_map.75), channel_id=1, source_target_pairs={{0,1},{1,0},{2,3},{3,2},{4,5},{5,4},{6,7},{7,6},{8,9},{9,8},{10,11... | collective-permute-start | bytes 393224 | tf_op jit(solution)/shard_map/ppermute | solution.py:385
  (5 other events, 7.4 us)

commit v4 on v3

--- a/solution.py
+++ b/solution.py
@@ -11,6 +11,7 @@
 DH = 128
 NEG_BIG = -1e30
 CORES = 2
+SOON = 2
 GROUPS = 4
 
 
@@ -320,18 +321,29 @@
     )(w)
 
 
-def project_kernel(start, n_parts, *refs):
+def project_kernel(seq, width, other, start, n_parts, *refs):
     parts, w, out = refs[:n_parts], refs[n_parts], refs[n_parts + 1]
+    me = lax.div(lax.axis_index("seq"), seq // GROUPS)
+    x = lax.axis_index("head")
+    half = lax.bitwise_xor(x, 1) if other else x
     n = out.shape[1]
-    attended = jnp.concatenate([p[...] for p in parts], axis=1)
-    out[...] = jnp.dot(
-        attended, w[:, start : start + n], preferred_element_type=jnp.float32
-    ).astype(out.dtype)
-
-
-def project(parts, w, start, n, dtype):
+    cols = pl.ds(pl.multiple_of(half * (w.shape[1] // 2) + start, 128), n)
+    total = None
+    for j in range(GROUPS):
+        group = parts[j * n_parts // GROUPS : (j + 1) * n_parts // GROUPS]
+        attended = group[0][...]
+        if len(group) > 1:
+            attended = jnp.concatenate([p[...] for p in group], axis=1)
+        first = pl.multiple_of(lax.bitwise_xor(me, j) * width, 128)
+        rows = w[pl.ds(first, attended.shape[1]), cols]
+        term = jnp.dot(attended, rows, preferred_element_type=jnp.float32)
+        total = term if total is None else total + term
+    out[...] = total.astype(out.dtype)
+
+
+def project(seq, width, other, parts, w, start, n, dtype):
     return pl.pallas_call(
-        functools.partial(project_kernel, start, len(parts)),
+        functools.partial(project_kernel, seq, width, other, start, len(parts)),
         out_shape=jax.ShapeDtypeStruct((parts[0].shape[0], n), dtype),
         in_specs=[inside()] * (len(parts) + 1),
         out_specs=inside(),
@@ -340,13 +352,19 @@
     )(*parts, w)
 
 
-def finish_kernel(own, attended, w_mine, w_near, *refs):
-    out, start = refs[-1], 0
+def finish_kernel(n_pieces, order, own, w_mine, w_near, *refs):
+    pieces, theirs, out, attended = refs[:n_pieces], refs[n_pieces:-2], refs[-2], refs[-1]
     n = w_mine.shape[0]
+    each = n * CORES // len(order)
+    for i, place in enumerate(order):
+        per = len(order) // n_pieces
+        at = slice(i % per * each, (i % per + 1) * each)
+        attended[:, place * each : (place + 1) * each] = pieces[i // per][:, at]
     core = lax.rem(lax.axis_index("seq"), CORES)
     mine = attended[:, pl.ds(pl.multiple_of(core * n, n), n)]
     near = attended[:, pl.ds(pl.multiple_of((1 - core) * n, n), n)]
-    for piece in refs[:-1]:
+    start = 0
+    for piece in theirs:
         at = slice(start, start + piece.shape[1])
         total = own[:, at] + piece[...].astype(jnp.float32)
         total += jnp.dot(mine, w_mine[:, at], preferred_element_type=jnp.float32)
@@ -355,15 +373,16 @@
         start += piece.shape[1]
 
 
-def finish(own, attended, w_mine, w_near, pieces):
+def finish(own, attended, order, w_mine, w_near, theirs):
     return pl.pallas_call(
-        finish_kernel,
+        functools.partial(finish_kernel, len(attended), tuple(order)),
         out_shape=jax.ShapeDtypeStruct(own.shape, jnp.bfloat16),
-        in_specs=[inside()] * (4 + len(pieces)),
+        in_specs=[inside()] * (3 + len(attended) + len(theirs)),
         out_specs=inside(),
+        scratch_shapes=[pltpu.VMEM((own.shape[0], w_mine.shape[0] * CORES), jnp.bfloat16)],
         compiler_params=pltpu.CompilerParams(vmem_limit_bytes=8 << 20),
         name="finish",
-    )(own, attended, w_mine, w_near, *pieces)
+    )(own, w_mine, w_near, *attended, *theirs)
 
 
 def dealt_plan(
@@ -414,33 +433,39 @@
     parts = [near_parts[0], over_z(near_parts[1], 1)]
     parts += [over_z(far_parts[j], j + 2) for j in range(2)]
     rows = 2 * tokens + 2 * slots + 16
-    joined = join(0, ends, rows)
-    far = over(joined, CORES)
-    near, across = over(joined, 1), over(far, 1)
-    places = [(i, 0, early) for i in range(4)]
-    places += [(4 + i, j * rows, 0) for i in range(4) for j in range(GROUPS - 1)]
+    joined = join(0, ends[1:], rows)
+    pieces = []
+    for piece in (ends[0], joined):
+        far = over(piece, CORES)
+        near, across = over(piece, 1), over(far, 1)
+        pieces += [piece, near, far, across]
+    places = [(i, 0, early) for i in range(4)] + [(4 + i, 0, 0) for i in range(4)]
+    places += [(8 + i, j * rows, 0) for i in range(4) for j in range(GROUPS - 2)]
     end_parts, _ = gather_and_attend(
-        owns + [joined, near, far, across, held_q] + ends,
+        owns + pieces + [held_q] + ends[1:],
         places,
-        [(8, 0, early)] + [(9 + j, rows, 0) for j in range(GROUPS - 1)],
+        [(12, 0, early), (4, rows, 0)] + [(13 + j, rows, 0) for j in range(GROUPS - 2)],
         late,
         tokens,
         slots,
     )
     end_parts = [end_parts[0]] + [over_z(end_parts[j], j) for j in steps]
     half = out_weight.shape[1] // 2
-    w_other = stage(seq, width, 0, early, GROUPS, False, True, out_weight)
     cuts = [0, half // 4, half]
     arrived = []
     for i in range(len(cuts) - 1):
-        theirs = project(parts, w_other, cuts[i], cuts[i + 1] - cuts[i], jnp.bfloat16)
+        theirs = project(
+            seq, width, True, parts, out_weight, cuts[i], cuts[i + 1] - cuts[i], jnp.bfloat16
+        )
         arrived.append(over_x(theirs))
-    ending = join(1, end_parts, late)
-    attended = over_x(ending)
-    w_own = stage(seq, width, 0, width, GROUPS, False, False, out_weight)
+    order = (0, SOON, *(j for j in steps if j != SOON))
+    attended = []
+    for i in range(2):
+        ending = join(1, [end_parts[j] for j in order[2 * i : 2 * i + 2]], late)
+        attended.append(over_x(ending))
     both = [p for pair in zip(parts, end_parts) for p in pair]
-    own = project(both, w_own, 0, half, jnp.float32)
-    return finish(own, attended, w_mine, w_near, arrived)
+    own = project(seq, width, False, both, out_weight, 0, half, jnp.float32)
+    return finish(own, attended, order, w_mine, w_near, arrived)
 
 
 def on_device(seq, head, *args):

time: 109 us -> 121 us (1.11)
  waiting for transfers between devices: 43.5 us -> 52.5 us
  local copies, waits for them, and re-layouts: 1.83 us -> 7.33 us
  Pallas kernels: 20.9 us -> 15.5 us
  starting transfers between devices: 41.8 us -> 44.2 us
    ppermute x4 -> x5, waiting for transfers between devices: 16.7 us -> 24.2 us  [over_x(): return lax.ppermute(x, 'head', [(0, 1), (1, 0)])]
    pallas_call x3 -> x1, Pallas kernels: 7.18 us -> 1.3 us  [stage(): pl.pallas_call(functools.partial(stage_kernel, seq, width, start, each, c...]
    unnamed x4 -> x20, local copies, waits for them, and re-layouts: 1.83 us -> 7.33 us
    ppermute x4 -> x5, starting transfers between devices: 5.7 us -> 8.2 us  [over_x(): return lax.ppermute(x, 'head', [(0, 1), (1, 0)])]
    ppermute x31 -> x34, waiting for transfers between devices: 26.8 us -> 28.3 us  [over(): return lax.ppermute(x, 'seq', [(s, s ^ flip) for s in range(seq)])]
    ppermute x31 -> x34, starting transfers between devices: 36.1 us -> 36 us  [over(): return lax.ppermute(x, 'seq', [(s, s ^ flip) for s in range(seq)])]
  transfers between devices with their start and end apart: 35 -> 39, of which waited for: 13 -> 13; matrix products, arithmetic and copies ran while one was open for 0% -> 0% of each run, Pallas kernels for 17% -> 11%
where the time goes in v4:
time: 121 us; the launch traced here: 120 us
  waiting for transfers between devices  52.5 us (43%)
  starting transfers between devices  44.2 us (37%)
  Pallas kernels  15.5 us (13%)
  local copies, waits for them, and re-layouts  7.33 us (6%)
    ppermute x34, starting transfers between devices, over(): return lax.ppermute(x, 'seq', [(s, s ^ flip) for s in range(seq)])  36 us
    ppermute x34, waiting for transfers between devices, over(): return lax.ppermute(x, 'seq', [(s, s ^ flip) for s in range(seq)])  28.3 us
    ppermute x5, waiting for transfers between devices, over_x(): return lax.ppermute(x, 'head', [(0, 1), (1, 0)])  24.2 us
    ppermute x5, starting transfers between devices, over_x(): return lax.ppermute(x, 'head', [(0, 1), (1, 0)])  8.2 us
    unnamed x20, local copies, waits for them, and re-layouts  7.33 us
    pallas_call x2, Pallas kernels, gather_and_attend(): pl.pallas_call(functools.partial(gather_and_attend_kernel, len(arrays), t...  5.24 us
    pallas_call x1, Pallas kernels, pack(): pl.pallas_call(functools.partial(pack_kernel, seq, width, late, slots), o...  2.73 us
    pallas_call x3, Pallas kernels, project(): pl.pallas_call(functools.partial(project_kernel, seq, width, other, start...  2.65 us
  transfers between devices with their start and end apart: 39, of which 13 were waited for; matrix products, arithmetic and copies ran while one was open for 0% of the time, Pallas kernels for 11%

profile of v4, /device:TPU:0, one launch (start us, length us, event | category | flops | bytes accessed | tf_op | source)
XLA Modules:
  0.0 120.3 jit_solution(10171706240463155593)
XLA Ops:
  1.3 3.0 %collective-permute-start.33 = (bf16[256,2560]{1,0:T(8,128)(2,1)S(1)}, bf16[256,2560]{1,0:T(8,128)(2,1)S(1)}, u32[]{:S(2)}, u32[]{:S(2)}) collective-permute-start(bf16[256,2560]{1,0:T(8,128)(2,1)S(1)} %shard_map.74), channel_id=1, source_target_pairs={{0,1},{1,0},{2,3},{3,2},{4,5},{5,4},{6,7},{7,6},{8,9},{9,8},{10,11... | collective-permute-start | bytes 3932168 | tf_op jit(solution)/shard_map/ppermute | solution.py:404
  5.0 2.7 %pack.1 = (bf16[304,384]{1,0:T(8,128)(2,1)}, bf16[128,384]{1,0:T(8,128)(2,1)}, bf16[304,256]{1,0:T(8,128)(2,1)}, bf16[128,256]{1,0:T(8,128)(2,1)}, bf16[304,256]...) custom-call(s32[1]{0:T(128)S(6)} %copy.8.len_ref, ...), custom_call_target="tpu_custom_call" | custom-call | tf_op jit(solution)/shard_map/pack/pallas_call | solution.py:138
  7.7 2.7 %collective-permute-start.7 = (bf16[304,256]{1,0:T(8,128)(2,1)}, bf16[304,256]{1,0:T(8,128)(2,1)S(1)}, u32[]{:S(2)}, u32[]{:S(2)}) collective-permute-start(bf16[304,256]{1,0:T(8,128)(2,1)} %get-tuple-element.33), channel_id=1, source_target_pairs={{0,16},{2,18},{4,20},{6,22},{8,24},{10,26},{12,28},{14,30},{16,0},... | collective-permute-start | bytes 466952 | tf_op jit(solution)/shard_map/ppermute | solution.py:398
  10.4 22.7 %collective-permute-done.33.w_mine = bf16[256,2560]{1,0:T(8,128)(2,1)S(1)} collective-permute-done((bf16[256,2560]{1,0:T(8,128)(2,1)S(1)}, bf16[256,2560]{1,0:T(8,128)(2,1)S(1)}, u32[]{:S(2)}, u32[]{:S(2)}) %collective-permute-start.33) | collective-permute-done | bytes 1310752 | tf_op jit(solution)/shard_map/ppermute | solution.py:404
  33.1 2.8 %collective-permute-start.15 = (bf16[128,256]{1,0:T(8,128)(2,1)}, bf16[128,256]{1,0:T(8,128)(2,1)S(1)}, u32[]{:S(2)}, u32[]{:S(2)}) collective-permute-start(bf16[128,256]{1,0:T(8,128)(2,1)} %get-tuple-element.35), channel_id=1, source_target_pairs={{0,16},{2,18},{4,20},{6,22},{8,24},{10,26},{12,28},{14,30},{16,0},... | collective-permute-start | bytes 196616 | tf_op jit(solution)/shard_map/ppermute | solution.py:398
  36.0 1.3 %collective-permute-start.16 = (bf16[128,256]{1,0:T(8,128)(2,1)}, bf16[128,256]{1,0:T(8,128)(2,1)S(1)}, u32[]{:S(2)}, u32[]{:S(2)}) collective-permute-start(bf16[128,256]{1,0:T(8,128)(2,1)} %get-tuple-element.36), channel_id=1, source_target_pairs={{0,24},{2,26},{4,28},{6,30},{8,16},{10,18},{12,20},{14,22},{16,8},... | collective-permute-start | bytes 196616 | tf_op jit(solution)/shard_map/ppermute | solution.py:398
  37.3 1.5 %collective-permute-start.1 = (bf16[304,384]{1,0:T(8,128)(2,1)}, bf16[304,384]{1,0:T(8,128)(2,1)S(1)}, u32[]{:S(2)}, u32[]{:S(2)}) collective-permute-start(bf16[304,384]{1,0:T(8,128)(2,1)} %get-tuple-element.29.refs_0_), channel_id=1, source_target_pairs={{0,4},{2,6},{4,0},{6,2},{8,12},{10,14},{12,8},{14,10},{16,20},{18,... | collective-permute-start | bytes 700424 | tf_op jit(solution)/shard_map/ppermute | solution.py:398
  38.8 1.7 %collective-permute-done.15.refs_16_ = bf16[128,256]{1,0:T(8,128)(2,1)S(1)} collective-permute-done((bf16[128,256]{1,0:T(8,128)(2,1)}, bf16[128,256]{1,0:T(8,128)(2,1)S(1)}, u32[]{:S(2)}, u32[]{:S(2)}) %collective-permute-start.15) | collective-permute-done | bytes 65568 | tf_op jit(solution)/shard_map/ppermute | solution.py:398
  40.6 4.7 %collective-permute-start.11 = (bf16[304,256]{1,0:T(8,128)(2,1)}, bf16[304,256]{1,0:T(8,128)(2,1)S(1)}, u32[]{:S(2)}, u32[]{:S(2)}) collective-permute-start(bf16[304,256]{1,0:T(8,128)(2,1)} %get-tuple-element.34), channel_id=1, source_target_pairs={{0,24},{2,26},{4,28},{6,30},{8,16},{10,18},{12,20},{14,22},{16,8},... | collective-permute-start | bytes 466952 | tf_op jit(solution)/shard_map/ppermute | solution.py:398
  45.4 5.0 %collective-permute-done.11.refs_12_ = bf16[304,256]{1,0:T(8,128)(2,1)S(1)} collective-permute-done((bf16[304,256]{1,0:T(8,128)(2,1)}, bf16[304,256]{1,0:T(8,128)(2,1)S(1)}, u32[]{:S(2)}, u32[]{:S(2)}) %collective-permute-start.11) | collective-permute-done | bytes 155680 | tf_op jit(solution)/shard_map/ppermute | solution.py:398
  50.5 1.5 %collective-permute-start.9 = (bf16[304,256]{1,0:T(8,128)(2,1)S(1)}, bf16[304,256]{1,0:T(8,128)(2,1)S(1)}, u32[]{:S(2)}, u32[]{:S(2)}) collective-permute-start(bf16[304,256]{1,0:T(8,128)(2,1)S(1)} %collective-permute-done.7.refs_8_), channel_id=1, source_target_pairs={{0,4},{2,6},{4,0},{6,2},{8,12},{10,14},{12,8},{14,10},{16,20},{18,... | collective-permute-start | bytes 466952 | tf_op jit(solution)/shard_map/ppermute | solution.py:398
  53.2 1.5 %collective-permute-start.13 = (bf16[304,256]{1,0:T(8,128)(2,1)S(1)}, bf16[304,256]{1,0:T(8,128)(2,1)S(1)}, u32[]{:S(2)}, u32[]{:S(2)}) collective-permute-start(bf16[304,256]{1,0:T(8,128)(2,1)S(1)} %collective-permute-done.11.refs_12_), channel_id=1, source_target_pairs={{0,4},{2,6},{4,0},{6,2},{8,12},{10,14},{12,8},{14,10},{16,20},{18,... | collective-permute-start | bytes 466952 | tf_op jit(solution)/shard_map/ppermute | solution.py:398
  55.7 4.3 %collective-permute-done.13.refs_14_ = bf16[304,256]{1,0:T(8,128)(2,1)S(1)} collective-permute-done((bf16[304,256]{1,0:T(8,128)(2,1)S(1)}, bf16[304,256]{1,0:T(8,128)(2,1)S(1)}, u32[]{:S(2)}, u32[]{:S(2)}) %collective-permute-start.13) | collective-permute-done | bytes 155680 | tf_op jit(solution)/shard_map/ppermute | solution.py:398
  60.1 2.4 %collective-permute-done.5.refs_6_ = bf16[304,256]{1,0:T(8,128)(2,1)S(1)} collective-permute-done((bf16[304,256]{1,0:T(8,128)(2,1)S(1)}, bf16[304,256]{1,0:T(8,128)(2,1)S(1)}, u32[]{:S(2)}, u32[]{:S(2)}) %collective-permute-start.5) | collective-permute-done | bytes 155680 | tf_op jit(solution)/shard_map/ppermute | solution.py:398
  64.0 1.6 %collective-permute-start.17 = (bf16[128,256]{1,0:T(8,128)(2,1)}, bf16[128,256]{1,0:T(8,128)(2,1)S(1)}, u32[]{:S(2)}, u32[]{:S(2)}) collective-permute-start(bf16[128,256]{1,0:T(8,128)(2,1)} %get-tuple-element.41), channel_id=1, source_target_pairs={{0,8},{2,10},{4,12},{6,14},{8,0},{10,2},{12,4},{14,6},{16,24},{18,... | collective-permute-start | bytes 196616 | tf_op jit(solution)/shard_map/ppermute | solution.py:398
  67.4 2.2 %gather_and_attend.2 = (bf16[128,256]{1,0:T(8,128)(2,1)S(1)}, bf16[128,256]{1,0:T(8,128)(2,1)S(1)}, bf16[2304,256]{1,0:T(8,128)(2,1)S(1)}, bf16[2304,256]{1,0:T(8,128)(2,1)S(1)}, f32[16,256]{1,0:T(8,128)S(1)}) custom-call(bf16[304,384]{1,0:T(8,128)(2,1)S(1)} %get-tuple-element.31.refs_0_, bf16[304,384]{1,0:T(8,128)(2,1)S(1)} %collective-permute-done.refs_1_, ...), custom_call_target="tpu_custom_call" | custom-call | tf_op jit(solution)/shard_map/gather_and_attend/pallas_call | solution.py:260
  69.6 2.1 %attend.1 = (bf16[128,256]{1,0:T(8,128)(2,1)S(1)}, bf16[128,256]{1,0:T(8,128)(2,1)S(1)}) custom-call(bf16[2304,256]{1,0:T(8,128)(2,1)S(1)} %get-tuple-element.37.refs_0_, bf16[2304,256]{1,0:T(8,128)(2,1)S(1)} %get-tuple-element.38.refs_1_, f32[16,256]{1,0:T(8,128)S(1)} %get-tuple-element.39.refs_2_, bf16[128,384]{1,0:T(8,128)(2,1)S(1)} %get-tuple-element.40.refs_3_.refs_12_, ...), custom_call_target="tpu_custom_call" | custom-call | tf_op jit(solution)/shard_map/attend/pallas_call | solution.py:282
  72.2 1.8 %collective-permute-start.29 = (bf16[128,256]{1,0:T(8,128)(2,1)S(1)}, bf16[128,256]{1,0:T(8,128)(2,1)S(1)}, u32[]{:S(2)}, u32[]{:S(2)}) collective-permute-start(bf16[128,256]{1,0:T(8,128)(2,1)S(1)} %get-tuple-element.49), channel_id=1, source_target_pairs={{0,16},{2,18},{4,20},{6,22},{8,24},{10,26},{12,28},{14,30},{16,0},... | collective-permute-start | bytes 196616 | tf_op jit(solution)/shard_map/ppermute | solution.py:398
  74.1 2.1 %collective-permute-start.31 = (bf16[128,256]{1,0:T(8,128)(2,1)S(1)}, bf16[128,256]{1,0:T(8,128)(2,1)S(1)}, u32[]{:S(2)}, u32[]{:S(2)}) collective-permute-start(bf16[128,256]{1,0:T(8,128)(2,1)S(1)} %get-tuple-element.51), channel_id=1, source_target_pairs={{0,24},{2,26},{4,28},{6,30},{8,16},{10,18},{12,20},{14,22},{16,8},... | collective-permute-start | bytes 196616 | tf_op jit(solution)/shard_map/ppermute | solution.py:398
  78.1 7.0 %collective-permute-done.29.refs_4_.refs_2_ = bf16[128,256]{1,0:T(8,128)(2,1)S(1)} collective-permute-done((bf16[128,256]{1,0:T(8,128)(2,1)S(1)}, bf16[128,256]{1,0:T(8,128)(2,1)S(1)}, u32[]{:S(2)}, u32[]{:S(2)}) %collective-permute-start.29) | collective-permute-done | bytes 65568 | tf_op jit(solution)/shard_map/ppermute | solution.py:398
  85.1 5.5 %copy-done = bf16[1536,5120]{1,0:T(8,128)(2,1)S(1)} copy-done((bf16[1536,5120]{1,0:T(8,128)(2,1)S(1)}, bf16[1536,5120]{1,0:T(8,128)(2,1)}, u32[]{:S(2)}) %copy-start) | copy-done | bytes 15728664
  91.3 1.6 %collective-permute-start.38 = (bf16[128,1920]{1,0:T(8,128)(2,1)S(1)}, bf16[128,1920]{1,0:T(8,128)(2,1)S(1)}, u32[]{:S(2)}, u32[]{:S(2)}) collective-permute-start(bf16[128,1920]{1,0:T(8,128)(2,1)S(1)} %project.5), channel_id=1, source_target_pairs={{0,1},{1,0},{2,3},{3,2},{4,5},{5,4},{6,7},{7,6},{8,9},{9,8},{10,11... | collective-permute-start | bytes 1474568 | tf_op jit(solution)/shard_map/ppermute | solution.py:404
  92.9 1.6 %collective-permute-start.25 = (bf16[608,128]{1,0:T(8,128)(2,1)S(1)}, bf16[608,128]{1,0:T(8,128)(2,1)S(1)}, u32[]{:S(2)}, u32[]{:S(2)}) collective-permute-start(bf16[608,128]{1,0:T(8,128)(2,1)S(1)} %shard_map.73.refs_8_), channel_id=1, source_target_pairs={{0,4},{2,6},{4,0},{6,2},{8,12},{10,14},{12,8},{14,10},{16,20},{18,... | collective-permute-start | bytes 466952 | tf_op jit(solution)/shard_map/ppermute | solution.py:398
  95.0 4.4 %collective-permute-done.20.refs_6_ = bf16[432,128]{1,0:T(8,128)(2,1)S(1)} collective-permute-done((bf16[432,128]{1,0:T(8,128)(2,1)S(1)}, bf16[432,128]{1,0:T(8,128)(2,1)S(1)}, u32[]{:S(2)}, u32[]{:S(2)}) %collective-permute-start.20) | collective-permute-done | bytes 110624 | tf_op jit(solution)/shard_map/ppermute | solution.py:398
  101.3 3.1 %gather_and_attend.3 = (bf16[128,128]{1,0:T(8,128)(2,1)S(1)}, bf16[128,128]{1,0:T(8,128)(2,1)S(1)}, bf16[128,128]{1,0:T(8,128)(2,1)S(1)}, bf16[128,128]{1,0:T(8,...) custom-call(bf16[304,384]{1,0:T(8,128)(2,1)S(1)} %get-tuple-element.31.refs_0_, ...), custom_call_target="tpu_custom_call" | custom-call | tf_op jit(solution)/shard_map/gather_and_attend/pallas_call | solution.py:260
  104.4 2.6 %collective-permute-start.28 = (bf16[128,128]{1,0:T(8,128)(2,1)S(1)}, bf16[128,128]{1,0:T(8,128)(2,1)S(1)}, u32[]{:S(2)}, u32[]{:S(2)}) collective-permute-start(bf16[128,128]{1,0:T(8,128)(2,1)S(1)} %get-tuple-element.48), channel_id=1, source_target_pairs={{0,8},{2,10},{4,12},{6,14},{8,0},{10,2},{12,4},{14,6},{16,24},{18,... | collective-permute-start | bytes 98312 | tf_op jit(solution)/shard_map/ppermute | solution.py:398
  107.0 2.4 %collective-permute-start.32 = (bf16[128,128]{1,0:T(8,128)(2,1)S(1)}, bf16[128,128]{1,0:T(8,128)(2,1)S(1)}, u32[]{:S(2)}, u32[]{:S(2)}) collective-permute-start(bf16[128,128]{1,0:T(8,128)(2,1)S(1)} %get-tuple-element.52), channel_id=1, source_target_pairs={{0,24},{2,26},{4,28},{6,30},{8,16},{10,18},{12,20},{14,22},{16,8},... | collective-permute-start | bytes 98312 | tf_op jit(solution)/shard_map/ppermute | solution.py:398
  109.4 2.5 %collective-permute-start.30 = (bf16[128,128]{1,0:T(8,128)(2,1)S(1)}, bf16[128,128]{1,0:T(8,128)(2,1)S(1)}, u32[]{:S(2)}, u32[]{:S(2)}) collective-permute-start(bf16[128,128]{1,0:T(8,128)(2,1)S(1)} %get-tuple-element.50), channel_id=1, source_target_pairs={{0,16},{2,18},{4,20},{6,22},{8,24},{10,26},{12,28},{14,30},{16,0},... | collective-permute-start | bytes 98312 | tf_op jit(solution)/shard_map/ppermute | solution.py:398
  112.8 1.8 %collective-permute-start.36 = (bf16[128,256]{1,0:T(8,128)(2,1)S(1)}, bf16[128,256]{1,0:T(8,128)(2,1)S(1)}, u32[]{:S(2)}, u32[]{:S(2)}) collective-permute-start(bf16[128,256]{1,0:T(8,128)(2,1)S(1)} %shard_map.76), channel_id=1, source_target_pairs={{0,1},{1,0},{2,3},{3,2},{4,5},{5,4},{6,7},{7,6},{8,9},{9,8},{10,11... | collective-permute-start | bytes 196616 | tf_op jit(solution)/shard_map/ppermute | solution.py:404
  115.9 1.5 %project.3.own = f32[128,2560]{1,0:T(8,128)S(1)} custom-call(bf16[128,256]{1,0:T(8,128)(2,1)S(1)} %get-tuple-element.42.refs_0_, bf16[128,128]{1,0:T(8,128)(2,1)S(1)} %get-tuple-element.46.refs_1_.refs_0_, bf16[128,256]{1,0:T(8,128)(2,1)S(1)} %collective-permute-done.27.refs_2_.refs_1_, bf16[128,128]{1,0:T(8,128)(2,1)S(1)} %collective-permute-done.28.refs_3_.refs_0_, ...), custom_call_target="tpu_custom_call" | custom-call | tf_op jit(solution)/shard_map/project/pallas_call | solution.py:345
  117.4 1.5 %collective-permute-done.35.refs_0_ = bf16[128,256]{1,0:T(8,128)(2,1)S(1)} collective-permute-done((bf16[128,256]{1,0:T(8,128)(2,1)S(1)}, bf16[128,256]{1,0:T(8,128)(2,1)S(1)}, u32[]{:S(2)}, u32[]{:S(2)}) %collective-permute-start.35) | collective-permute-done | bytes 65568 | tf_op jit(solution)/shard_map/ppermute | solution.py:404
  118.9 1.4 %finish.1 = bf16[128,2560]{1,0:T(8,128)(2,1)} custom-call(f32[128,2560]{1,0:T(8,128)S(1)} %project.3.own, bf16[256,2560]{1,0:T(8,128)(2,1)S(1)} %collective-permute-done.33.w_mine, bf16[256,2560]{1,0:T(8,128)(2,1)S(1)} %collective-permute-done.34.w_near, bf16[128,256]{1,0:T(8,128)(2,1)S(1)} %collective-permute-done.35.refs_0_, ...), custom_call_target="tpu_custom_call" | custom-call | tf_op jit(solution)/shard_map/finish/pallas_call | solution.py:377
  (80 shorter events, 14.8 us)
Async XLA Ops:
  1.3 31.8 %collective-permute-start.33 = (bf16[256,2560]{1,0:T(8,128)(2,1)S(1)}, bf16[256,2560]{1,0:T(8,128)(2,1)S(1)}, u32[]{:S(2)}, u32[]{:S(2)}) collective-permute-start(bf16[256,2560]{1,0:T(8,128)(2,1)S(1)} %shard_map.74), channel_id=1, source_target_pairs={{0,1},{1,0},{2,3},{3,2},{4,5},{5,4},{6,7},{7,6},{8,9},{9,8},{10,11... | collective-permute-start | bytes 3932168 | tf_op jit(solution)/shard_map/ppermute | solution.py:404
  7.7 37.6 %collective-permute-start.7 = (bf16[304,256]{1,0:T(8,128)(2,1)}, bf16[304,256]{1,0:T(8,128)(2,1)S(1)}, u32[]{:S(2)}, u32[]{:S(2)}) collective-permute-start(bf16[304,256]{1,0:T(8,128)(2,1)} %get-tuple-element.33), channel_id=1, source_target_pairs={{0,16},{2,18},{4,20},{6,22},{8,24},{10,26},{12,28},{14,30},{16,0},... | collective-permute-start | bytes 466952 | tf_op jit(solution)/shard_map/ppermute | solution.py:398
  33.1 85.8 %collective-permute-start.34 = (bf16[256,2560]{1,0:T(8,128)(2,1)S(1)}, bf16[256,2560]{1,0:T(8,128)(2,1)S(1)}, u32[]{:S(2)}, u32[]{:S(2)}) collective-permute-start(bf16[256,2560]{1,0:T(8,128)(2,1)S(1)} %collective-permute-done.33.w_mine), channel_id=1, source_target_pairs={{0,2},{2,0},{4,6},{6,4},{8,10},{10,8},{12,14},{14,12},{16,18},{18,... | collective-permute-start | bytes 3932168 | tf_op jit(solution)/shard_map/ppermute | solution.py:398
  33.1 7.5 %collective-permute-start.15 = (bf16[128,256]{1,0:T(8,128)(2,1)}, bf16[128,256]{1,0:T(8,128)(2,1)S(1)}, u32[]{:S(2)}, u32[]{:S(2)}) collective-permute-start(bf16[128,256]{1,0:T(8,128)(2,1)} %get-tuple-element.35), channel_id=1, source_target_pairs={{0,16},{2,18},{4,20},{6,22},{8,24},{10,26},{12,28},{14,30},{16,0},... | collective-permute-start | bytes 196616 | tf_op jit(solution)/shard_map/ppermute | solution.py:398
  36.0 9.4 %collective-permute-start.16 = (bf16[128,256]{1,0:T(8,128)(2,1)}, bf16[128,256]{1,0:T(8,128)(2,1)S(1)}, u32[]{:S(2)}, u32[]{:S(2)}) collective-permute-start(bf16[128,256]{1,0:T(8,128)(2,1)} %get-tuple-element.36), channel_id=1, source_target_pairs={{0,24},{2,26},{4,28},{6,30},{8,16},{10,18},{12,20},{14,22},{16,8},... | collective-permute-start | bytes 196616 | tf_op jit(solution)/shard_map/ppermute | solution.py:398
  37.3 17.4 %collective-permute-start.1 = (bf16[304,384]{1,0:T(8,128)(2,1)}, bf16[304,384]{1,0:T(8,128)(2,1)S(1)}, u32[]{:S(2)}, u32[]{:S(2)}) collective-permute-start(bf16[304,384]{1,0:T(8,128)(2,1)} %get-tuple-element.29.refs_0_), channel_id=1, source_target_pairs={{0,4},{2,6},{4,0},{6,2},{8,12},{10,14},{12,8},{14,10},{16,20},{18,... | collective-permute-start | bytes 700424 | tf_op jit(solution)/shard_map/ppermute | solution.py:398
  40.6 9.9 %collective-permute-start.11 = (bf16[304,256]{1,0:T(8,128)(2,1)}, bf16[304,256]{1,0:T(8,128)(2,1)S(1)}, u32[]{:S(2)}, u32[]{:S(2)}) collective-permute-start(bf16[304,256]{1,0:T(8,128)(2,1)} %get-tuple-element.34), channel_id=1, source_target_pairs={{0,24},{2,26},{4,28},{6,30},{8,16},{10,18},{12,20},{14,22},{16,8},... | collective-permute-start | bytes 466952 | tf_op jit(solution)/shard_map/ppermute | solution.py:398
  45.3 7.9 %collective-permute-start.3 = (bf16[304,256]{1,0:T(8,128)(2,1)}, bf16[304,256]{1,0:T(8,128)(2,1)S(1)}, u32[]{:S(2)}, u32[]{:S(2)}) collective-permute-start(bf16[304,256]{1,0:T(8,128)(2,1)} %get-tuple-element.32), channel_id=1, source_target_pairs={{0,8},{2,10},{4,12},{6,14},{8,0},{10,2},{12,4},{14,6},{16,24},{18,... | collective-permute-start | bytes 466952 | tf_op jit(solution)/shard_map/ppermute | solution.py:398
  45.3 9.9 %collective-permute-start = (bf16[304,384]{1,0:T(8,128)(2,1)}, bf16[304,384]{1,0:T(8,128)(2,1)S(1)}, u32[]{:S(2)}, u32[]{:S(2)}) collective-permute-start(bf16[304,384]{1,0:T(8,128)(2,1)} %get-tuple-element.29.refs_0_), channel_id=1, source_target_pairs={{0,2},{2,0},{4,6},{6,4},{8,10},{10,8},{12,14},{14,12},{16,18},{18,... | collective-permute-start | bytes 700424 | tf_op jit(solution)/shard_map/ppermute | solution.py:398
  50.5 5.2 %collective-permute-start.9 = (bf16[304,256]{1,0:T(8,128)(2,1)S(1)}, bf16[304,256]{1,0:T(8,128)(2,1)S(1)}, u32[]{:S(2)}, u32[]{:S(2)}) collective-permute-start(bf16[304,256]{1,0:T(8,128)(2,1)S(1)} %collective-permute-done.7.refs_8_), channel_id=1, source_target_pairs={{0,4},{2,6},{4,0},{6,2},{8,12},{10,14},{12,8},{14,10},{16,20},{18,... | collective-permute-start | bytes 466952 | tf_op jit(solution)/shard_map/ppermute | solution.py:398
  53.2 6.9 %collective-permute-start.13 = (bf16[304,256]{1,0:T(8,128)(2,1)S(1)}, bf16[304,256]{1,0:T(8,128)(2,1)S(1)}, u32[]{:S(2)}, u32[]{:S(2)}) collective-permute-start(bf16[304,256]{1,0:T(8,128)(2,1)S(1)} %collective-permute-done.11.refs_12_), channel_id=1, source_target_pairs={{0,4},{2,6},{4,0},{6,2},{8,12},{10,14},{12,8},{14,10},{16,20},{18,... | collective-permute-start | bytes 466952 | tf_op jit(solution)/shard_map/ppermute | solution.py:398
  54.7 7.8 %collective-permute-start.5 = (bf16[304,256]{1,0:T(8,128)(2,1)S(1)}, bf16[304,256]{1,0:T(8,128)(2,1)S(1)}, u32[]{:S(2)}, u32[]{:S(2)}) collective-permute-start(bf16[304,256]{1,0:T(8,128)(2,1)S(1)} %collective-permute-done.3.refs_4_), channel_id=1, source_target_pairs={{0,4},{2,6},{4,0},{6,2},{8,12},{10,14},{12,8},{14,10},{16,20},{18,... | collective-permute-start | bytes 466952 | tf_op jit(solution)/shard_map/ppermute | solution.py:398
  55.2 7.3 %collective-permute-start.12 = (bf16[304,256]{1,0:T(8,128)(2,1)S(1)}, bf16[304,256]{1,0:T(8,128)(2,1)S(1)}, u32[]{:S(2)}, u32[]{:S(2)}) collective-permute-start(bf16[304,256]{1,0:T(8,128)(2,1)S(1)} %collective-permute-done.11.refs_12_), channel_id=1, source_target_pairs={{0,2},{2,0},{4,6},{6,4},{8,10},{10,8},{12,14},{14,12},{16,18},{18,... | collective-permute-start | bytes 466952 | tf_op jit(solution)/shard_map/ppermute | solution.py:398
  55.7 7.3 %collective-permute-start.4 = (bf16[304,256]{1,0:T(8,128)(2,1)S(1)}, bf16[304,256]{1,0:T(8,128)(2,1)S(1)}, u32[]{:S(2)}, u32[]{:S(2)}) collective-permute-start(bf16[304,256]{1,0:T(8,128)(2,1)S(1)} %collective-permute-done.3.refs_4_), channel_id=1, source_target_pairs={{0,2},{2,0},{4,6},{6,4},{8,10},{10,8},{12,14},{14,12},{16,18},{18,... | collective-permute-start | bytes 466952 | tf_op jit(solution)/shard_map/ppermute | solution.py:398
  62.5 4.9 %collective-permute-start.10 = (bf16[304,256]{1,0:T(8,128)(2,1)S(1)}, bf16[304,256]{1,0:T(8,128)(2,1)S(1)}, u32[]{:S(2)}, u32[]{:S(2)}) collective-permute-start(bf16[304,256]{1,0:T(8,128)(2,1)S(1)} %collective-permute-done.9.refs_10_), channel_id=1, source_target_pairs={{0,2},{2,0},{4,6},{6,4},{8,10},{10,8},{12,14},{14,12},{16,18},{18,... | collective-permute-start | bytes 466952 | tf_op jit(solution)/shard_map/ppermute | solution.py:398
  63.0 4.4 %collective-permute-start.14 = (bf16[304,256]{1,0:T(8,128)(2,1)S(1)}, bf16[304,256]{1,0:T(8,128)(2,1)S(1)}, u32[]{:S(2)}, u32[]{:S(2)}) collective-permute-start(bf16[304,256]{1,0:T(8,128)(2,1)S(1)} %collective-permute-done.13.refs_14_), channel_id=1, source_target_pairs={{0,2},{2,0},{4,6},{6,4},{8,10},{10,8},{12,14},{14,12},{16,18},{18,... | collective-permute-start | bytes 466952 | tf_op jit(solution)/shard_map/ppermute | solution.py:398
  64.0 5.6 %collective-permute-start.17 = (bf16[128,256]{1,0:T(8,128)(2,1)}, bf16[128,256]{1,0:T(8,128)(2,1)S(1)}, u32[]{:S(2)}, u32[]{:S(2)}) collective-permute-start(bf16[128,256]{1,0:T(8,128)(2,1)} %get-tuple-element.41), channel_id=1, source_target_pairs={{0,8},{2,10},{4,12},{6,14},{8,0},{10,2},{12,4},{14,6},{16,24},{18,... | collective-permute-start | bytes 196616 | tf_op jit(solution)/shard_map/ppermute | solution.py:398
  71.7 5.5 %collective-permute-start.27 = (bf16[128,256]{1,0:T(8,128)(2,1)S(1)}, bf16[128,256]{1,0:T(8,128)(2,1)S(1)}, u32[]{:S(2)}, u32[]{:S(2)}) collective-permute-start(bf16[128,256]{1,0:T(8,128)(2,1)S(1)} %get-tuple-element.47), channel_id=1, source_target_pairs={{0,8},{2,10},{4,12},{6,14},{8,0},{10,2},{12,4},{14,6},{16,24},{18,... | collective-permute-start | bytes 196616 | tf_op jit(solution)/shard_map/ppermute | solution.py:398
  72.2 12.9 %collective-permute-start.29 = (bf16[128,256]{1,0:T(8,128)(2,1)S(1)}, bf16[128,256]{1,0:T(8,128)(2,1)S(1)}, u32[]{:S(2)}, u32[]{:S(2)}) collective-permute-start(bf16[128,256]{1,0:T(8,128)(2,1)S(1)} %get-tuple-element.49), channel_id=1, source_target_pairs={{0,16},{2,18},{4,20},{6,22},{8,24},{10,26},{12,28},{14,30},{16,0},... | collective-permute-start | bytes 196616 | tf_op jit(solution)/shard_map/ppermute | solution.py:398
  74.1 11.0 %collective-permute-start.31 = (bf16[128,256]{1,0:T(8,128)(2,1)S(1)}, bf16[128,256]{1,0:T(8,128)(2,1)S(1)}, u32[]{:S(2)}, u32[]{:S(2)}) collective-permute-start(bf16[128,256]{1,0:T(8,128)(2,1)S(1)} %get-tuple-element.51), channel_id=1, source_target_pairs={{0,24},{2,26},{4,28},{6,30},{8,16},{10,18},{12,20},{14,22},{16,8},... | collective-permute-start | bytes 196616 | tf_op jit(solution)/shard_map/ppermute | solution.py:398
  76.1 16.7 %collective-permute-start.22 = (bf16[432,128]{1,0:T(8,128)(2,1)S(1)}, bf16[432,128]{1,0:T(8,128)(2,1)S(1)}, u32[]{:S(2)}, u32[]{:S(2)}) collective-permute-start(bf16[432,128]{1,0:T(8,128)(2,1)S(1)} %copy-done.5), channel_id=1, source_target_pairs={{0,16},{2,18},{4,20},{6,22},{8,24},{10,26},{12,28},{14,30},{16,0},... | collective-permute-start | bytes 331784 | tf_op jit(solution)/shard_map/ppermute | solution.py:398
  77.2 15.7 %collective-permute-start.23 = (bf16[432,128]{1,0:T(8,128)(2,1)S(1)}, bf16[432,128]{1,0:T(8,128)(2,1)S(1)}, u32[]{:S(2)}, u32[]{:S(2)}) collective-permute-start(bf16[432,128]{1,0:T(8,128)(2,1)S(1)} %copy-done.4), channel_id=1, source_target_pairs={{0,24},{2,26},{4,28},{6,30},{8,16},{10,18},{12,20},{14,22},{16,8},... | collective-permute-start | bytes 331784 | tf_op jit(solution)/shard_map/ppermute | solution.py:398
  85.1 9.4 %collective-permute-start.18 = (bf16[432,128]{1,0:T(8,128)(2,1)S(1)}, bf16[432,128]{1,0:T(8,128)(2,1)S(1)}, u32[]{:S(2)}, u32[]{:S(2)}) collective-permute-start(bf16[432,128]{1,0:T(8,128)(2,1)S(1)} %copy-done.3), channel_id=1, source_target_pairs={{0,8},{2,10},{4,12},{6,14},{8,0},{10,2},{12,4},{14,6},{16,24},{18,... | collective-permute-start | bytes 331784 | tf_op jit(solution)/shard_map/ppermute | solution.py:398
  91.3 27.6 %collective-permute-start.38 = (bf16[128,1920]{1,0:T(8,128)(2,1)S(1)}, bf16[128,1920]{1,0:T(8,128)(2,1)S(1)}, u32[]{:S(2)}, u32[]{:S(2)}) collective-permute-start(bf16[128,1920]{1,0:T(8,128)(2,1)S(1)} %project.5), channel_id=1, source_target_pairs={{0,1},{1,0},{2,3},{3,2},{4,5},{5,4},{6,7},{7,6},{8,9},{9,8},{10,11... | collective-permute-start | bytes 1474568 | tf_op jit(solution)/shard_map/ppermute | solution.py:404
  92.9 6.5 %collective-permute-start.25 = (bf16[608,128]{1,0:T(8,128)(2,1)S(1)}, bf16[608,128]{1,0:T(8,128)(2,1)S(1)}, u32[]{:S(2)}, u32[]{:S(2)}) collective-permute-start(bf16[608,128]{1,0:T(8,128)(2,1)S(1)} %shard_map.73.refs_8_), channel_id=1, source_target_pairs={{0,4},{2,6},{4,0},{6,2},{8,12},{10,14},{12,8},{14,10},{16,20},{18,... | collective-permute-start | bytes 466952 | tf_op jit(solution)/shard_map/ppermute | solution.py:398
  94.5 4.9 %collective-permute-start.20 = (bf16[432,128]{1,0:T(8,128)(2,1)S(1)}, bf16[432,128]{1,0:T(8,128)(2,1)S(1)}, u32[]{:S(2)}, u32[]{:S(2)}) collective-permute-start(bf16[432,128]{1,0:T(8,128)(2,1)S(1)} %collective-permute-done.18.refs_4_), channel_id=1, source_target_pairs={{0,4},{2,6},{4,0},{6,2},{8,12},{10,14},{12,8},{14,10},{16,20},{18,... | collective-permute-start | bytes 331784 | tf_op jit(solution)/shard_map/ppermute | solution.py:398
  95.0 4.9 %collective-permute-start.19 = (bf16[432,128]{1,0:T(8,128)(2,1)S(1)}, bf16[432,128]{1,0:T(8,128)(2,1)S(1)}, u32[]{:S(2)}, u32[]{:S(2)}) collective-permute-start(bf16[432,128]{1,0:T(8,128)(2,1)S(1)} %collective-permute-done.18.refs_4_), channel_id=1, source_target_pairs={{0,2},{2,0},{4,6},{6,4},{8,10},{10,8},{12,14},{14,12},{16,18},{18,... | collective-permute-start | bytes 331784 | tf_op jit(solution)/shard_map/ppermute | solution.py:398
  100.8 18.1 %collective-permute-start.37 = (bf16[128,640]{1,0:T(8,128)(2,1)S(1)}, bf16[128,640]{1,0:T(8,128)(2,1)S(1)}, u32[]{:S(2)}, u32[]{:S(2)}) collective-permute-start(bf16[128,640]{1,0:T(8,128)(2,1)S(1)} %project.4), channel_id=1, source_target_pairs={{0,1},{1,0},{2,3},{3,2},{4,5},{5,4},{6,7},{7,6},{8,9},{9,8},{10,11... | collective-permute-start | bytes 491528 | tf_op jit(solution)/shard_map/ppermute | solution.py:404
  104.4 5.0 %collective-permute-start.28 = (bf16[128,128]{1,0:T(8,128)(2,1)S(1)}, bf16[128,128]{1,0:T(8,128)(2,1)S(1)}, u32[]{:S(2)}, u32[]{:S(2)}) collective-permute-start(bf16[128,128]{1,0:T(8,128)(2,1)S(1)} %get-tuple-element.48), channel_id=1, source_target_pairs={{0,8},{2,10},{4,12},{6,14},{8,0},{10,2},{12,4},{14,6},{16,24},{18,... | collective-permute-start | bytes 98312 | tf_op jit(solution)/shard_map/ppermute | solution.py:398
  107.0 5.7 %collective-permute-start.32 = (bf16[128,128]{1,0:T(8,128)(2,1)S(1)}, bf16[128,128]{1,0:T(8,128)(2,1)S(1)}, u32[]{:S(2)}, u32[]{:S(2)}) collective-permute-start(bf16[128,128]{1,0:T(8,128)(2,1)S(1)} %get-tuple-element.52), channel_id=1, source_target_pairs={{0,24},{2,26},{4,28},{6,30},{8,16},{10,18},{12,20},{14,22},{16,8},... | collective-permute-start | bytes 98312 | tf_op jit(solution)/shard_map/ppermute | solution.py:398
  109.4 5.1 %collective-permute-start.30 = (bf16[128,128]{1,0:T(8,128)(2,1)S(1)}, bf16[128,128]{1,0:T(8,128)(2,1)S(1)}, u32[]{:S(2)}, u32[]{:S(2)}) collective-permute-start(bf16[128,128]{1,0:T(8,128)(2,1)S(1)} %get-tuple-element.50), channel_id=1, source_target_pairs={{0,16},{2,18},{4,20},{6,22},{8,24},{10,26},{12,28},{14,30},{16,0},... | collective-permute-start | bytes 98312 | tf_op jit(solution)/shard_map/ppermute | solution.py:398
  112.8 4.7 %collective-permute-start.36 = (bf16[128,256]{1,0:T(8,128)(2,1)S(1)}, bf16[128,256]{1,0:T(8,128)(2,1)S(1)}, u32[]{:S(2)}, u32[]{:S(2)}) collective-permute-start(bf16[128,256]{1,0:T(8,128)(2,1)S(1)} %shard_map.76), channel_id=1, source_target_pairs={{0,1},{1,0},{2,3},{3,2},{4,5},{5,4},{6,7},{7,6},{8,9},{9,8},{10,11... | collective-permute-start | bytes 196616 | tf_op jit(solution)/shard_map/ppermute | solution.py:404
  (17 other events, 151.3 us)

commit v5 on v4

--- a/solution.py
+++ b/solution.py
@@ -116,7 +116,7 @@
     for copy in started:
         copy.start()
     row = 2 * k.shape[0] + 2 * slots
-    for kv in (own_kv, *first[::2], *last):
+    for kv in (own_kv, *first[::2]):
         lane = lax.broadcasted_iota(jnp.int32, (16, kv.shape[1]), 1)
         kv[row : row + 16, :] = jnp.where(lax.rem(lane, slots) < len_ref[0], 1.0, 0.0).astype(
             jnp.bfloat16
@@ -134,7 +134,7 @@
 
     shapes = [array(rows, width), array(tokens, width)]
     shapes += [array(rows, width - late), array(tokens, width - late)] * (GROUPS - 1)
-    shapes += [array(rows + tokens, late)] * (GROUPS - 1)
+    shapes += [array(rows - 16 + tokens, late)] * (GROUPS - 1)
     made = pl.pallas_call(
         functools.partial(pack_kernel, seq, width, late, slots),
         out_shape=shapes,
@@ -187,7 +187,7 @@
     )(*pieces)
 
 
-def gather_kernel(places, tokens, slots, refs, keys, values, usable):
+def gather_kernel(places, tokens, slots, refs, keys, values):
     block = len(places) * tokens
     n = keys.shape[1]
     for i, (which, row, col) in enumerate(places):
@@ -199,6 +199,9 @@
         row += 2 * tokens
         keys[at, :] = kv[row : row + slots, cols]
         values[at, :] = kv[row + slots : row + 2 * slots, cols]
+
+
+def flag_kernel(places, tokens, slots, refs, usable):
     lane = lax.broadcasted_iota(jnp.int32, (16, 128), 1)
     each = 128 // slots
     for start in range(0, len(places), each):
@@ -245,26 +248,40 @@
                 outs[(start + row) // tokens][:, cols] = out[row : row + tokens]
 
 
-def gather_and_attend_kernel(n_in, kv_places, q_places, tokens, slots, *refs):
+def gather_and_attend_kernel(n_in, kv_places, q_places, tokens, slots, flagged, *refs):
     ins, outs = refs[:n_in], refs[n_in : n_in + len(q_places)]
-    whole, query = refs[n_in + len(q_places) : -1], refs[-1]
-    gather_kernel(kv_places, tokens, slots, ins, *whole)
-    attend_kernel(len(kv_places) * tokens, tokens, q_places, ins, *whole, outs, query)
-
-
-def gather_and_attend(arrays, kv_places, q_places, width, tokens, slots):
+    kept, query = refs[n_in + len(q_places) : -1], refs[-1]
+    gather_kernel(kv_places, tokens, slots, ins, *kept[:2])
+    if not flagged:
+        flag_kernel(kv_places, tokens, slots, ins, kept[2])
+    usable = ins[-1] if flagged else kept[2]
+    attend_kernel(len(kv_places) * tokens, tokens, q_places, ins, *kept[:2], usable, outs, query)
+
+
+def gather_and_attend(arrays, kv_places, q_places, width, tokens, slots, usable=None):
+    flagged = usable is not None
+    arrays = [*arrays, usable] if flagged else arrays
     rows = len(kv_places) * (tokens + slots)
-    out = jax.ShapeDtypeStruct((tokens, width), jnp.bfloat16)
-    rows_kept = jax.ShapeDtypeStruct((rows, width), jnp.bfloat16)
-    flags = jax.ShapeDtypeStruct((16, len(kv_places) * slots), jnp.float32)
+    shapes = [jax.ShapeDtypeStruct((tokens, width), jnp.bfloat16)] * len(q_places)
+    whole = [pltpu.VMEM((rows, width), jnp.bfloat16)] * 2
+    if not flagged:
+        shapes += [jax.ShapeDtypeStruct((rows, width), jnp.bfloat16)] * 2
+        shapes += [jax.ShapeDtypeStruct((16, len(kv_places) * slots), jnp.float32)]
     made = pl.pallas_call(
         functools.partial(
-            gather_and_attend_kernel, len(arrays), tuple(kv_places), tuple(q_places), tokens, slots
+            gather_and_attend_kernel,
+            len(arrays),
+            tuple(kv_places),
+            tuple(q_places),
+            tokens,
+            slots,
+            flagged,
         ),
-        out_shape=[out] * len(q_places) + [rows_kept, rows_kept, flags],
+        out_shape=shapes,
         in_specs=[inside()] * len(arrays),
-        out_specs=[inside()] * (len(q_places) + 3),
-        scratch_shapes=[pltpu.VMEM((len(q_places) * tokens, width), jnp.bfloat16)],
+        out_specs=[inside()] * len(shapes),
+        scratch_shapes=whole * flagged
+        + [pltpu.VMEM((len(q_places) * tokens, width), jnp.bfloat16)],
         compiler_params=pltpu.CompilerParams(vmem_limit_bytes=20 << 20),
         name="gather_and_attend",
     )(*arrays)
@@ -353,7 +370,7 @@
 
 
 def finish_kernel(n_pieces, order, own, w_mine, w_near, *refs):
-    pieces, theirs, out, attended = refs[:n_pieces], refs[n_pieces:-2], refs[-2], refs[-1]
+    pieces, theirs, (out, attended, made, sems) = refs[:n_pieces], refs[n_pieces:-4], refs[-4:]
     n = w_mine.shape[0]
     each = n * CORES // len(order)
     for i, place in enumerate(order):
@@ -363,14 +380,21 @@
     core = lax.rem(lax.axis_index("seq"), CORES)
     mine = attended[:, pl.ds(pl.multiple_of(core * n, n), n)]
     near = attended[:, pl.ds(pl.multiple_of((1 - core) * n, n), n)]
-    start = 0
+    start, copies = 0, []
     for piece in theirs:
-        at = slice(start, start + piece.shape[1])
-        total = own[:, at] + piece[...].astype(jnp.float32)
-        total += jnp.dot(mine, w_mine[:, at], preferred_element_type=jnp.float32)
-        total += jnp.dot(near, w_near[:, at], preferred_element_type=jnp.float32)
-        out[:, at] = total.astype(out.dtype)
-        start += piece.shape[1]
+        step = theirs[0].shape[1]
+        for first in range(0, piece.shape[1], step):
+            at = slice(start, start + step)
+            total = own[:, at] + piece[:, first : first + step].astype(jnp.float32)
+            total += jnp.dot(mine, w_mine[:, at], preferred_element_type=jnp.float32)
+            total += jnp.dot(near, w_near[:, at], preferred_element_type=jnp.float32)
+            made[:, at] = total.astype(made.dtype)
+            copy = pltpu.make_async_copy(made.at[:, at], out.at[:, at], sems.at[len(copies)])
+            copy.start()
+            copies.append(copy)
+            start += step
+    for copy in copies:
+        copy.wait()
 
 
 def finish(own, attended, order, w_mine, w_near, theirs):
@@ -378,8 +402,12 @@
         functools.partial(finish_kernel, len(attended), tuple(order)),
         out_shape=jax.ShapeDtypeStruct(own.shape, jnp.bfloat16),
         in_specs=[inside()] * (3 + len(attended) + len(theirs)),
-        out_specs=inside(),
-        scratch_shapes=[pltpu.VMEM((own.shape[0], w_mine.shape[0] * CORES), jnp.bfloat16)],
+        out_specs=outside(),
+        scratch_shapes=[
+            pltpu.VMEM((own.shape[0], w_mine.shape[0] * CORES), jnp.bfloat16),
+            pltpu.VMEM(own.shape, jnp.bfloat16),
+            pltpu.SemaphoreType.DMA((own.shape[1] // theirs[0].shape[1],)),
+        ],
         compiler_params=pltpu.CompilerParams(vmem_limit_bytes=8 << 20),
         name="finish",
     )(own, w_mine, w_near, *attended, *theirs)
@@ -432,7 +460,7 @@
     near_parts = attend(kept, [held_q, qs[0]], [(0, 0, 0), (1, 0, 0)], tokens)
     parts = [near_parts[0], over_z(near_parts[1], 1)]
     parts += [over_z(far_parts[j], j + 2) for j in range(2)]
-    rows = 2 * tokens + 2 * slots + 16
+    rows = 2 * tokens + 2 * slots
     joined = join(0, ends[1:], rows)
     pieces = []
     for piece in (ends[0], joined):
@@ -440,7 +468,7 @@
         near, across = over(piece, 1), over(far, 1)
         pieces += [piece, near, far, across]
     places = [(i, 0, early) for i in range(4)] + [(4 + i, 0, 0) for i in range(4)]
-    places += [(8 + i, j * rows, 0) for i in range(4) for j in range(GROUPS - 2)]
+    places += [(8 + i, j * rows, 0) for j in range(GROUPS - 2) for i in range(4)]
     end_parts, _ = gather_and_attend(
         owns + pieces + [held_q] + ends[1:],
         places,
@@ -448,6 +476,7 @@
         late,
         tokens,
         slots,
+        kept[2],
     )
     end_parts = [end_parts[0]] + [over_z(end_parts[j], j) for j in steps]
     half = out_weight.shape[1] // 2

time: 121 us -> 129 us (1.066)
  waiting for transfers between devices: 52.5 us -> 65.1 us
  starting transfers between devices: 44.2 us -> 41.2 us
    ppermute x5, waiting for transfers between devices: 24.2 us -> 30.5 us  [over_x(): return lax.ppermute(x, 'head', [(0, 1), (1, 0)])]
    ppermute x34, waiting for transfers between devices: 28.3 us -> 34.6 us  [over(): return lax.ppermute(x, 'seq', [(s, s ^ flip) for s in range(seq)])]
    ppermute x34, starting transfers between devices: 36 us -> 33.4 us  [over(): return lax.ppermute(x, 'seq', [(s, s ^ flip) for s in range(seq)])]
  transfers between devices with their start and end apart: 39 -> 39, of which waited for: 13 -> 15; matrix products, arithmetic and copies ran while one was open for 0% -> 0% of each run, Pallas kernels for 11% -> 9%
where the time goes in v5:
time: 129 us
  waiting for transfers between devices  65.1 us (50%)
  starting transfers between devices  41.2 us (32%)
  Pallas kernels  14.4 us (11%)
  local copies, waits for them, and re-layouts  7.33 us (6%)
    ppermute x34, waiting for transfers between devices, over(): return lax.ppermute(x, 'seq', [(s, s ^ flip) for s in range(seq)])  34.6 us
    ppermute x34, starting transfers between devices, over(): return lax.ppermute(x, 'seq', [(s, s ^ flip) for s in range(seq)])  33.4 us
    ppermute x5, waiting for transfers between devices, over_x(): return lax.ppermute(x, 'head', [(0, 1), (1, 0)])  30.5 us
    ppermute x5, starting transfers between devices, over_x(): return lax.ppermute(x, 'head', [(0, 1), (1, 0)])  7.78 us
    unnamed x20, local copies, waits for them, and re-layouts  7.33 us
    pallas_call x2, Pallas kernels, gather_and_attend(): pl.pallas_call(functools.partial(gather_and_attend_kernel, len(arrays), t...  4.27 us
    pallas_call x1, Pallas kernels, pack(): pl.pallas_call(functools.partial(pack_kernel, seq, width, late, slots), o...  2.73 us
    pallas_call x3, Pallas kernels, project(): pl.pallas_call(functools.partial(project_kernel, seq, width, other, start...  2.67 us
  transfers between devices with their start and end apart: 39, of which 15 were waited for; matrix products, arithmetic and copies ran while one was open for 0% of the time, Pallas kernels for 9%

profile of v5, /device:TPU:0, one launch (start us, length us, event | category | flops | bytes accessed | tf_op | source)
XLA Modules:
  0.0 128.9 jit_solution(11065527825527950250)
XLA Ops:
  1.3 3.0 %collective-permute-start.33 = (bf16[256,2560]{1,0:T(8,128)(2,1)S(1)}, bf16[256,2560]{1,0:T(8,128)(2,1)S(1)}, u32[]{:S(2)}, u32[]{:S(2)}) collective-permute-start(bf16[256,2560]{1,0:T(8,128)(2,1)S(1)} %shard_map.74), channel_id=1, source_target_pairs={{0,1},{1,0},{2,3},{3,2},{4,5},{5,4},{6,7},{7,6},{8,9},{9,8},{10,11... | collective-permute-start | bytes 3932168 | tf_op jit(solution)/shard_map/ppermute | solution.py:432
  4.3 28.8 %collective-permute-done.33.w_mine = bf16[256,2560]{1,0:T(8,128)(2,1)S(1)} collective-permute-done((bf16[256,2560]{1,0:T(8,128)(2,1)S(1)}, bf16[256,2560]{1,0:T(8,128)(2,1)S(1)}, u32[]{:S(2)}, u32[]{:S(2)}) %collective-permute-start.33) | collective-permute-done | bytes 1310752 | tf_op jit(solution)/shard_map/ppermute | solution.py:432
  33.8 2.7 %pack.1 = (bf16[304,384]{1,0:T(8,128)(2,1)}, bf16[128,384]{1,0:T(8,128)(2,1)}, bf16[304,256]{1,0:T(8,128)(2,1)}, bf16[128,256]{1,0:T(8,128)(2,1)}, bf16[304,256]...) custom-call(s32[1]{0:T(128)S(6)} %copy.8.len_ref, ...), custom_call_target="tpu_custom_call" | custom-call | tf_op jit(solution)/shard_map/pack/pallas_call | solution.py:138
  36.5 2.9 %collective-permute-start.7 = (bf16[304,256]{1,0:T(8,128)(2,1)}, bf16[304,256]{1,0:T(8,128)(2,1)S(1)}, u32[]{:S(2)}, u32[]{:S(2)}) collective-permute-start(bf16[304,256]{1,0:T(8,128)(2,1)} %get-tuple-element.33), channel_id=1, source_target_pairs={{0,16},{2,18},{4,20},{6,22},{8,24},{10,26},{12,28},{14,30},{16,0},... | collective-permute-start | bytes 466952 | tf_op jit(solution)/shard_map/ppermute | solution.py:426
  39.5 3.9 %collective-permute-start.16 = (bf16[128,256]{1,0:T(8,128)(2,1)}, bf16[128,256]{1,0:T(8,128)(2,1)S(1)}, u32[]{:S(2)}, u32[]{:S(2)}) collective-permute-start(bf16[128,256]{1,0:T(8,128)(2,1)} %get-tuple-element.36), channel_id=1, source_target_pairs={{0,24},{2,26},{4,28},{6,30},{8,16},{10,18},{12,20},{14,22},{16,8},... | collective-permute-start | bytes 196616 | tf_op jit(solution)/shard_map/ppermute | solution.py:426
  43.4 1.5 %collective-permute-start.1 = (bf16[304,384]{1,0:T(8,128)(2,1)}, bf16[304,384]{1,0:T(8,128)(2,1)S(1)}, u32[]{:S(2)}, u32[]{:S(2)}) collective-permute-start(bf16[304,384]{1,0:T(8,128)(2,1)} %get-tuple-element.29.refs_0_), channel_id=1, source_target_pairs={{0,4},{2,6},{4,0},{6,2},{8,12},{10,14},{12,8},{14,10},{16,20},{18,... | collective-permute-start | bytes 700424 | tf_op jit(solution)/shard_map/ppermute | solution.py:426
  44.9 7.3 %collective-permute-done.15.refs_16_ = bf16[128,256]{1,0:T(8,128)(2,1)S(1)} collective-permute-done((bf16[128,256]{1,0:T(8,128)(2,1)}, bf16[128,256]{1,0:T(8,128)(2,1)S(1)}, u32[]{:S(2)}, u32[]{:S(2)}) %collective-permute-start.15) | collective-permute-done | bytes 65568 | tf_op jit(solution)/shard_map/ppermute | solution.py:426
  52.1 3.3 %collective-permute-start.11 = (bf16[304,256]{1,0:T(8,128)(2,1)}, bf16[304,256]{1,0:T(8,128)(2,1)S(1)}, u32[]{:S(2)}, u32[]{:S(2)}) collective-permute-start(bf16[304,256]{1,0:T(8,128)(2,1)} %get-tuple-element.34), channel_id=1, source_target_pairs={{0,24},{2,26},{4,28},{6,30},{8,16},{10,18},{12,20},{14,22},{16,8},... | collective-permute-start | bytes 466952 | tf_op jit(solution)/shard_map/ppermute | solution.py:426
  55.5 5.5 %collective-permute-done.11.refs_12_ = bf16[304,256]{1,0:T(8,128)(2,1)S(1)} collective-permute-done((bf16[304,256]{1,0:T(8,128)(2,1)}, bf16[304,256]{1,0:T(8,128)(2,1)S(1)}, u32[]{:S(2)}, u32[]{:S(2)}) %collective-permute-start.11) | collective-permute-done | bytes 155680 | tf_op jit(solution)/shard_map/ppermute | solution.py:426
  61.0 1.8 %collective-permute-start.9 = (bf16[304,256]{1,0:T(8,128)(2,1)S(1)}, bf16[304,256]{1,0:T(8,128)(2,1)S(1)}, u32[]{:S(2)}, u32[]{:S(2)}) collective-permute-start(bf16[304,256]{1,0:T(8,128)(2,1)S(1)} %collective-permute-done.7.refs_8_), channel_id=1, source_target_pairs={{0,4},{2,6},{4,0},{6,2},{8,12},{10,14},{12,8},{14,10},{16,20},{18,... | collective-permute-start | bytes 466952 | tf_op jit(solution)/shard_map/ppermute | solution.py:426
  63.3 1.5 %collective-permute-start.13 = (bf16[304,256]{1,0:T(8,128)(2,1)S(1)}, bf16[304,256]{1,0:T(8,128)(2,1)S(1)}, u32[]{:S(2)}, u32[]{:S(2)}) collective-permute-start(bf16[304,256]{1,0:T(8,128)(2,1)S(1)} %collective-permute-done.11.refs_12_), channel_id=1, source_target_pairs={{0,4},{2,6},{4,0},{6,2},{8,12},{10,14},{12,8},{14,10},{16,20},{18,... | collective-permute-start | bytes 466952 | tf_op jit(solution)/shard_map/ppermute | solution.py:426
  65.3 1.3 %collective-permute-done.9.refs_10_ = bf16[304,256]{1,0:T(8,128)(2,1)S(1)} collective-permute-done((bf16[304,256]{1,0:T(8,128)(2,1)S(1)}, bf16[304,256]{1,0:T(8,128)(2,1)S(1)}, u32[]{:S(2)}, u32[]{:S(2)}) %collective-permute-start.9) | collective-permute-done | bytes 155680 | tf_op jit(solution)/shard_map/ppermute | solution.py:426
  66.7 3.5 %collective-permute-done.13.refs_14_ = bf16[304,256]{1,0:T(8,128)(2,1)S(1)} collective-permute-done((bf16[304,256]{1,0:T(8,128)(2,1)S(1)}, bf16[304,256]{1,0:T(8,128)(2,1)S(1)}, u32[]{:S(2)}, u32[]{:S(2)}) %collective-permute-start.13) | collective-permute-done | bytes 155680 | tf_op jit(solution)/shard_map/ppermute | solution.py:426
  70.2 2.7 %collective-permute-done.5.refs_6_ = bf16[304,256]{1,0:T(8,128)(2,1)S(1)} collective-permute-done((bf16[304,256]{1,0:T(8,128)(2,1)S(1)}, bf16[304,256]{1,0:T(8,128)(2,1)S(1)}, u32[]{:S(2)}, u32[]{:S(2)}) %collective-permute-start.5) | collective-permute-done | bytes 155680 | tf_op jit(solution)/shard_map/ppermute | solution.py:426
  77.5 2.2 %gather_and_attend.2 = (bf16[128,256]{1,0:T(8,128)(2,1)S(1)}, bf16[128,256]{1,0:T(8,128)(2,1)S(1)}, bf16[2304,256]{1,0:T(8,128)(2,1)S(1)}, bf16[2304,256]{1,0:T(8,128)(2,1)S(1)}, f32[16,256]{1,0:T(8,128)S(1)}) custom-call(bf16[304,384]{1,0:T(8,128)(2,1)S(1)} %get-tuple-element.31.refs_0_, bf16[304,384]{1,0:T(8,128)(2,1)S(1)} %collective-permute-done.refs_1_, ...), custom_call_target="tpu_custom_call" | custom-call | tf_op jit(solution)/shard_map/gather_and_attend/pallas_call | solution.py:270
  79.7 2.1 %attend.1 = (bf16[128,256]{1,0:T(8,128)(2,1)S(1)}, bf16[128,256]{1,0:T(8,128)(2,1)S(1)}) custom-call(bf16[2304,256]{1,0:T(8,128)(2,1)S(1)} %get-tuple-element.37.refs_0_, bf16[2304,256]{1,0:T(8,128)(2,1)S(1)} %get-tuple-element.38.refs_1_, f32[16,256]{1,0:T(8,128)S(1)} %get-tuple-element.39.refs_2_.refs_15_, ...), custom_call_target="tpu_custom_call" | custom-call | tf_op jit(solution)/shard_map/attend/pallas_call | solution.py:299
  83.9 2.4 %collective-permute-start.31 = (bf16[128,256]{1,0:T(8,128)(2,1)S(1)}, bf16[128,256]{1,0:T(8,128)(2,1)S(1)}, u32[]{:S(2)}, u32[]{:S(2)}) collective-permute-start(bf16[128,256]{1,0:T(8,128)(2,1)S(1)} %get-tuple-element.51), channel_id=1, source_target_pairs={{0,24},{2,26},{4,28},{6,30},{8,16},{10,18},{12,20},{14,22},{16,8},... | collective-permute-start | bytes 196616 | tf_op jit(solution)/shard_map/ppermute | solution.py:426
  87.0 1.6 %collective-permute-start.23 = (bf16[416,128]{1,0:T(8,128)(2,1)S(1)}, bf16[416,128]{1,0:T(8,128)(2,1)S(1)}, u32[]{:S(2)}, u32[]{:S(2)}) collective-permute-start(bf16[416,128]{1,0:T(8,128)(2,1)S(1)} %copy-done.4), channel_id=1, source_target_pairs={{0,24},{2,26},{4,28},{6,30},{8,16},{10,18},{12,20},{14,22},{16,8},... | collective-permute-start | bytes 319496 | tf_op jit(solution)/shard_map/ppermute | solution.py:426
  88.6 7.0 %collective-permute-done.29.refs_4_.refs_2_ = bf16[128,256]{1,0:T(8,128)(2,1)S(1)} collective-permute-done((bf16[128,256]{1,0:T(8,128)(2,1)S(1)}, bf16[128,256]{1,0:T(8,128)(2,1)S(1)}, u32[]{:S(2)}, u32[]{:S(2)}) %collective-permute-start.29) | collective-permute-done | bytes 65568 | tf_op jit(solution)/shard_map/ppermute | solution.py:426
  95.5 5.5 %copy-done = bf16[1536,5120]{1,0:T(8,128)(2,1)S(1)} copy-done((bf16[1536,5120]{1,0:T(8,128)(2,1)S(1)}, bf16[1536,5120]{1,0:T(8,128)(2,1)}, u32[]{:S(2)}) %copy-start) | copy-done | bytes 15728664
  101.7 1.7 %collective-permute-start.38 = (bf16[128,1920]{1,0:T(8,128)(2,1)S(1)}, bf16[128,1920]{1,0:T(8,128)(2,1)S(1)}, u32[]{:S(2)}, u32[]{:S(2)}) collective-permute-start(bf16[128,1920]{1,0:T(8,128)(2,1)S(1)} %project.5), channel_id=1, source_target_pairs={{0,1},{1,0},{2,3},{3,2},{4,5},{5,4},{6,7},{7,6},{8,9},{9,8},{10,11... | collective-permute-start | bytes 1474568 | tf_op jit(solution)/shard_map/ppermute | solution.py:432
  103.5 1.6 %collective-permute-start.25 = (bf16[576,128]{1,0:T(8,128)(2,1)S(1)}, bf16[576,128]{1,0:T(8,128)(2,1)S(1)}, u32[]{:S(2)}, u32[]{:S(2)}) collective-permute-start(bf16[576,128]{1,0:T(8,128)(2,1)S(1)} %shard_map.73.refs_8_), channel_id=1, source_target_pairs={{0,4},{2,6},{4,0},{6,2},{8,12},{10,14},{12,8},{14,10},{16,20},{18,... | collective-permute-start | bytes 442376 | tf_op jit(solution)/shard_map/ppermute | solution.py:426
  105.6 4.3 %collective-permute-done.20.refs_6_ = bf16[416,128]{1,0:T(8,128)(2,1)S(1)} collective-permute-done((bf16[416,128]{1,0:T(8,128)(2,1)S(1)}, bf16[416,128]{1,0:T(8,128)(2,1)S(1)}, u32[]{:S(2)}, u32[]{:S(2)}) %collective-permute-start.20) | collective-permute-done | bytes 106528 | tf_op jit(solution)/shard_map/ppermute | solution.py:426
  111.7 2.1 %gather_and_attend.3 = (bf16[128,128]{1,0:T(8,128)(2,1)S(1)}, bf16[128,128]{1,0:T(8,128)(2,1)S(1)}, bf16[128,128]{1,0:T(8,128)(2,1)S(1)}, bf16[128,128]{1,0:T(8,128)(2,1)S(1)}) custom-call(bf16[304,384]{1,0:T(8,128)(2,1)S(1)} %get-tuple-element.31.refs_0_, bf16[304,384]{1,0:T(8,128)(2,1)S(1)} %collective-permute-done.refs_1_, ...), custom_call_target="tpu_custom_call" | custom-call | tf_op jit(solution)/shard_map/gather_and_attend/pallas_call | solution.py:270
  113.8 2.1 %collective-permute-start.28 = (bf16[128,128]{1,0:T(8,128)(2,1)S(1)}, bf16[128,128]{1,0:T(8,128)(2,1)S(1)}, u32[]{:S(2)}, u32[]{:S(2)}) collective-permute-start(bf16[128,128]{1,0:T(8,128)(2,1)S(1)} %get-tuple-element.48), channel_id=1, source_target_pairs={{0,8},{2,10},{4,12},{6,14},{8,0},{10,2},{12,4},{14,6},{16,24},{18,... | collective-permute-start | bytes 98312 | tf_op jit(solution)/shard_map/ppermute | solution.py:426
  115.9 1.8 %collective-permute-start.32 = (bf16[128,128]{1,0:T(8,128)(2,1)S(1)}, bf16[128,128]{1,0:T(8,128)(2,1)S(1)}, u32[]{:S(2)}, u32[]{:S(2)}) collective-permute-start(bf16[128,128]{1,0:T(8,128)(2,1)S(1)} %get-tuple-element.52), channel_id=1, source_target_pairs={{0,24},{2,26},{4,28},{6,30},{8,16},{10,18},{12,20},{14,22},{16,8},... | collective-permute-start | bytes 98312 | tf_op jit(solution)/shard_map/ppermute | solution.py:426
  117.8 2.3 %collective-permute-start.30 = (bf16[128,128]{1,0:T(8,128)(2,1)S(1)}, bf16[128,128]{1,0:T(8,128)(2,1)S(1)}, u32[]{:S(2)}, u32[]{:S(2)}) collective-permute-start(bf16[128,128]{1,0:T(8,128)(2,1)S(1)} %get-tuple-element.50), channel_id=1, source_target_pairs={{0,16},{2,18},{4,20},{6,22},{8,24},{10,26},{12,28},{14,30},{16,0},... | collective-permute-start | bytes 98312 | tf_op jit(solution)/shard_map/ppermute | solution.py:426
  120.1 1.5 %collective-permute-done.32.refs_7_.refs_1_ = bf16[128,128]{1,0:T(8,128)(2,1)S(1)} collective-permute-done((bf16[128,128]{1,0:T(8,128)(2,1)S(1)}, bf16[128,128]{1,0:T(8,128)(2,1)S(1)}, u32[]{:S(2)}, u32[]{:S(2)}) %collective-permute-start.32) | collective-permute-done | bytes 32800 | tf_op jit(solution)/shard_map/ppermute | solution.py:426
  121.6 1.6 %collective-permute-start.36 = (bf16[128,256]{1,0:T(8,128)(2,1)S(1)}, bf16[128,256]{1,0:T(8,128)(2,1)S(1)}, u32[]{:S(2)}, u32[]{:S(2)}) collective-permute-start(bf16[128,256]{1,0:T(8,128)(2,1)S(1)} %shard_map.76), channel_id=1, source_target_pairs={{0,1},{1,0},{2,3},{3,2},{4,5},{5,4},{6,7},{7,6},{8,9},{9,8},{10,11... | collective-permute-start | bytes 196616 | tf_op jit(solution)/shard_map/ppermute | solution.py:432
  124.3 1.6 %project.3.own = f32[128,2560]{1,0:T(8,128)S(1)} custom-call(bf16[128,256]{1,0:T(8,128)(2,1)S(1)} %get-tuple-element.42.refs_0_, bf16[128,128]{1,0:T(8,128)(2,1)S(1)} %get-tuple-element.46.refs_1_.refs_0_, bf16[128,256]{1,0:T(8,128)(2,1)S(1)} %collective-permute-done.27.refs_2_.refs_1_, bf16[128,128]{1,0:T(8,128)(2,1)S(1)} %collective-permute-done.28.refs_3_.refs_0_, ...), custom_call_target="tpu_custom_call" | custom-call | tf_op jit(solution)/shard_map/project/pallas_call | solution.py:362
  126.0 1.6 %collective-permute-done.35.refs_0_ = bf16[128,256]{1,0:T(8,128)(2,1)S(1)} collective-permute-done((bf16[128,256]{1,0:T(8,128)(2,1)S(1)}, bf16[128,256]{1,0:T(8,128)(2,1)S(1)}, u32[]{:S(2)}, u32[]{:S(2)}) %collective-permute-start.35) | collective-permute-done | bytes 65568 | tf_op jit(solution)/shard_map/ppermute | solution.py:432
  127.6 1.3 %finish.1 = bf16[128,2560]{1,0:T(8,128)(2,1)} custom-call(f32[128,2560]{1,0:T(8,128)S(1)} %project.3.own, bf16[256,2560]{1,0:T(8,128)(2,1)S(1)} %collective-permute-done.33.w_mine, bf16[256,2560]{1,0:T(8,128)(2,1)S(1)} %collective-permute-done.34.w_near, bf16[128,256]{1,0:T(8,128)(2,1)S(1)} %collective-permute-done.35.refs_0_, ...), custom_call_target="tpu_custom_call" | custom-call | tf_op jit(solution)/shard_map/finish/pallas_call | solution.py:401
  (80 shorter events, 14.3 us)
Async XLA Ops:
  1.3 31.8 %collective-permute-start.33 = (bf16[256,2560]{1,0:T(8,128)(2,1)S(1)}, bf16[256,2560]{1,0:T(8,128)(2,1)S(1)}, u32[]{:S(2)}, u32[]{:S(2)}) collective-permute-start(bf16[256,2560]{1,0:T(8,128)(2,1)S(1)} %shard_map.74), channel_id=1, source_target_pairs={{0,1},{1,0},{2,3},{3,2},{4,5},{5,4},{6,7},{7,6},{8,9},{9,8},{10,11... | collective-permute-start | bytes 3932168 | tf_op jit(solution)/shard_map/ppermute | solution.py:432
  33.1 94.5 %collective-permute-start.34 = (bf16[256,2560]{1,0:T(8,128)(2,1)S(1)}, bf16[256,2560]{1,0:T(8,128)(2,1)S(1)}, u32[]{:S(2)}, u32[]{:S(2)}) collective-permute-start(bf16[256,2560]{1,0:T(8,128)(2,1)S(1)} %collective-permute-done.33.w_mine), channel_id=1, source_target_pairs={{0,2},{2,0},{4,6},{6,4},{8,10},{10,8},{12,14},{14,12},{16,18},{18,... | collective-permute-start | bytes 3932168 | tf_op jit(solution)/shard_map/ppermute | solution.py:426
  36.5 18.9 %collective-permute-start.7 = (bf16[304,256]{1,0:T(8,128)(2,1)}, bf16[304,256]{1,0:T(8,128)(2,1)S(1)}, u32[]{:S(2)}, u32[]{:S(2)}) collective-permute-start(bf16[304,256]{1,0:T(8,128)(2,1)} %get-tuple-element.33), channel_id=1, source_target_pairs={{0,16},{2,18},{4,20},{6,22},{8,24},{10,26},{12,28},{14,30},{16,0},... | collective-permute-start | bytes 466952 | tf_op jit(solution)/shard_map/ppermute | solution.py:426
  39.4 12.7 %collective-permute-start.15 = (bf16[128,256]{1,0:T(8,128)(2,1)}, bf16[128,256]{1,0:T(8,128)(2,1)S(1)}, u32[]{:S(2)}, u32[]{:S(2)}) collective-permute-start(bf16[128,256]{1,0:T(8,128)(2,1)} %get-tuple-element.35), channel_id=1, source_target_pairs={{0,16},{2,18},{4,20},{6,22},{8,24},{10,26},{12,28},{14,30},{16,0},... | collective-permute-start | bytes 196616 | tf_op jit(solution)/shard_map/ppermute | solution.py:426
  39.5 15.9 %collective-permute-start.16 = (bf16[128,256]{1,0:T(8,128)(2,1)}, bf16[128,256]{1,0:T(8,128)(2,1)S(1)}, u32[]{:S(2)}, u32[]{:S(2)}) collective-permute-start(bf16[128,256]{1,0:T(8,128)(2,1)} %get-tuple-element.36), channel_id=1, source_target_pairs={{0,24},{2,26},{4,28},{6,30},{8,16},{10,18},{12,20},{14,22},{16,8},... | collective-permute-start | bytes 196616 | tf_op jit(solution)/shard_map/ppermute | solution.py:426
  43.4 21.5 %collective-permute-start.1 = (bf16[304,384]{1,0:T(8,128)(2,1)}, bf16[304,384]{1,0:T(8,128)(2,1)S(1)}, u32[]{:S(2)}, u32[]{:S(2)}) collective-permute-start(bf16[304,384]{1,0:T(8,128)(2,1)} %get-tuple-element.29.refs_0_), channel_id=1, source_target_pairs={{0,4},{2,6},{4,0},{6,2},{8,12},{10,14},{12,8},{14,10},{16,20},{18,... | collective-permute-start | bytes 700424 | tf_op jit(solution)/shard_map/ppermute | solution.py:426
  52.1 8.9 %collective-permute-start.11 = (bf16[304,256]{1,0:T(8,128)(2,1)}, bf16[304,256]{1,0:T(8,128)(2,1)S(1)}, u32[]{:S(2)}, u32[]{:S(2)}) collective-permute-start(bf16[304,256]{1,0:T(8,128)(2,1)} %get-tuple-element.34), channel_id=1, source_target_pairs={{0,24},{2,26},{4,28},{6,30},{8,16},{10,18},{12,20},{14,22},{16,8},... | collective-permute-start | bytes 466952 | tf_op jit(solution)/shard_map/ppermute | solution.py:426
  55.4 7.9 %collective-permute-start.3 = (bf16[304,256]{1,0:T(8,128)(2,1)}, bf16[304,256]{1,0:T(8,128)(2,1)S(1)}, u32[]{:S(2)}, u32[]{:S(2)}) collective-permute-start(bf16[304,256]{1,0:T(8,128)(2,1)} %get-tuple-element.32), channel_id=1, source_target_pairs={{0,8},{2,10},{4,12},{6,14},{8,0},{10,2},{12,4},{14,6},{16,24},{18,... | collective-permute-start | bytes 466952 | tf_op jit(solution)/shard_map/ppermute | solution.py:426
  55.5 9.9 %collective-permute-start = (bf16[304,384]{1,0:T(8,128)(2,1)}, bf16[304,384]{1,0:T(8,128)(2,1)S(1)}, u32[]{:S(2)}, u32[]{:S(2)}) collective-permute-start(bf16[304,384]{1,0:T(8,128)(2,1)} %get-tuple-element.29.refs_0_), channel_id=1, source_target_pairs={{0,2},{2,0},{4,6},{6,4},{8,10},{10,8},{12,14},{14,12},{16,18},{18,... | collective-permute-start | bytes 700424 | tf_op jit(solution)/shard_map/ppermute | solution.py:426
  61.0 5.6 %collective-permute-start.9 = (bf16[304,256]{1,0:T(8,128)(2,1)S(1)}, bf16[304,256]{1,0:T(8,128)(2,1)S(1)}, u32[]{:S(2)}, u32[]{:S(2)}) collective-permute-start(bf16[304,256]{1,0:T(8,128)(2,1)S(1)} %collective-permute-done.7.refs_8_), channel_id=1, source_target_pairs={{0,4},{2,6},{4,0},{6,2},{8,12},{10,14},{12,8},{14,10},{16,20},{18,... | collective-permute-start | bytes 466952 | tf_op jit(solution)/shard_map/ppermute | solution.py:426
  63.3 6.9 %collective-permute-start.13 = (bf16[304,256]{1,0:T(8,128)(2,1)S(1)}, bf16[304,256]{1,0:T(8,128)(2,1)S(1)}, u32[]{:S(2)}, u32[]{:S(2)}) collective-permute-start(bf16[304,256]{1,0:T(8,128)(2,1)S(1)} %collective-permute-done.11.refs_12_), channel_id=1, source_target_pairs={{0,4},{2,6},{4,0},{6,2},{8,12},{10,14},{12,8},{14,10},{16,20},{18,... | collective-permute-start | bytes 466952 | tf_op jit(solution)/shard_map/ppermute | solution.py:426
  64.8 8.1 %collective-permute-start.5 = (bf16[304,256]{1,0:T(8,128)(2,1)S(1)}, bf16[304,256]{1,0:T(8,128)(2,1)S(1)}, u32[]{:S(2)}, u32[]{:S(2)}) collective-permute-start(bf16[304,256]{1,0:T(8,128)(2,1)S(1)} %collective-permute-done.3.refs_4_), channel_id=1, source_target_pairs={{0,4},{2,6},{4,0},{6,2},{8,12},{10,14},{12,8},{14,10},{16,20},{18,... | collective-permute-start | bytes 466952 | tf_op jit(solution)/shard_map/ppermute | solution.py:426
  65.3 7.6 %collective-permute-start.12 = (bf16[304,256]{1,0:T(8,128)(2,1)S(1)}, bf16[304,256]{1,0:T(8,128)(2,1)S(1)}, u32[]{:S(2)}, u32[]{:S(2)}) collective-permute-start(bf16[304,256]{1,0:T(8,128)(2,1)S(1)} %collective-permute-done.11.refs_12_), channel_id=1, source_target_pairs={{0,2},{2,0},{4,6},{6,4},{8,10},{10,8},{12,14},{14,12},{16,18},{18,... | collective-permute-start | bytes 466952 | tf_op jit(solution)/shard_map/ppermute | solution.py:426
  66.7 6.8 %collective-permute-start.4 = (bf16[304,256]{1,0:T(8,128)(2,1)S(1)}, bf16[304,256]{1,0:T(8,128)(2,1)S(1)}, u32[]{:S(2)}, u32[]{:S(2)}) collective-permute-start(bf16[304,256]{1,0:T(8,128)(2,1)S(1)} %collective-permute-done.3.refs_4_), channel_id=1, source_target_pairs={{0,2},{2,0},{4,6},{6,4},{8,10},{10,8},{12,14},{14,12},{16,18},{18,... | collective-permute-start | bytes 466952 | tf_op jit(solution)/shard_map/ppermute | solution.py:426
  72.9 4.6 %collective-permute-start.10 = (bf16[304,256]{1,0:T(8,128)(2,1)S(1)}, bf16[304,256]{1,0:T(8,128)(2,1)S(1)}, u32[]{:S(2)}, u32[]{:S(2)}) collective-permute-start(bf16[304,256]{1,0:T(8,128)(2,1)S(1)} %collective-permute-done.9.refs_10_), channel_id=1, source_target_pairs={{0,2},{2,0},{4,6},{6,4},{8,10},{10,8},{12,14},{14,12},{16,18},{18,... | collective-permute-start | bytes 466952 | tf_op jit(solution)/shard_map/ppermute | solution.py:426
  73.5 4.1 %collective-permute-start.14 = (bf16[304,256]{1,0:T(8,128)(2,1)S(1)}, bf16[304,256]{1,0:T(8,128)(2,1)S(1)}, u32[]{:S(2)}, u32[]{:S(2)}) collective-permute-start(bf16[304,256]{1,0:T(8,128)(2,1)S(1)} %collective-permute-done.13.refs_14_), channel_id=1, source_target_pairs={{0,2},{2,0},{4,6},{6,4},{8,10},{10,8},{12,14},{14,12},{16,18},{18,... | collective-permute-start | bytes 466952 | tf_op jit(solution)/shard_map/ppermute | solution.py:426
  74.4 5.3 %collective-permute-start.17 = (bf16[128,256]{1,0:T(8,128)(2,1)}, bf16[128,256]{1,0:T(8,128)(2,1)S(1)}, u32[]{:S(2)}, u32[]{:S(2)}) collective-permute-start(bf16[128,256]{1,0:T(8,128)(2,1)} %get-tuple-element.41), channel_id=1, source_target_pairs={{0,8},{2,10},{4,12},{6,14},{8,0},{10,2},{12,4},{14,6},{16,24},{18,... | collective-permute-start | bytes 196616 | tf_op jit(solution)/shard_map/ppermute | solution.py:426
  81.8 5.2 %collective-permute-start.27 = (bf16[128,256]{1,0:T(8,128)(2,1)S(1)}, bf16[128,256]{1,0:T(8,128)(2,1)S(1)}, u32[]{:S(2)}, u32[]{:S(2)}) collective-permute-start(bf16[128,256]{1,0:T(8,128)(2,1)S(1)} %get-tuple-element.47), channel_id=1, source_target_pairs={{0,8},{2,10},{4,12},{6,14},{8,0},{10,2},{12,4},{14,6},{16,24},{18,... | collective-permute-start | bytes 196616 | tf_op jit(solution)/shard_map/ppermute | solution.py:426
  82.7 12.8 %collective-permute-start.29 = (bf16[128,256]{1,0:T(8,128)(2,1)S(1)}, bf16[128,256]{1,0:T(8,128)(2,1)S(1)}, u32[]{:S(2)}, u32[]{:S(2)}) collective-permute-start(bf16[128,256]{1,0:T(8,128)(2,1)S(1)} %get-tuple-element.49), channel_id=1, source_target_pairs={{0,16},{2,18},{4,20},{6,22},{8,24},{10,26},{12,28},{14,30},{16,0},... | collective-permute-start | bytes 196616 | tf_op jit(solution)/shard_map/ppermute | solution.py:426
  83.9 11.7 %collective-permute-start.31 = (bf16[128,256]{1,0:T(8,128)(2,1)S(1)}, bf16[128,256]{1,0:T(8,128)(2,1)S(1)}, u32[]{:S(2)}, u32[]{:S(2)}) collective-permute-start(bf16[128,256]{1,0:T(8,128)(2,1)S(1)} %get-tuple-element.51), channel_id=1, source_target_pairs={{0,24},{2,26},{4,28},{6,30},{8,16},{10,18},{12,20},{14,22},{16,8},... | collective-permute-start | bytes 196616 | tf_op jit(solution)/shard_map/ppermute | solution.py:426
  86.3 17.2 %collective-permute-start.22 = (bf16[416,128]{1,0:T(8,128)(2,1)S(1)}, bf16[416,128]{1,0:T(8,128)(2,1)S(1)}, u32[]{:S(2)}, u32[]{:S(2)}) collective-permute-start(bf16[416,128]{1,0:T(8,128)(2,1)S(1)} %copy-done.5), channel_id=1, source_target_pairs={{0,16},{2,18},{4,20},{6,22},{8,24},{10,26},{12,28},{14,30},{16,0},... | collective-permute-start | bytes 319496 | tf_op jit(solution)/shard_map/ppermute | solution.py:426
  87.0 16.4 %collective-permute-start.23 = (bf16[416,128]{1,0:T(8,128)(2,1)S(1)}, bf16[416,128]{1,0:T(8,128)(2,1)S(1)}, u32[]{:S(2)}, u32[]{:S(2)}) collective-permute-start(bf16[416,128]{1,0:T(8,128)(2,1)S(1)} %copy-done.4), channel_id=1, source_target_pairs={{0,24},{2,26},{4,28},{6,30},{8,16},{10,18},{12,20},{14,22},{16,8},... | collective-permute-start | bytes 319496 | tf_op jit(solution)/shard_map/ppermute | solution.py:426
  95.5 9.5 %collective-permute-start.18 = (bf16[416,128]{1,0:T(8,128)(2,1)S(1)}, bf16[416,128]{1,0:T(8,128)(2,1)S(1)}, u32[]{:S(2)}, u32[]{:S(2)}) collective-permute-start(bf16[416,128]{1,0:T(8,128)(2,1)S(1)} %copy-done.3), channel_id=1, source_target_pairs={{0,8},{2,10},{4,12},{6,14},{8,0},{10,2},{12,4},{14,6},{16,24},{18,... | collective-permute-start | bytes 319496 | tf_op jit(solution)/shard_map/ppermute | solution.py:426
  101.7 25.8 %collective-permute-start.38 = (bf16[128,1920]{1,0:T(8,128)(2,1)S(1)}, bf16[128,1920]{1,0:T(8,128)(2,1)S(1)}, u32[]{:S(2)}, u32[]{:S(2)}) collective-permute-start(bf16[128,1920]{1,0:T(8,128)(2,1)S(1)} %project.5), channel_id=1, source_target_pairs={{0,1},{1,0},{2,3},{3,2},{4,5},{5,4},{6,7},{7,6},{8,9},{9,8},{10,11... | collective-permute-start | bytes 1474568 | tf_op jit(solution)/shard_map/ppermute | solution.py:432
  103.5 6.4 %collective-permute-start.25 = (bf16[576,128]{1,0:T(8,128)(2,1)S(1)}, bf16[576,128]{1,0:T(8,128)(2,1)S(1)}, u32[]{:S(2)}, u32[]{:S(2)}) collective-permute-start(bf16[576,128]{1,0:T(8,128)(2,1)S(1)} %shard_map.73.refs_8_), channel_id=1, source_target_pairs={{0,4},{2,6},{4,0},{6,2},{8,12},{10,14},{12,8},{14,10},{16,20},{18,... | collective-permute-start | bytes 442376 | tf_op jit(solution)/shard_map/ppermute | solution.py:426
  105.1 4.8 %collective-permute-start.20 = (bf16[416,128]{1,0:T(8,128)(2,1)S(1)}, bf16[416,128]{1,0:T(8,128)(2,1)S(1)}, u32[]{:S(2)}, u32[]{:S(2)}) collective-permute-start(bf16[416,128]{1,0:T(8,128)(2,1)S(1)} %collective-permute-done.18.refs_4_), channel_id=1, source_target_pairs={{0,4},{2,6},{4,0},{6,2},{8,12},{10,14},{12,8},{14,10},{16,20},{18,... | collective-permute-start | bytes 319496 | tf_op jit(solution)/shard_map/ppermute | solution.py:426
  105.6 4.8 %collective-permute-start.19 = (bf16[416,128]{1,0:T(8,128)(2,1)S(1)}, bf16[416,128]{1,0:T(8,128)(2,1)S(1)}, u32[]{:S(2)}, u32[]{:S(2)}) collective-permute-start(bf16[416,128]{1,0:T(8,128)(2,1)S(1)} %collective-permute-done.18.refs_4_), channel_id=1, source_target_pairs={{0,2},{2,0},{4,6},{6,4},{8,10},{10,8},{12,14},{14,12},{16,18},{18,... | collective-permute-start | bytes 319496 | tf_op jit(solution)/shard_map/ppermute | solution.py:426
  111.2 16.4 %collective-permute-start.37 = (bf16[128,640]{1,0:T(8,128)(2,1)S(1)}, bf16[128,640]{1,0:T(8,128)(2,1)S(1)}, u32[]{:S(2)}, u32[]{:S(2)}) collective-permute-start(bf16[128,640]{1,0:T(8,128)(2,1)S(1)} %project.4), channel_id=1, source_target_pairs={{0,1},{1,0},{2,3},{3,2},{4,5},{5,4},{6,7},{7,6},{8,9},{9,8},{10,11... | collective-permute-start | bytes 491528 | tf_op jit(solution)/shard_map/ppermute | solution.py:432
  115.9 5.7 %collective-permute-start.32 = (bf16[128,128]{1,0:T(8,128)(2,1)S(1)}, bf16[128,128]{1,0:T(8,128)(2,1)S(1)}, u32[]{:S(2)}, u32[]{:S(2)}) collective-permute-start(bf16[128,128]{1,0:T(8,128)(2,1)S(1)} %get-tuple-element.52), channel_id=1, source_target_pairs={{0,24},{2,26},{4,28},{6,30},{8,16},{10,18},{12,20},{14,22},{16,8},... | collective-permute-start | bytes 98312 | tf_op jit(solution)/shard_map/ppermute | solution.py:426
  117.8 5.5 %collective-permute-start.30 = (bf16[128,128]{1,0:T(8,128)(2,1)S(1)}, bf16[128,128]{1,0:T(8,128)(2,1)S(1)}, u32[]{:S(2)}, u32[]{:S(2)}) collective-permute-start(bf16[128,128]{1,0:T(8,128)(2,1)S(1)} %get-tuple-element.50), channel_id=1, source_target_pairs={{0,16},{2,18},{4,20},{6,22},{8,24},{10,26},{12,28},{14,30},{16,0},... | collective-permute-start | bytes 98312 | tf_op jit(solution)/shard_map/ppermute | solution.py:426
  121.6 4.3 %collective-permute-start.36 = (bf16[128,256]{1,0:T(8,128)(2,1)S(1)}, bf16[128,256]{1,0:T(8,128)(2,1)S(1)}, u32[]{:S(2)}, u32[]{:S(2)}) collective-permute-start(bf16[128,256]{1,0:T(8,128)(2,1)S(1)} %shard_map.76), channel_id=1, source_target_pairs={{0,1},{1,0},{2,3},{3,2},{4,5},{5,4},{6,7},{7,6},{8,9},{9,8},{10,11... | collective-permute-start | bytes 196616 | tf_op jit(solution)/shard_map/ppermute | solution.py:432
  123.3 4.3 %collective-permute-start.35 = (bf16[128,256]{1,0:T(8,128)(2,1)S(1)}, bf16[128,256]{1,0:T(8,128)(2,1)S(1)}, u32[]{:S(2)}, u32[]{:S(2)}) collective-permute-start(bf16[128,256]{1,0:T(8,128)(2,1)S(1)} %shard_map.75), channel_id=1, source_target_pairs={{0,1},{1,0},{2,3},{3,2},{4,5},{5,4},{6,7},{7,6},{8,9},{9,8},{10,11... | collective-permute-start | bytes 196616 | tf_op jit(solution)/shard_map/ppermute | solution.py:432
  (17 other events, 142.4 us)
